TPU v7x, 256 devices: a whole 4x4x8 slice. The times are simulated.
256 devices in a mesh: freq: 16 (over x_lo, y, core), gz: 16 (over x_hi, z).
Axes of the slice: x: 4 (x_hi: 2, x_lo: 2; x = x_hi * 2 + x_lo), y: 4, z: 8, core: 2. Of those that a mesh axis runs over, the one named last changes fastest.
Arguments:
- displacement: float32 [16, 2, 3, 64, 64, 128], P('freq', None, None, 'gz'), may hold values from -6 to 6
- freq_index: int32 [16], P('freq'), may hold values from 0 to 7
- tissue: int32 [64, 64, 128], P('gz'), may hold values from 0 to 1, as said below
Outputs:
- modulus: float32 [2, 64, 64, 128], P(None, 'gz')
- residual: float32 [2, 64, 64, 128], P(None, 'gz')
Inputs may be any that keep to these rules, and one draw needn't show every extreme that they name: 0 outside tissue, 1 inside; the share of tissue rises along z from about 0.15 to about 0.95.
All inputs are finite; a program needn't handle non-finite values.
Results may differ from a plain program's by a relative error of at most 0.0003.
Values sent between devices are 32-bit elements; how exact they have to be, the bound alone decides.
No kernel may reach another device: no remote copies, remote signals or barrier semaphores. Data moves between devices by JAX's collectives and lax.ppermute only.
A program may use at most 64 MiB of HBM per device.

v0:
```python
import jax
import jax.numpy as jnp
from jax import lax
from jax.sharding import PartitionSpec as P

ITERS = 2


DAMPING = 0.05


def passed_along(array, axis, by):
    peers = lax.axis_size(axis)
    pairs = [(i, i + by) for i in range(peers) if 0 <= i + by < peers]
    return lax.ppermute(array, axis, pairs)


def cut_along(array, dim, peers):
    before, after = (array.shape[:dim], array.shape[dim + 1 :])
    return jnp.moveaxis(array.reshape(*before, peers, -1, *after), dim, 0)


def summed_on_arrival(array, axis, dim):
    parts = cut_along(array, dim, lax.axis_size(axis))
    arrived = lax.all_to_all(parts, axis, split_axis=0, concat_axis=0, tiled=True)
    return arrived.sum(axis=0)


def filled_up(lines, peers):
    spare = -len(lines) % peers
    return jnp.pad(lines, [(0, spare)] + [(0, 0)] * (lines.ndim - 1))


def copy_for_each(array, axis):
    copies = jnp.broadcast_to(array, (lax.axis_size(axis), *array.shape))
    return lax.all_to_all(copies, axis, split_axis=0, concat_axis=0, tiled=True)


def laid_out(parts, dim):
    shape = list(parts.shape[1:])
    shape[dim] *= parts.shape[0]
    return jnp.moveaxis(parts, 0, dim).reshape(shape)


def collect(array, axis, dim):
    parts = copy_for_each(array, axis)
    return laid_out(parts, dim)


def sum_by_parts(array, axes):
    lines = array.reshape(-1, array.shape[-1])
    own = summed_on_arrival(filled_up(lines, lax.axis_size(axes)), axes, 0)
    whole = collect(own, axes, 0)
    return whole[: len(lines)].reshape(array.shape)


def over_copies(array, axis):
    return copy_for_each(array, axis).sum(axis=0)


def zero_plane(field, spatial):
    return jnp.zeros_like(lax.slice_in_dim(field, 0, 1, axis=spatial))


def ahead(field, spatial, tail):
    moved = lax.slice_in_dim(field, 1, field.shape[spatial], axis=spatial)
    return jnp.concatenate([moved, tail], axis=spatial)


def behind(field, spatial, head):
    moved = lax.slice_in_dim(field, 0, field.shape[spatial] - 1, axis=spatial)
    return jnp.concatenate([head, moved], axis=spatial)


def gradients(field):
    above = passed_along(field[:, :, :1], "gz", -1)
    grads = [ahead(field, 2, above) - field]
    for spatial in (3, 4):
        grads.append(ahead(field, spatial, zero_plane(field, spatial)) - field)
    return grads


def forward(modulus, grads):
    total = None
    for spatial, grad in zip((2, 3, 4), grads):
        real = modulus[0] * grad[0] - modulus[1] * grad[1]
        imag = modulus[0] * grad[1] + modulus[1] * grad[0]
        flux = jnp.stack([real, imag])
        if spatial == 2:
            head = passed_along(flux[:, :, -1:], "gz", 1)
        else:
            head = zero_plane(flux, spatial)
        term = flux - behind(flux, spatial, head)
        total = term if total is None else total + term
    return total


def adjoint(values, grads):
    real = None
    imag = None
    for spatial, grad in zip((2, 3, 4), grads):
        if spatial == 2:
            tail = passed_along(values[:, :, :1], "gz", -1)
        else:
            tail = zero_plane(values, spatial)
        diff = values - ahead(values, spatial, tail)
        part_real = jnp.sum(grad[0] * diff[0] + grad[1] * diff[1], axis=0)
        part_imag = jnp.sum(grad[0] * diff[1] - grad[1] * diff[0], axis=0)
        real = part_real if real is None else real + part_real
        imag = part_imag if imag is None else imag + part_imag
    return jnp.stack([real, imag])


def body(displacement, freq_index, tissue):
    field = displacement[0]
    weight = tissue.astype(jnp.float32)
    kappa = 0.2 * (freq_index[0] + 1).astype(jnp.float32)
    grads = gradients(field)
    right_local = adjoint(weight * (-kappa * field), grads)

    def summed_all(local):
        return sum_by_parts(local, "freq")

    def inner(first, second):
        return over_copies(jnp.sum(first * second), "gz")

    residual = summed_all(right_local)
    modulus = jnp.zeros_like(residual)
    direction = residual
    norm_now = inner(residual, residual)
    for iteration in range(ITERS):
        image = summed_all(adjoint(weight * forward(direction, grads), grads)) + DAMPING * direction
        step_size = norm_now / inner(direction, image)
        modulus = modulus + step_size * direction
        residual = residual - step_size * image
        norm_next = inner(residual, residual)
        direction = residual + norm_next / norm_now * direction
        norm_now = norm_next
    return (modulus, residual)


def solution(mesh):
    placed = (P("freq", None, None, "gz", None, None), P("freq"), P("gz", None, None))
    return jax.shard_map(
        body,
        mesh=mesh,
        in_specs=placed,
        out_specs=(P(None, "gz", None, None), P(None, "gz", None, None)),
        check_vma=False,
    )
```

profile of v0, /device:TPU:1, one launch (start us, length us, event | category | flops | bytes accessed | tf_op | source)
XLA Modules:
  0.0 202.7 jit_solution(2608026394885356694)
XLA Ops:
  0.6 1.0 slice.303
  1.7 1.3 collective-permute-start
  3.0 1.1 slice.302
  4.1 0.3 slice.316
  4.4 0.1 slice.310
  5.1 0.2 copy-done.1
  5.3 3.8 %collective-permute-done = f32[2,3,1,64,128]{4,3,2,1,0:T(8,128)S(1)} collective-permute-done((f32[2,3,1,64,128]{4,3,2,1,0:T(8,128)S(1)}, f32[2,3,1,64,128]{4,3,2,1,0:T(8,128)S(1)}, u32[]{:S(2)}, u32[]{:S(2)}) %collective-permute-start) | collective-permute-done | bytes 196640 | tf_op jit(solution)/shard_map/ppermute | solution.py:15
  9.1 0.4 pad_subtract_fusion.7
  9.5 1.3 collective-permute-start.1
  10.9 0.1 slice.312
  11.0 0.3 slice.318
  11.3 6.3 %collective-permute-done.1 = f32[2,3,1,64,128]{4,3,2,1,0:T(8,128)S(1)} collective-permute-done((f32[2,3,1,64,128]{4,3,2,1,0:T(8,128)S(1)}, f32[2,3,1,64,128]{4,3,2,1,0:T(8,128)S(1)}, u32[]{:S(2)}, u32[]{:S(2)}) %collective-permute-start.1) | collective-permute-done | bytes 196640 | tf_op jit(solution)/shard_map/ppermute | solution.py:15
  17.6 0.4 pad_subtract_fusion.6
  18.0 0.2 add_reduce_fusion.7
  18.1 0.2 add_reduce_fusion.6
  18.3 0.2 add_reduce_fusion.8
  18.6 15.2 %all_to_all.54 = f32[16,32,128]{2,1,0:T(8,128)S(1)} all-to-all(f32[16,32,128]{2,1,0:T(8,128)S(1)} %bitcast.39), channel_id=1, replica_groups=mesh['freq'=16,'gz'=16] {'freq'}, dimensions={0} | all-to-all | bytes 524288 | tf_op jit(solution)/shard_map/all_to_all | solution.py:25
  33.8 10.6 %all_to_all.55 = f32[16,32,128]{2,1,0:T(8,128)S(1)} all-to-all(f32[16,32,128]{2,1,0:T(8,128)S(1)} %broadcast_in_dim.24), channel_id=1, replica_groups=mesh['freq'=16,'gz'=16] {'freq'}, dimensions={0} | all-to-all | bytes 524288 | tf_op jit(solution)/shard_map/all_to_all | solution.py:36
  44.5 0.3 multiply_subtract_fusion.5
  44.8 3.6 %collective-permute-start.2 = (f32[2,3,1,64,128]{4,3,2,1,0:T(8,128)S(1)}, f32[2,3,1,64,128]{4,3,2,1,0:T(8,128)S(1)}, u32[]{:S(2)}, u32[]{:S(2)}) collective-permute-start(f32[2,3,1,64,128]{4,3,2,1,0:T(8,128)S(1)} %fusion.19), channel_id=1, source_target_pairs={{0,1},{1,2},{2,3},{3,4},{4,5},{5,6},{6,7},{7,8},{8,9},{9,10},{10,1... | collective-permute-start | bytes 589832 | tf_op jit(solution)/shard_map/ppermute | solution.py:15
  48.4 0.1 fusion.11
  48.6 3.0 %collective-permute-done.2 = f32[2,3,1,64,128]{4,3,2,1,0:T(8,128)S(1)} collective-permute-done((f32[2,3,1,64,128]{4,3,2,1,0:T(8,128)S(1)}, f32[2,3,1,64,128]{4,3,2,1,0:T(8,128)S(1)}, u32[]{:S(2)}, u32[]{:S(2)}) %collective-permute-start.2) | collective-permute-done | bytes 196640 | tf_op jit(solution)/shard_map/ppermute | solution.py:15
  51.6 0.5 fusion.10
  52.1 1.3 collective-permute-start.3
  53.4 0.1 slice.336
  53.5 0.3 slice.339
  53.8 6.1 %collective-permute-done.3 = f32[2,3,1,64,128]{4,3,2,1,0:T(8,128)S(1)} collective-permute-done((f32[2,3,1,64,128]{4,3,2,1,0:T(8,128)S(1)}, f32[2,3,1,64,128]{4,3,2,1,0:T(8,128)S(1)}, u32[]{:S(2)}, u32[]{:S(2)}) %collective-permute-start.3) | collective-permute-done | bytes 196640 | tf_op jit(solution)/shard_map/ppermute | solution.py:15
  59.9 0.4 pad_subtract_fusion.3
  60.2 0.2 add_reduce_fusion.4
  60.4 0.2 add_reduce_fusion.3
  60.6 0.2 add_reduce_fusion.5
  60.9 13.7 %all_to_all.56 = f32[16,32,128]{2,1,0:T(8,128)S(1)} all-to-all(f32[16,32,128]{2,1,0:T(8,128)S(1)} %bitcast.40), channel_id=1, replica_groups=mesh['freq'=16,'gz'=16] {'freq'}, dimensions={0} | all-to-all | bytes 524288 | tf_op jit(solution)/shard_map/all_to_all | solution.py:25
  74.6 10.6 %all_to_all.57 = f32[16,32,128]{2,1,0:T(8,128)S(1)} all-to-all(f32[16,32,128]{2,1,0:T(8,128)S(1)} %broadcast_in_dim.26), channel_id=1, replica_groups=mesh['freq'=16,'gz'=16] {'freq'}, dimensions={0} | all-to-all | bytes 524288 | tf_op jit(solution)/shard_map/all_to_all | solution.py:36
  85.2 0.7 multiply_reduce_fusion.2
  85.9 0.6 broadcast_in_dim.25
  86.6 25.1 %all_to_all.58 = f32[16,1,1]{2,1,0:T(1,128)S(1)} all-to-all(f32[16,1,1]{2,1,0:T(1,128)S(1)} %broadcast_in_dim.25), channel_id=1, replica_groups=mesh['freq'=16,'gz'=16] {'gz'}, dimensions={0} | all-to-all | bytes 128 | tf_op jit(solution)/shard_map/all_to_all | solution.py:36
  111.7 1.2 broadcast_in_dim.27
  112.9 3.5 %all-to-all-start.5 = ((f32[16,1,1]{2,1,0:T(1,128)}), f32[16,1,1]{2,1,0:T(1,128)S(1)}, u32[]{:S(2)}, u32[]{:S(2)}) async-start(f32[16,1,1]{2,1,0:T(1,128)} %broadcast_in_dim.27), calls=%async_computation.5 | async-start | bytes 16384 | tf_op jit(solution)/shard_map/all_to_all | solution.py:36
  116.4 0.6 reduce_sum.269
  117.0 8.1 %all-to-all-done.5 = f32[16,1,1]{2,1,0:T(1,128)S(1)} async-done(((f32[16,1,1]{2,1,0:T(1,128)}), f32[16,1,1]{2,1,0:T(1,128)S(1)}, u32[]{:S(2)}, u32[]{:S(2)}) %all-to-all-start.5) | async-done | bytes 96 | tf_op jit(solution)/shard_map/all_to_all | solution.py:36
  125.1 0.6 reduce_sum.278
  127.1 0.7 multiply_reduce_fusion.1
  127.7 0.6 broadcast_in_dim.28
  128.4 11.4 %all_to_all.59 = f32[16,1,1]{2,1,0:T(1,128)S(1)} all-to-all(f32[16,1,1]{2,1,0:T(1,128)S(1)} %broadcast_in_dim.28), channel_id=1, replica_groups=mesh['freq'=16,'gz'=16] {'gz'}, dimensions={0} | all-to-all | bytes 128 | tf_op jit(solution)/shard_map/all_to_all | solution.py:36
  139.8 0.6 reduce_sum.280
  141.8 0.3 multiply_subtract_fusion.2
  142.2 2.2 %collective-permute-start.4 = (f32[2,3,1,64,128]{4,3,2,1,0:T(8,128)S(1)}, f32[2,3,1,64,128]{4,3,2,1,0:T(8,128)S(1)}, u32[]{:S(2)}, u32[]{:S(2)}) collective-permute-start(f32[2,3,1,64,128]{4,3,2,1,0:T(8,128)S(1)} %fusion.18), channel_id=1, source_target_pairs={{0,1},{1,2},{2,3},{3,4},{4,5},{5,6},{6,7},{7,8},{8,9},{9,10},{10,1... | collective-permute-start | bytes 589832 | tf_op jit(solution)/shard_map/ppermute | solution.py:15
  144.5 0.1 fusion
  144.6 2.4 %collective-permute-done.4 = f32[2,3,1,64,128]{4,3,2,1,0:T(8,128)S(1)} collective-permute-done((f32[2,3,1,64,128]{4,3,2,1,0:T(8,128)S(1)}, f32[2,3,1,64,128]{4,3,2,1,0:T(8,128)S(1)}, u32[]{:S(2)}, u32[]{:S(2)}) %collective-permute-start.4) | collective-permute-done | bytes 196640 | tf_op jit(solution)/shard_map/ppermute | solution.py:15
  147.0 0.5 fusion.3
  147.5 1.3 collective-permute-start.5
  148.8 0.1 slice.356
  148.9 0.3 slice.359
  149.2 5.2 %collective-permute-done.5 = f32[2,3,1,64,128]{4,3,2,1,0:T(8,128)S(1)} collective-permute-done((f32[2,3,1,64,128]{4,3,2,1,0:T(8,128)S(1)}, f32[2,3,1,64,128]{4,3,2,1,0:T(8,128)S(1)}, u32[]{:S(2)}, u32[]{:S(2)}) %collective-permute-start.5) | collective-permute-done | bytes 196640 | tf_op jit(solution)/shard_map/ppermute | solution.py:15
  154.3 0.4 pad_subtract_fusion.1
  154.7 0.2 add_reduce_fusion.2
  154.9 0.4 add_reduce_fusion
  155.4 16.4 %all_to_all.60 = f32[16,32,128]{2,1,0:T(8,128)S(1)} all-to-all(f32[16,32,128]{2,1,0:T(8,128)S(1)} %bitcast.41), channel_id=1, replica_groups=mesh['freq'=16,'gz'=16] {'freq'}, dimensions={0} | all-to-all | bytes 524288 | tf_op jit(solution)/shard_map/all_to_all | solution.py:25
  171.8 10.6 %all_to_all.61 = f32[16,32,128]{2,1,0:T(8,128)S(1)} all-to-all(f32[16,32,128]{2,1,0:T(8,128)S(1)} %broadcast_in_dim.29), channel_id=1, replica_groups=mesh['freq'=16,'gz'=16] {'freq'}, dimensions={0} | all-to-all | bytes 524288 | tf_op jit(solution)/shard_map/all_to_all | solution.py:36
  182.5 0.7 multiply_reduce_fusion
  183.2 0.6 broadcast_in_dim.30
  183.8 16.0 %all_to_all.62 = f32[16,1,1]{2,1,0:T(1,128)S(1)} all-to-all(f32[16,1,1]{2,1,0:T(1,128)S(1)} %broadcast_in_dim.30), channel_id=1, replica_groups=mesh['freq'=16,'gz'=16] {'gz'}, dimensions={0} | all-to-all | bytes 128 | tf_op jit(solution)/shard_map/all_to_all | solution.py:36
  199.8 0.6 reduce_sum.289
  201.8 0.9 multiply_subtract_fusion.6
  (34 shorter events, 0.9 us)
Async XLA Ops:
  0.6 3.4 %copy-start = (f32[1,2,3,4,64,128]{5,4,3,2,1,0:T(8,128)S(1)}, f32[1,2,3,4,64,128]{5,4,3,2,1,0:T(8,128)}, u32[]{:S(2)}) copy-start(f32[1,2,3,4,64,128]{5,4,3,2,1,0:T(8,128)} %param.3) | copy-start | bytes 2359300
  1.7 7.4 %collective-permute-start = (f32[2,3,1,64,128]{4,3,2,1,0:T(8,128)S(1)}, f32[2,3,1,64,128]{4,3,2,1,0:T(8,128)S(1)}, u32[]{:S(2)}, u32[]{:S(2)}) collective-permute-start(f32[2,3,1,64,128]{4,3,2,1,0:T(8,128)S(1)} %slice.303), channel_id=1, source_target_pairs={{1,0},{2,1},{3,2},{4,3},{5,4},{6,5},{7,6},{8,7},{9,8},{10,9},{11,1... | collective-permute-start | bytes 589832 | tf_op jit(solution)/shard_map/ppermute | solution.py:15
  4.4 0.9 copy-start.1
  9.5 8.1 %collective-permute-start.1 = (f32[2,3,1,64,128]{4,3,2,1,0:T(8,128)S(1)}, f32[2,3,1,64,128]{4,3,2,1,0:T(8,128)S(1)}, u32[]{:S(2)}, u32[]{:S(2)}) collective-permute-start(f32[2,3,1,64,128]{4,3,2,1,0:T(8,128)S(1)} %slice.306), channel_id=1, source_target_pairs={{1,0},{2,1},{3,2},{4,3},{5,4},{6,5},{7,6},{8,7},{9,8},{10,9},{11,1... | collective-permute-start | bytes 589832 | tf_op jit(solution)/shard_map/ppermute | solution.py:15
  44.8 6.7 %collective-permute-start.2 = (f32[2,3,1,64,128]{4,3,2,1,0:T(8,128)S(1)}, f32[2,3,1,64,128]{4,3,2,1,0:T(8,128)S(1)}, u32[]{:S(2)}, u32[]{:S(2)}) collective-permute-start(f32[2,3,1,64,128]{4,3,2,1,0:T(8,128)S(1)} %fusion.19), channel_id=1, source_target_pairs={{0,1},{1,2},{2,3},{3,4},{4,5},{5,6},{6,7},{7,8},{8,9},{9,10},{10,1... | collective-permute-start | bytes 589832 | tf_op jit(solution)/shard_map/ppermute | solution.py:15
  52.1 7.8 %collective-permute-start.3 = (f32[2,3,1,64,128]{4,3,2,1,0:T(8,128)S(1)}, f32[2,3,1,64,128]{4,3,2,1,0:T(8,128)S(1)}, u32[]{:S(2)}, u32[]{:S(2)}) collective-permute-start(f32[2,3,1,64,128]{4,3,2,1,0:T(8,128)S(1)} %slice.333), channel_id=1, source_target_pairs={{1,0},{2,1},{3,2},{4,3},{5,4},{6,5},{7,6},{8,7},{9,8},{10,9},{11,1... | collective-permute-start | bytes 589832 | tf_op jit(solution)/shard_map/ppermute | solution.py:15
  112.9 12.2 %all-to-all-start.5 = ((f32[16,1,1]{2,1,0:T(1,128)}), f32[16,1,1]{2,1,0:T(1,128)S(1)}, u32[]{:S(2)}, u32[]{:S(2)}) async-start(f32[16,1,1]{2,1,0:T(1,128)} %broadcast_in_dim.27), calls=%async_computation.5 | async-start | bytes 16384 | tf_op jit(solution)/shard_map/all_to_all | solution.py:36
  142.2 4.8 %collective-permute-start.4 = (f32[2,3,1,64,128]{4,3,2,1,0:T(8,128)S(1)}, f32[2,3,1,64,128]{4,3,2,1,0:T(8,128)S(1)}, u32[]{:S(2)}, u32[]{:S(2)}) collective-permute-start(f32[2,3,1,64,128]{4,3,2,1,0:T(8,128)S(1)} %fusion.18), channel_id=1, source_target_pairs={{0,1},{1,2},{2,3},{3,4},{4,5},{5,6},{6,7},{7,8},{8,9},{9,10},{10,1... | collective-permute-start | bytes 589832 | tf_op jit(solution)/shard_map/ppermute | solution.py:15
  147.5 6.9 %collective-permute-start.5 = (f32[2,3,1,64,128]{4,3,2,1,0:T(8,128)S(1)}, f32[2,3,1,64,128]{4,3,2,1,0:T(8,128)S(1)}, u32[]{:S(2)}, u32[]{:S(2)}) collective-permute-start(f32[2,3,1,64,128]{4,3,2,1,0:T(8,128)S(1)} %slice.353), channel_id=1, source_target_pairs={{1,0},{2,1},{3,2},{4,3},{5,4},{6,5},{7,6},{8,7},{9,8},{10,9},{11,1... | collective-permute-start | bytes 589832 | tf_op jit(solution)/shard_map/ppermute | solution.py:15
where the time goes:
time: 204 us; the launch traced here: 203 us
  blocking collectives  130 us (64%)
  waiting for transfers between devices  34.8 us (17%)
  starting transfers between devices  14.4 us (7%)
  other arithmetic  10.9 us (5%)
  local copies, waits for them, and re-layouts  7.18 us (4%)
  between operations  5.75 us (3%)
    all_to_all x6, blocking collectives, copy_for_each(): return lax.all_to_all(copies, axis, split_axis=0, concat_axis=0, tiled=True)  84.4 us
    all_to_all x3, blocking collectives, summed_on_arrival(): lax.all_to_all(parts, axis, split_axis=0, concat_axis=0, tiled=True)  45.2 us
    ppermute x6, waiting for transfers between devices, passed_along(): return lax.ppermute(array, axis, pairs)  26.7 us
    ppermute x6, starting transfers between devices, passed_along(): return lax.ppermute(array, axis, pairs)  10.9 us
    all_to_all x1, waiting for transfers between devices, copy_for_each(): return lax.all_to_all(copies, axis, split_axis=0, concat_axis=0, tiled=True)  8.07 us
  transfers between devices with their start and end apart: 7, of which 7 were waited for; matrix products, arithmetic and copies ran while one was open for 2% of the time, Pallas kernels for 0%

commit v1 on v0

v1 whole, which is shorter than its diff:
```python
import jax
import jax.numpy as jnp
from jax import lax
from jax.sharding import PartitionSpec as P

DAMPING = 0.05
ROWS = 8


def swap_cores(array):
    pairs = [(i, i ^ 1) for i in range(lax.axis_size("freq"))]
    return lax.ppermute(array, "freq", pairs)


def to_slabs(array, first_up, cross):
    peers, slabs = lax.axis_size("freq"), lax.axis_size("gz")
    pairs = []
    for f in range(peers):
        for g in range(slabs):
            to = g + 1 if f % 2 == first_up else g - 1
            if 0 <= to < slabs:
                pairs.append((f * slabs + g, (f ^ cross) * slabs + to))
    return lax.ppermute(array, ("freq", "gz"), pairs)


def over_chips(parts):
    peers = lax.axis_size("freq")
    groups = [list(range(core, peers, 2)) for core in range(2)]
    return lax.all_to_all(parts, "freq", split_axis=0, concat_axis=0, tiled=True, axis_index_groups=groups)


def nxt(field, dim):
    dim = dim % field.ndim
    pad = [(0, 0)] * field.ndim
    pad[dim] = (0, 1)
    return lax.slice_in_dim(jnp.pad(field, pad), 1, field.shape[dim] + 1, axis=dim)


def prv(field, dim):
    dim = dim % field.ndim
    pad = [(0, 0)] * field.ndim
    pad[dim] = (1, 0)
    return lax.slice_in_dim(jnp.pad(field, pad), 0, field.shape[dim], axis=dim)


def herm(a, b):
    real = jnp.sum(a[:, 0] * b[:, 0] + a[:, 1] * b[:, 1], axis=(0, 1))
    imag = jnp.sum(a[:, 0] * b[:, 1] - a[:, 1] * b[:, 0], axis=(0, 1))
    return real, imag


def square(a):
    return jnp.sum(a * a, axis=(0, 1, 2))


def stencil(field, kappa, mask):
    own = field[:, :, :, 1:3]
    gz = field[:, :, :, 1:] - field[:, :, :, :-1]
    gy = nxt(own, -2) - own
    gx = nxt(own, -1) - own
    here = mask[:2]
    gz_own, gz_prv = gz[:, :, :, 1:], gz[:, :, :, :-1]
    total = gz_own + gy + gx
    gy_prv, gx_prv = prv(gy, -2), prv(gx, -1)
    my, mx = nxt(here, -2), nxt(here, -1)
    diag = here * square(total) + mask[1:] * square(gz_own) + my * square(gy) + mx * square(gx)
    rows = [diag]
    for other in (gz_prv, gy_prv, gx_prv):
        rows += [-here * part for part in herm(total, other)]
    for one, two in ((gz_prv, gy_prv), (gz_prv, gx_prv), (gy_prv, gx_prv)):
        rows += [here * part for part in herm(one, two)]
    scaled = -kappa[:, None, None, None, None, None] * field[:, :, :, 1:]
    target = scaled * mask
    mine = target[:, :, :, :2]
    right = [jnp.zeros_like(diag)] * 2
    for sign, grad, value in (
        (1.0, total, mine),
        (-1.0, gz_own, target[:, :, :, 1:]),
        (-1.0, gy, nxt(mine, -2)),
        (-1.0, gx, nxt(mine, -1)),
    ):
        right = [old + sign * part for old, part in zip(right, herm(grad, value))]
    return jnp.stack(rows + right)


def applied(coefs, field):
    planes, lines = field.shape[1:3]

    def at(array, dz, dy, dx):
        cut = array[..., 1 + dz : planes - 1 + dz, 1 + dy : lines - 1 + dy, :]
        return nxt(cut, -1) if dx == 1 else prv(cut, -1) if dx == -1 else cut

    def mul(c, m, conj):
        re, im = (c[0], -c[1]) if conj else (c[0], c[1])
        return re * m[0] - im * m[1], re * m[1] + im * m[0]

    middle = (coefs[0:1] + DAMPING) * field
    out = [at(middle[0], 0, 0, 0), at(middle[1], 0, 0, 0)]
    unit = ((1, 0, 0), (0, 1, 0), (0, 0, 1))
    for d in range(3):
        e = unit[d]
        pair = coefs[1 + 2 * d : 3 + 2 * d]
        for part in (
            mul(at(pair, 0, 0, 0), at(field, *(-v for v in e)), False),
            mul(at(pair, *e), at(field, *e), True),
        ):
            out = [old + new for old, new in zip(out, part)]
    for k, (d, q) in enumerate(((0, 1), (0, 2), (1, 2))):
        e, h = unit[d], unit[q]
        pair = coefs[7 + 2 * k : 9 + 2 * k]
        diff = tuple(v - w for v, w in zip(e, h))
        for part in (
            mul(at(pair, *e), at(field, *diff), False),
            mul(at(pair, *h), at(field, *(-v for v in diff)), True),
        ):
            out = [old + new for old, new in zip(out, part)]
    return jnp.stack(out)


def body(displacement, freq_index, tissue):
    core = lax.axis_index("freq") % 2
    chips = lax.axis_size("freq") // 2
    low = core == 0
    field = displacement[0]
    weight = tissue.astype(jnp.float32)
    ny, nx = field.shape[-2:]
    kappa = 0.2 * (freq_index[0] + 1).astype(jnp.float32)

    first = jnp.concatenate([field[:, :, 0].reshape(6, ny, nx), weight[0:1]])
    last = jnp.concatenate([field[:, :, 3].reshape(6, ny, nx), weight[3:4]])
    own_edge = to_slabs(jnp.where(low, last, first), 0, 0)
    other_edge = to_slabs(jnp.where(low, first, last), 1, 1)
    sent = jnp.where(low, field[:, :, 1:], field[:, :, :3])
    other_mid = swap_cores(sent)
    other_kappa = swap_cores(kappa.reshape(1, 1))[0, 0]

    bottom = low & (lax.axis_index("gz") == 0)

    def joined(edge, middle):
        edge = jnp.where(bottom, middle[:, :, :1], edge[:6].reshape(2, 3, 1, ny, nx))
        return jnp.where(low, jnp.concatenate([edge, middle], axis=2), jnp.concatenate([middle, edge], axis=2))

    own_mid = jnp.where(low, field[:, :, :3], field[:, :, 1:])
    groups = jnp.stack([joined(own_edge, own_mid), joined(other_edge, other_mid)])
    mask = jnp.where(low, weight[:3], jnp.concatenate([weight[2:], own_edge[6:7]]))
    local = stencil(groups, jnp.stack([kappa, other_kappa]), mask)

    padded = jnp.pad(local, [(0, 0), (0, 0), (2, 2), (0, 0)])
    parts = jnp.stack([padded[:, :, ROWS * j : ROWS * j + ROWS + 4] for j in range(chips)])
    arrived = over_chips(parts.reshape(chips, -1, nx))
    mine = arrived.sum(axis=0).reshape(15, 2, ROWS + 4, nx)

    near = swap_cores(mine)
    far = to_slabs(mine, 1, 1)
    below = jnp.where(low, far, near)
    above = jnp.where(low, near, far)
    block = jnp.concatenate([below, mine, above], axis=1)
    coefs, v0 = block[:13], block[13:]
    v1 = applied(coefs, v0)
    v2 = applied(coefs[:, 1:-1, 1:-1], v1)
    v0, v1 = v0[:, 2:4, 2:-2], v1[:, 1:3, 1:-1]
    moments = [jnp.sum(a * b) for a, b in ((v0, v0), (v0, v1), (v1, v1), (v1, v2))]
    lane = lax.broadcasted_iota(jnp.int32, (ROWS, nx), 1)
    note = sum(jnp.where(lane == k, value, 0.0) for k, value in enumerate(moments))
    tiles = jnp.concatenate([jnp.stack([v0, v1, v2]).reshape(12, ROWS, nx), note[None]])

    gathered = over_chips(jnp.broadcast_to(tiles, (chips, *tiles.shape)))
    others = swap_cores(gathered)
    both = jnp.stack([jnp.where(low, gathered, others), jnp.where(low, others, gathered)])

    sums = both[:, :, 12, 0].sum(axis=(0, 1))
    slabs = lax.axis_size("gz")
    sums = lax.all_to_all(jnp.broadcast_to(sums, (slabs, 1, nx)), "gz", split_axis=0, concat_axis=0, tiled=True)
    sums = sums.sum(axis=(0, 1))
    m0, m1, m2, m3 = (sums[k] for k in range(4))
    step = m0 / m1
    norm = step * step * m2 - m0
    ratio = norm / m0
    grown = 1.0 + ratio
    curve = grown * grown * m1 - 2.0 * step * grown * m2 + step * step * m3
    second = norm / curve
    p, q = step + second * grown, step * second

    vectors = both[:, :, :12].reshape(2, chips, 3, 2, 2, ROWS, nx)
    vectors = vectors.transpose(2, 3, 0, 4, 1, 5, 6).reshape(3, 2, 4, ny, nx)
    modulus = p * vectors[0] - q * vectors[1]
    residual = vectors[0] - p * vectors[1] + q * vectors[2]
    return modulus, residual


def solution(mesh):
    placed = (P("freq", None, None, "gz", None, None), P("freq"), P("gz", None, None))
    return jax.shard_map(
        body,
        mesh=mesh,
        in_specs=placed,
        out_specs=(P(None, "gz", None, None), P(None, "gz", None, None)),
        check_vma=False,
    )
```

time: 204 us -> 98.4 us (0.48)
  blocking collectives: 130 us -> 34.4 us
  waiting for transfers between devices: 34.8 us -> 14.5 us
  starting transfers between devices: 14.4 us -> 27.5 us
  local copies, waits for them, and re-layouts: 7.18 us -> 4.57 us
    all_to_all x9 -> x2, blocking collectives: 130 us -> 34.4 us  [over_chips(): lax.all_to_all(parts, 'freq', split_axis=0, concat_axis=0, tiled=True, ax...]
    ppermute x6 -> x7, waiting for transfers between devices: 26.7 us -> 5.89 us  [the longest x3 4.12 us: to_slabs(): return lax.ppermute(array, ('freq', 'gz'), pairs)]
    all_to_all x1, starting transfers between devices: 3.47 us -> 11.9 us  [body(): lax.all_to_all(jnp.broadcast_to(sums, (slabs, 1, nx)), 'gz', split_axis=0...]
    ppermute x6 -> x7, starting transfers between devices: 10.9 us -> 15.7 us  [the longest x3 14.1 us: to_slabs(): return lax.ppermute(array, ('freq', 'gz'), pairs)]
    sub x7 -> x0, other arithmetic: 3.1 us -> none  [the longest x3 1.13 us: adjoint(): diff = values - ahead(values, spatial, tail)]
    reduce_sum x18 -> x8, other arithmetic: 6.2 us -> 3.3 us  [the longest x2 1.95 us: herm(): imag = jnp.sum(a[:, 0] * b[:, 1] - a[:, 1] * b[:, 0], axis=(0, 1))]
    broadcast_in_dim x7 -> x2, local copies, waits for them, and re-layouts: 3.25 us -> 0.64 us  [the longest x1 0.61 us: body(): jnp.broadcast_to(sums, (slabs, 1, nx))]
    add x7 -> x2, other arithmetic: 0.22 us -> 2.62 us  [the longest x1 2.55 us: body(): sum((jnp.where(lane == k, value, 0.0) for k, value in enumerate(moments)))]
  transfers between devices with their start and end apart: 7 -> 8, of which waited for: 7 -> 4; matrix products, arithmetic and copies ran while one was open for 2% -> 1% of each run, Pallas kernels for 0% -> 0%
where the time goes in v1:
time: 98.4 us; the launch traced here: 98 us
  blocking collectives  34.4 us (35%)
  starting transfers between devices  27.5 us (28%)
  waiting for transfers between devices  14.5 us (15%)
  other arithmetic  9.78 us (10%)
  between operations  7.13 us (7%)
  local copies, waits for them, and re-layouts  4.57 us (5%)
    all_to_all x2, blocking collectives, over_chips(): lax.all_to_all(parts, 'freq', split_axis=0, concat_axis=0, tiled=True, ax...  34.4 us
    ppermute x3, starting transfers between devices, to_slabs(): return lax.ppermute(array, ('freq', 'gz'), pairs)  14.1 us
    all_to_all x1, starting transfers between devices, body(): lax.all_to_all(jnp.broadcast_to(sums, (slabs, 1, nx)), 'gz', split_axis=0...  11.9 us
    all_to_all x1, waiting for transfers between devices, body(): lax.all_to_all(jnp.broadcast_to(sums, (slabs, 1, nx)), 'gz', split_axis=0...  8.66 us
    ppermute x3, waiting for transfers between devices, to_slabs(): return lax.ppermute(array, ('freq', 'gz'), pairs)  4.12 us
    add x1, other arithmetic, body(): sum((jnp.where(lane == k, value, 0.0) for k, value in enumerate(moments)))  2.55 us
  transfers between devices with their start and end apart: 8, of which 4 were waited for; matrix products, arithmetic and copies ran while one was open for 1% of the time, Pallas kernels for 0%

profile of v1, /device:TPU:1, one launch (start us, length us, event | category | flops | bytes accessed | tf_op | source)
XLA Modules:
  0.0 98.0 jit_solution(7351053019711434798)
XLA Ops:
  0.6 0.0 copy-start.2
  0.7 1.0 %convert_element_type.45 = f32[4,64,128]{2,1,0:T(8,128)S(1)} convert(s32[4,64,128]{2,1,0:T(8,128)} %param.5) | non-fusion elementwise | flops 32768 | bytes 262144 | tf_op jit(solution)/shard_map/convert_element_type | solution.py:125
  1.7 1.1 %fusion.105 = (f32[2,3,1,64,128]{4,3,2,1,0:T(8,128)S(1)}, f32[2,3,1,64,128]{4,3,2,1,0:T(8,128)S(1)}) fusion(f32[2,3,4,64,128]{4,3,2,1,0:T(8,128)} %bitcast.193), kind=kLoop, calls=%fused_computation.302 | loop fusion | bytes 786432 | tf_op jit(solution)/shard_map/slice | solution.py:130
  2.8 1.3 %collective-permute-start = (f32[7,64,128]{2,1,0:T(8,128)S(1)}, f32[7,64,128]{2,1,0:T(8,128)S(1)}, u32[]{:S(2)}, u32[]{:S(2)}) collective-permute-start(f32[7,64,128]{2,1,0:T(8,128)S(1)} %get-tuple-element.88), channel_id=1, source_target_pairs={{0,1},{1,2},{2,3},{3,4},{4,5},{5,6},{6,7},{7,8},{8,9},{9,10},{10,1... | collective-permute-start | bytes 688136 | tf_op jit(solution)/shard_map/ppermute | solution.py:23
  4.1 7.5 %collective-permute-start.2 = (f32[7,64,128]{2,1,0:T(8,128)S(1)}, f32[7,64,128]{2,1,0:T(8,128)S(1)}, u32[]{:S(2)}, u32[]{:S(2)}) collective-permute-start(f32[7,64,128]{2,1,0:T(8,128)S(1)} %get-tuple-element.87), channel_id=1, source_target_pairs={{1,16},{2,17},{3,18},{4,19},{5,20},{6,21},{7,22},{8,23},{9,24},{10... | collective-permute-start | bytes 688136 | tf_op jit(solution)/shard_map/ppermute | solution.py:23
  11.5 0.0 copy-done.2
  11.6 0.2 broadcast_select_fusion
  11.8 0.1 collective-permute-start.1
  12.5 1.4 %collective-permute-start.3 = (f32[1,1]{1,0:T(1,128)}, f32[1,1]{1,0:T(1,128)}, u32[]{:S(2)}, u32[]{:S(2)}) collective-permute-start(f32[1,1]{1,0:T(1,128)} %bitcast.25), channel_id=1, source_target_pairs={{0,16},{16,0},{32,48},{48,32},{64,80},{80,64},{96,112},{112,96},{1... | collective-permute-start | bytes 20 | tf_op jit(solution)/shard_map/ppermute | solution.py:12
  13.9 0.1 copy_select_fusion
  14.0 0.0 collective-permute-done.3
  14.0 0.8 maximum_negate_fusion
  14.8 0.0 collective-permute-done
  14.8 0.0 copy-start
  14.9 0.4 collective-permute-done.2
  15.3 0.1 maximum_select_fusion
  15.4 0.0 collective-permute-done.1
  15.4 0.1 maximum_select_fusion.1
  15.5 0.1 pad_maximum_fusion.1
  15.6 0.0 copy-done
  15.6 0.2 multiply_multiply_fusion
  15.9 0.1 slice.1174
  15.9 0.4 multiply_reduce_fusion.3
  16.3 0.1 multiply_reduce_fusion
  16.5 1.0 subtract_reduce_fusion.2
  17.4 0.0 copy-start.1
  17.5 0.0 slice-start
  17.5 1.0 %subtract_reduce_fusion.1 = (f32[2,64,128]{2,1,0:T(8,128)S(1)}, f32[2,64,128]{2,1,0:T(8,128)S(1)}, f32[2,64,128]{2,1,0:T(8,128)S(1)}, f32[2,64,128]{2,1,0:T(8,12...) fusion(f32[2,2,3,2,64,128]{5,4,3,2,1,0:T(8,128)S(1)} %get-tuple, ...), kind=kLoop, calls=%fused_computation.69 | loop fusion | flops 3768320 | bytes 6160384 | tf_op jit(solution)/shard_map/reduce_sum | solution.py:48
  18.5 0.0 copy-done.1
  18.5 0.0 slice-done
  18.5 0.1 fusion.16
  18.8 0.3 pad_slice_fusion.41
  19.5 24.3 %all_to_all.15 = f32[8,360,128]{2,1,0:T(8,128)S(1)} all-to-all(f32[8,360,128]{2,1,0:T(8,128)S(1)} %constant_dynamic-update-slice_fusion), channel_id=1, replica_groups={{0,32,64,96,128,160,192,224},{16,48,80,112,144,176,208,240},{1,33,65,97..., dimensions={0} | all-to-all | bytes 2949120 | tf_op jit(solution)/shard_map/all_to_all | solution.py:29
  43.8 0.1 reduce_sum.303
  43.9 5.3 %collective-permute-start.4 = (f32[15,2,12,128]{3,2,1,0:T(8,128)S(1)}, f32[15,2,12,128]{3,2,1,0:T(8,128)S(1)}, u32[]{:S(2)}, u32[]{:S(2)}) collective-permute-start(f32[15,2,12,128]{3,2,1,0:T(8,128)S(1)} %reshape.518), channel_id=1, source_target_pairs={{1,16},{2,17},{3,18},{4,19},{5,20},{6,21},{7,22},{8,23},{9,24},{10... | collective-permute-start | bytes 552968 | tf_op jit(solution)/shard_map/ppermute | solution.py:23
  49.2 0.1 collective-permute-start.5
  49.3 3.7 %collective-permute-done.4 = f32[15,2,12,128]{3,2,1,0:T(8,128)S(1)} collective-permute-done((f32[15,2,12,128]{3,2,1,0:T(8,128)S(1)}, f32[15,2,12,128]{3,2,1,0:T(8,128)S(1)}, u32[]{:S(2)}, u32[]{:S(2)}) %collective-permute-start.4) | collective-permute-done | bytes 184352 | tf_op jit(solution)/shard_map/ppermute | solution.py:23
  53.1 0.0 collective-permute-done.5
  53.1 0.1 pad_maximum_fusion.3
  53.3 0.2 fusion.47
  53.6 0.2 fusion.59
  53.8 0.1 fusion.98
  54.0 0.1 fusion.86
  54.1 0.7 multiply_reduce_fusion.7
  54.8 2.5 %fusion.102 = f32[128]{0:T(128)S(1)} fusion(f32[]{:T(128)} %get-tuple-element.36, f32[]{:T(128)} %get-tuple-element.37, f32[]{:T(128)} %get-tuple-element.35, f32[]{:T(128)} %get-tuple-element.34), kind=kLoop, calls=%fused_computation.300 | loop fusion | flops 1408 | bytes 528 | tf_op jit(solution)/shard_map/add | solution.py:164
  57.4 10.2 %all_to_all.16 = f32[8,13,8,128]{3,2,1,0:T(8,128)S(1)} all-to-all(f32[8,13,8,128]{3,2,1,0:T(8,128)S(1)} %broadcast_in_dim.34), channel_id=1, replica_groups={{0,32,64,96,128,160,192,224},{16,48,80,112,144,176,208,240},{1,33,65,97..., dimensions={0} | all-to-all | bytes 851968 | tf_op jit(solution)/shard_map/all_to_all | solution.py:29
  67.5 0.0 collective-permute-start.6
  67.5 1.8 %collective-permute-done.6 = f32[8,13,8,128]{3,2,1,0:T(8,128)S(1)} collective-permute-done((f32[8,13,8,128]{3,2,1,0:T(8,128)S(1)}, f32[8,13,8,128]{3,2,1,0:T(8,128)S(1)}, u32[]{:S(2)}, u32[]{:S(2)}) %collective-permute-start.6) | collective-permute-done | bytes 426016 | tf_op jit(solution)/shard_map/ppermute | solution.py:12
  69.3 0.1 select_bitcast_fusion.1
  69.4 0.6 broadcast_in_dim.35
  70.0 11.9 %all-to-all-start.2 = ((f32[16,1,128]{2,1,0:T(1,128)}), f32[16,1,128]{2,1,0:T(1,128)S(1)}, u32[]{:S(2)}, u32[]{:S(2)}) async-start(f32[16,1,128]{2,1,0:T(1,128)} %broadcast_in_dim.35), calls=%async_computation.2 | async-start | bytes 16384 | tf_op jit(solution)/shard_map/all_to_all | solution.py:173
  81.9 0.1 pad_maximum_fusion
  82.0 8.7 %all-to-all-done.2 = f32[16,1,128]{2,1,0:T(1,128)S(1)} async-done(((f32[16,1,128]{2,1,0:T(1,128)}), f32[16,1,128]{2,1,0:T(1,128)S(1)}, u32[]{:S(2)}, u32[]{:S(2)}) %all-to-all-start.2) | async-done | bytes 8224 | tf_op jit(solution)/shard_map/all_to_all | solution.py:173
  90.6 0.7 fusion.108
  96.4 0.1 fusion.5
  96.5 0.7 copy.60
  97.2 0.7 copy.61
  (58 shorter events, 0.9 us)
Async XLA Ops:
  0.6 10.9 %copy-start.2 = (f32[1,2,3,4,64,128]{5,4,3,2,1,0:T(8,128)S(1)}, f32[1,2,3,4,64,128]{5,4,3,2,1,0:T(8,128)}, u32[]{:S(2)}) copy-start(f32[1,2,3,4,64,128]{5,4,3,2,1,0:T(8,128)} %param.3) | copy-start | bytes 2359300
  2.8 12.0 %collective-permute-start = (f32[7,64,128]{2,1,0:T(8,128)S(1)}, f32[7,64,128]{2,1,0:T(8,128)S(1)}, u32[]{:S(2)}, u32[]{:S(2)}) collective-permute-start(f32[7,64,128]{2,1,0:T(8,128)S(1)} %get-tuple-element.88), channel_id=1, source_target_pairs={{0,1},{1,2},{2,3},{3,4},{4,5},{5,6},{6,7},{7,8},{8,9},{9,10},{10,1... | collective-permute-start | bytes 688136 | tf_op jit(solution)/shard_map/ppermute | solution.py:23
  4.1 11.2 %collective-permute-start.2 = (f32[7,64,128]{2,1,0:T(8,128)S(1)}, f32[7,64,128]{2,1,0:T(8,128)S(1)}, u32[]{:S(2)}, u32[]{:S(2)}) collective-permute-start(f32[7,64,128]{2,1,0:T(8,128)S(1)} %get-tuple-element.87), channel_id=1, source_target_pairs={{1,16},{2,17},{3,18},{4,19},{5,20},{6,21},{7,22},{8,23},{9,24},{10... | collective-permute-start | bytes 688136 | tf_op jit(solution)/shard_map/ppermute | solution.py:23
  11.8 3.6 %collective-permute-start.1 = (f32[2,3,3,64,128]{4,3,2,1,0:T(8,128)S(1)}, f32[2,3,3,64,128]{4,3,2,1,0:T(8,128)S(1)}, u32[]{:S(2)}, u32[]{:S(2)}) collective-permute-start(f32[2,3,3,64,128]{4,3,2,1,0:T(8,128)S(1)} %get-tuple-element.72), channel_id=1, source_target_pairs={{0,16},{16,0},{32,48},{48,32},{64,80},{80,64},{96,112},{112,96},{1... | collective-permute-start | bytes 1769480 | tf_op jit(solution)/shard_map/ppermute | solution.py:12
  12.5 1.5 %collective-permute-start.3 = (f32[1,1]{1,0:T(1,128)}, f32[1,1]{1,0:T(1,128)}, u32[]{:S(2)}, u32[]{:S(2)}) collective-permute-start(f32[1,1]{1,0:T(1,128)} %bitcast.25), channel_id=1, source_target_pairs={{0,16},{16,0},{32,48},{48,32},{64,80},{80,64},{96,112},{112,96},{1... | collective-permute-start | bytes 20 | tf_op jit(solution)/shard_map/ppermute | solution.py:12
  14.8 0.8 copy-start
  17.4 1.0 %copy-start.1 = (f32[3,64,128]{2,1,0:T(8,128)S(1)}, f32[3,64,128]{2,1,0:T(8,128)}, u32[]{:S(2)}) copy-start(f32[3,64,128]{2,1,0:T(8,128)} %copy-done) | copy-start | bytes 294916
  17.5 1.0 %slice-start = ((f32[3,64,128]{2,1,0:T(8,128)}), f32[2,64,128]{2,1,0:T(8,128)S(1)}, s32[]{:S(2)}) async-start(f32[3,64,128]{2,1,0:T(8,128)} %copy-done), calls=%async_computation.3 | async-start | bytes 131072 | tf_op jit(solution)/shard_map/slice | solution.py:61
  43.9 9.2 %collective-permute-start.4 = (f32[15,2,12,128]{3,2,1,0:T(8,128)S(1)}, f32[15,2,12,128]{3,2,1,0:T(8,128)S(1)}, u32[]{:S(2)}, u32[]{:S(2)}) collective-permute-start(f32[15,2,12,128]{3,2,1,0:T(8,128)S(1)} %reshape.518), channel_id=1, source_target_pairs={{1,16},{2,17},{3,18},{4,19},{5,20},{6,21},{7,22},{8,23},{9,24},{10... | collective-permute-start | bytes 552968 | tf_op jit(solution)/shard_map/ppermute | solution.py:23
  49.2 3.9 %collective-permute-start.5 = (f32[15,2,12,128]{3,2,1,0:T(8,128)S(1)}, f32[15,2,12,128]{3,2,1,0:T(8,128)S(1)}, u32[]{:S(2)}, u32[]{:S(2)}) collective-permute-start(f32[15,2,12,128]{3,2,1,0:T(8,128)S(1)} %reshape.518), channel_id=1, source_target_pairs={{0,16},{16,0},{32,48},{48,32},{64,80},{80,64},{96,112},{112,96},{1... | collective-permute-start | bytes 552968 | tf_op jit(solution)/shard_map/ppermute | solution.py:12
  67.5 1.8 %collective-permute-start.6 = (f32[8,13,8,128]{3,2,1,0:T(8,128)S(1)}, f32[8,13,8,128]{3,2,1,0:T(8,128)S(1)}, u32[]{:S(2)}, u32[]{:S(2)}) collective-permute-start(f32[8,13,8,128]{3,2,1,0:T(8,128)S(1)} %all_to_all.16), channel_id=1, source_target_pairs={{0,16},{16,0},{32,48},{48,32},{64,80},{80,64},{96,112},{112,96},{1... | collective-permute-start | bytes 1277960 | tf_op jit(solution)/shard_map/ppermute | solution.py:12
  70.0 20.6 %all-to-all-start.2 = ((f32[16,1,128]{2,1,0:T(1,128)}), f32[16,1,128]{2,1,0:T(1,128)S(1)}, u32[]{:S(2)}, u32[]{:S(2)}) async-start(f32[16,1,128]{2,1,0:T(1,128)} %broadcast_in_dim.35), calls=%async_computation.2 | async-start | bytes 16384 | tf_op jit(solution)/shard_map/all_to_all | solution.py:173

commit v2 on v1

--- a/solution.py
+++ b/solution.py
@@ -150,28 +150,34 @@
     arrived = over_chips(parts.reshape(chips, -1, nx))
     mine = arrived.sum(axis=0).reshape(15, 2, ROWS + 4, nx)
 
-    near = swap_cores(mine)
-    far = to_slabs(mine, 1, 1)
-    below = jnp.where(low, far, near)
-    above = jnp.where(low, near, far)
-    block = jnp.concatenate([below, mine, above], axis=1)
-    coefs, v0 = block[:13], block[13:]
+    edge = jnp.where(low, mine[:13, 0], mine[:13, 1])
+    inner = jnp.where(low, mine[:13, 1], mine[:13, 0])
+    steps = jnp.concatenate([mine[1:3, 1], mine[7:11, 1]])
+    rights = mine[13:].reshape(4, ROWS + 4, nx)
+    near = swap_cores(jnp.concatenate([inner, steps, rights]))
+    far = to_slabs(jnp.concatenate([edge, steps, rights]), 1, 1)
+    below, above = jnp.where(low, far, near), jnp.where(low, near, far)
+    blank = jnp.zeros_like(above[:1])
+    beyond = jnp.concatenate([blank, above[13:15], blank, blank, blank, blank, above[15:19], blank, blank])
+    coefs = jnp.stack([below[:13], mine[:13, 0], mine[:13, 1], above[:13], beyond], axis=1)
+    v0 = jnp.concatenate([below[19:].reshape(2, 2, ROWS + 4, nx), mine[13:], above[19:].reshape(2, 2, ROWS + 4, nx)], axis=1)
+    coefs = jnp.concatenate([jnp.zeros_like(coefs[:, :1]), coefs], axis=1)
     v1 = applied(coefs, v0)
     v2 = applied(coefs[:, 1:-1, 1:-1], v1)
     v0, v1 = v0[:, 2:4, 2:-2], v1[:, 1:3, 1:-1]
-    moments = [jnp.sum(a * b) for a, b in ((v0, v0), (v0, v1), (v1, v1), (v1, v2))]
-    lane = lax.broadcasted_iota(jnp.int32, (ROWS, nx), 1)
-    note = sum(jnp.where(lane == k, value, 0.0) for k, value in enumerate(moments))
+    moments = [jnp.sum(a * b, axis=(0, 1)) for a, b in ((v0, v0), (v0, v1), (v1, v1), (v1, v2))]
+    moments = [jnp.sum(m, axis=0, keepdims=True) for m in moments]
+    note = jnp.concatenate(moments + [jnp.zeros((ROWS - 4, nx), jnp.float32)])
     tiles = jnp.concatenate([jnp.stack([v0, v1, v2]).reshape(12, ROWS, nx), note[None]])
 
     gathered = over_chips(jnp.broadcast_to(tiles, (chips, *tiles.shape)))
     others = swap_cores(gathered)
-    both = jnp.stack([jnp.where(low, gathered, others), jnp.where(low, others, gathered)])
-
-    sums = both[:, :, 12, 0].sum(axis=(0, 1))
+
+    sums = (gathered[:, 12] + others[:, 12]).sum(axis=0)
     slabs = lax.axis_size("gz")
-    sums = lax.all_to_all(jnp.broadcast_to(sums, (slabs, 1, nx)), "gz", split_axis=0, concat_axis=0, tiled=True)
-    sums = sums.sum(axis=(0, 1))
+    sums = lax.all_to_all(jnp.broadcast_to(sums, (slabs, *sums.shape)), "gz", split_axis=0, concat_axis=0, tiled=True)
+    sums = sums.sum(axis=0)
+    sums = jnp.broadcast_to(sums.sum(axis=1, keepdims=True), sums.shape)
     m0, m1, m2, m3 = (sums[k] for k in range(4))
     step = m0 / m1
     norm = step * step * m2 - m0
@@ -181,6 +187,7 @@
     second = norm / curve
     p, q = step + second * grown, step * second
 
+    both = jnp.stack([jnp.where(low, gathered, others), jnp.where(low, others, gathered)])
     vectors = both[:, :, :12].reshape(2, chips, 3, 2, 2, ROWS, nx)
     vectors = vectors.transpose(2, 3, 0, 4, 1, 5, 6).reshape(3, 2, 4, ny, nx)
     modulus = p * vectors[0] - q * vectors[1]

time: 98.4 us -> 101 us (1.026)
  blocking collectives: 34.4 us -> 11.6 us
  waiting for transfers between devices: 14.5 us -> 33.5 us
  local copies, waits for them, and re-layouts: 4.57 us -> 10.1 us
  starting transfers between devices: 27.5 us -> 31 us
  other arithmetic: 9.78 us -> 6.79 us
    all_to_all x2 -> x1, blocking collectives: 34.4 us -> 11.6 us  [over_chips(): lax.all_to_all(parts, 'freq', split_axis=0, concat_axis=0, tiled=True, ax...]
    all_to_all x1 -> x2, waiting for transfers between devices: 8.66 us -> 28.3 us  [the longest x1 19.5 us: over_chips(): lax.all_to_all(parts, 'freq', split_axis=0, concat_axis=0, tiled=True, ax...]
    unnamed x13 -> x20, local copies, waits for them, and re-layouts: 0.12 us -> 4.87 us
    all_to_all x1 -> x2, starting transfers between devices: 11.9 us -> 16.4 us  [the longest x1 11.3 us: body(): lax.all_to_all(jnp.broadcast_to(sums, (slabs, *sums.shape)), 'gz', split_...]
    add x1 -> x0, other arithmetic: 2.55 us -> none  [body(): sum((jnp.where(lane == k, value, 0.0) for k, value in enumerate(moments)))]
    ppermute x3, starting transfers between devices: 14.1 us -> 12.9 us  [to_slabs(): return lax.ppermute(array, ('freq', 'gz'), pairs)]
  transfers between devices with their start and end apart: 8 -> 9, of which waited for: 4 -> 5; matrix products, arithmetic and copies ran while one was open for 1% -> 1% of each run, Pallas kernels for 0% -> 0%
where the time goes in v2:
time: 101 us; the launch traced here: 100 us
  waiting for transfers between devices  33.5 us (33%)
  starting transfers between devices  31 us (31%)
  blocking collectives  11.6 us (11%)
  local copies, waits for them, and re-layouts  10.1 us (10%)
  between operations  7.22 us (7%)
  other arithmetic  6.79 us (7%)
    all_to_all x1, waiting for transfers between devices, over_chips(): lax.all_to_all(parts, 'freq', split_axis=0, concat_axis=0, tiled=True, ax...  19.5 us
    ppermute x3, starting transfers between devices, to_slabs(): return lax.ppermute(array, ('freq', 'gz'), pairs)  12.9 us
    all_to_all x1, blocking collectives, over_chips(): lax.all_to_all(parts, 'freq', split_axis=0, concat_axis=0, tiled=True, ax...  11.6 us
    all_to_all x1, starting transfers between devices, body(): lax.all_to_all(jnp.broadcast_to(sums, (slabs, *sums.shape)), 'gz', split_...  11.3 us
    all_to_all x1, waiting for transfers between devices, body(): lax.all_to_all(jnp.broadcast_to(sums, (slabs, *sums.shape)), 'gz', split_...  8.73 us
    all_to_all x1, starting transfers between devices, over_chips(): lax.all_to_all(parts, 'freq', split_axis=0, concat_axis=0, tiled=True, ax...  5.12 us
    unnamed x20, local copies, waits for them, and re-layouts  4.87 us
    ppermute x3, waiting for transfers between devices, to_slabs(): return lax.ppermute(array, ('freq', 'gz'), pairs)  3.48 us
  transfers between devices with their start and end apart: 9, of which 5 were waited for; matrix products, arithmetic and copies ran while one was open for 1% of the time, Pallas kernels for 0%

profile of v2, /device:TPU:1, one launch (start us, length us, event | category | flops | bytes accessed | tf_op | source)
XLA Modules:
  0.0 100.2 jit_solution(10544527487605023396)
XLA Ops:
  0.6 0.0 copy-start.2
  0.7 1.0 convert_element_type.45
  1.7 1.1 %fusion.92 = (f32[2,3,1,64,128]{4,3,2,1,0:T(8,128)S(1)}, f32[2,3,1,64,128]{4,3,2,1,0:T(8,128)S(1)}) fusion(f32[2,3,4,64,128]{4,3,2,1,0:T(8,128)} %bitcast.235), kind=kLoop, calls=%fused_computation.303 | loop fusion | bytes 786432 | tf_op jit(solution)/shard_map/slice | solution.py:130
  2.8 1.3 %collective-permute-start = (f32[7,64,128]{2,1,0:T(8,128)S(1)}, f32[7,64,128]{2,1,0:T(8,128)S(1)}, u32[]{:S(2)}, u32[]{:S(2)}) collective-permute-start(f32[7,64,128]{2,1,0:T(8,128)S(1)} %get-tuple-element.89), channel_id=1, source_target_pairs={{0,1},{1,2},{2,3},{3,4},{4,5},{5,6},{6,7},{7,8},{8,9},{9,10},{10,1... | collective-permute-start | bytes 688136 | tf_op jit(solution)/shard_map/ppermute | solution.py:23
  4.1 7.5 %collective-permute-start.2 = (f32[7,64,128]{2,1,0:T(8,128)S(1)}, f32[7,64,128]{2,1,0:T(8,128)S(1)}, u32[]{:S(2)}, u32[]{:S(2)}) collective-permute-start(f32[7,64,128]{2,1,0:T(8,128)S(1)} %get-tuple-element.88), channel_id=1, source_target_pairs={{1,16},{2,17},{3,18},{4,19},{5,20},{6,21},{7,22},{8,23},{9,24},{10... | collective-permute-start | bytes 688136 | tf_op jit(solution)/shard_map/ppermute | solution.py:23
  11.5 0.0 copy-done.2
  11.6 0.2 broadcast_select_fusion
  11.8 0.1 collective-permute-start.1
  12.5 1.4 %collective-permute-start.3 = (f32[1,1]{1,0:T(1,128)}, f32[1,1]{1,0:T(1,128)}, u32[]{:S(2)}, u32[]{:S(2)}) collective-permute-start(f32[1,1]{1,0:T(1,128)} %bitcast.25), channel_id=1, source_target_pairs={{0,16},{16,0},{32,48},{48,32},{64,80},{80,64},{96,112},{112,96},{1... | collective-permute-start | bytes 20 | tf_op jit(solution)/shard_map/ppermute | solution.py:12
  13.9 0.1 copy_select_fusion
  14.0 0.8 maximum_negate_fusion.2
  14.8 0.0 collective-permute-done
  14.8 0.0 copy-start
  14.9 0.4 collective-permute-done.2
  15.3 0.1 maximum_select_fusion
  15.4 0.0 collective-permute-done.1
  15.4 0.1 maximum_select_fusion.1
  15.5 0.1 pad_maximum_fusion.1
  15.6 0.0 copy-done
  15.6 0.2 multiply_multiply_fusion
  15.9 0.1 slice.1235
  15.9 0.4 multiply_reduce_fusion.3
  16.3 0.1 multiply_reduce_fusion
  16.5 1.0 subtract_reduce_fusion.2
  17.4 0.0 copy-start.1
  17.5 0.0 slice-start
  17.5 1.0 subtract_reduce_fusion.1
  18.5 0.0 copy-done.1
  18.5 0.0 slice-done
  18.5 0.1 constant_dynamic-update-slice_fusion.14
  18.8 0.3 pad_slice_fusion.9
  19.2 0.7 constant_dynamic-update-slice_fusion.22
  20.0 0.7 constant_dynamic-update-slice_fusion.21
  20.7 0.7 constant_dynamic-update-slice_fusion.20
  21.4 0.7 constant_dynamic-update-slice_fusion.19
  22.1 0.7 constant_dynamic-update-slice_fusion.18
  22.8 0.7 constant_dynamic-update-slice_fusion.17
  23.4 0.7 constant_dynamic-update-slice_fusion.16
  24.1 0.7 constant_dynamic-update-slice_fusion.15
  24.8 5.1 %all-to-all-start = ((f32[8,360,128]{2,1,0:T(8,128)}), f32[8,360,128]{2,1,0:T(8,128)S(1)}, u32[]{:S(2)}, u32[]{:S(2)}) async-start(f32[8,360,128]{2,1,0:T(8,128)} %constant_dynamic-update-slice_fusion.15), calls=%async_computation | async-start | bytes 2949120 | tf_op jit(solution)/shard_map/all_to_all | solution.py:29
  30.0 19.5 %all-to-all-done = f32[8,360,128]{2,1,0:T(8,128)S(1)} async-done(((f32[8,360,128]{2,1,0:T(8,128)}), f32[8,360,128]{2,1,0:T(8,128)S(1)}, u32[]{:S(2)}, u32[]{:S(2)}) %all-to-all-start) | async-done | bytes 1474592 | tf_op jit(solution)/shard_map/all_to_all | solution.py:29
  49.5 0.1 reduce_sum.323
  49.8 4.2 %collective-permute-start.4 = (f32[23,12,128]{2,1,0:T(8,128)S(1)}, f32[23,12,128]{2,1,0:T(8,128)S(1)}, u32[]{:S(2)}, u32[]{:S(2)}) collective-permute-start(f32[23,12,128]{2,1,0:T(8,128)S(1)} %get-tuple-element.112), channel_id=1, source_target_pairs={{1,16},{2,17},{3,18},{4,19},{5,20},{6,21},{7,22},{8,23},{9,24},{10... | collective-permute-start | bytes 423944 | tf_op jit(solution)/shard_map/ppermute | solution.py:23
  54.0 0.1 collective-permute-start.5
  54.1 3.1 %collective-permute-done.4 = f32[23,12,128]{2,1,0:T(8,128)S(1)} collective-permute-done((f32[23,12,128]{2,1,0:T(8,128)S(1)}, f32[23,12,128]{2,1,0:T(8,128)S(1)}, u32[]{:S(2)}, u32[]{:S(2)}) %collective-permute-start.4) | collective-permute-done | bytes 141344 | tf_op jit(solution)/shard_map/ppermute | solution.py:23
  57.2 0.0 collective-permute-done.5
  57.5 0.1 select_maximum_fusion.1
  57.7 0.2 fusion.44
  57.9 0.2 fusion.56
  58.2 0.1 fusion.89
  58.3 0.1 fusion.77
  58.6 11.6 %all_to_all.15 = f32[8,13,8,128]{3,2,1,0:T(8,128)S(1)} all-to-all(f32[8,13,8,128]{3,2,1,0:T(8,128)S(1)} %broadcast_in_dim.48), channel_id=1, replica_groups={{0,32,64,96,128,160,192,224},{16,48,80,112,144,176,208,240},{1,33,65,97..., dimensions={0} | all-to-all | bytes 851968 | tf_op jit(solution)/shard_map/all_to_all | solution.py:29
  70.2 0.0 collective-permute-start.6
  70.2 1.8 %collective-permute-done.6 = f32[8,13,8,128]{3,2,1,0:T(8,128)S(1)} collective-permute-done((f32[8,13,8,128]{3,2,1,0:T(8,128)S(1)}, f32[8,13,8,128]{3,2,1,0:T(8,128)S(1)}, u32[]{:S(2)}, u32[]{:S(2)}) %collective-permute-start.6) | collective-permute-done | bytes 426016 | tf_op jit(solution)/shard_map/ppermute | solution.py:12
  71.9 0.6 broadcast_in_dim.49
  72.6 11.3 %all-to-all-start.2 = ((f32[16,8,128]{2,1,0:T(8,128)}), f32[16,8,128]{2,1,0:T(8,128)S(1)}, u32[]{:S(2)}, u32[]{:S(2)}) async-start(f32[16,8,128]{2,1,0:T(8,128)} %broadcast_in_dim.49), calls=%async_computation.2 | async-start | bytes 131072 | tf_op jit(solution)/shard_map/all_to_all | solution.py:178
  83.9 0.1 select_bitcast_fusion.1
  84.0 0.1 pad_maximum_fusion
  84.1 8.7 %all-to-all-done.2 = f32[16,8,128]{2,1,0:T(8,128)S(1)} async-done(((f32[16,8,128]{2,1,0:T(8,128)}), f32[16,8,128]{2,1,0:T(8,128)S(1)}, u32[]{:S(2)}, u32[]{:S(2)}) %all-to-all-start.2) | async-done | bytes 65568 | tf_op jit(solution)/shard_map/all_to_all | solution.py:178
  92.8 0.1 reduce_sum.329
  92.9 0.7 fusion.98
  98.7 0.1 fusion.5
  98.8 0.7 copy.87
  99.5 0.7 copy.88
  (74 shorter events, 1.0 us)
Async XLA Ops:
  0.6 10.9 %copy-start.2 = (f32[1,2,3,4,64,128]{5,4,3,2,1,0:T(8,128)S(1)}, f32[1,2,3,4,64,128]{5,4,3,2,1,0:T(8,128)}, u32[]{:S(2)}) copy-start(f32[1,2,3,4,64,128]{5,4,3,2,1,0:T(8,128)} %param.3) | copy-start | bytes 2359300
  2.8 12.0 %collective-permute-start = (f32[7,64,128]{2,1,0:T(8,128)S(1)}, f32[7,64,128]{2,1,0:T(8,128)S(1)}, u32[]{:S(2)}, u32[]{:S(2)}) collective-permute-start(f32[7,64,128]{2,1,0:T(8,128)S(1)} %get-tuple-element.89), channel_id=1, source_target_pairs={{0,1},{1,2},{2,3},{3,4},{4,5},{5,6},{6,7},{7,8},{8,9},{9,10},{10,1... | collective-permute-start | bytes 688136 | tf_op jit(solution)/shard_map/ppermute | solution.py:23
  4.1 11.2 %collective-permute-start.2 = (f32[7,64,128]{2,1,0:T(8,128)S(1)}, f32[7,64,128]{2,1,0:T(8,128)S(1)}, u32[]{:S(2)}, u32[]{:S(2)}) collective-permute-start(f32[7,64,128]{2,1,0:T(8,128)S(1)} %get-tuple-element.88), channel_id=1, source_target_pairs={{1,16},{2,17},{3,18},{4,19},{5,20},{6,21},{7,22},{8,23},{9,24},{10... | collective-permute-start | bytes 688136 | tf_op jit(solution)/shard_map/ppermute | solution.py:23
  11.8 3.6 %collective-permute-start.1 = (f32[2,3,3,64,128]{4,3,2,1,0:T(8,128)S(1)}, f32[2,3,3,64,128]{4,3,2,1,0:T(8,128)S(1)}, u32[]{:S(2)}, u32[]{:S(2)}) collective-permute-start(f32[2,3,3,64,128]{4,3,2,1,0:T(8,128)S(1)} %get-tuple-element.81), channel_id=1, source_target_pairs={{0,16},{16,0},{32,48},{48,32},{64,80},{80,64},{96,112},{112,96},{1... | collective-permute-start | bytes 1769480 | tf_op jit(solution)/shard_map/ppermute | solution.py:12
  12.5 1.5 %collective-permute-start.3 = (f32[1,1]{1,0:T(1,128)}, f32[1,1]{1,0:T(1,128)}, u32[]{:S(2)}, u32[]{:S(2)}) collective-permute-start(f32[1,1]{1,0:T(1,128)} %bitcast.25), channel_id=1, source_target_pairs={{0,16},{16,0},{32,48},{48,32},{64,80},{80,64},{96,112},{112,96},{1... | collective-permute-start | bytes 20 | tf_op jit(solution)/shard_map/ppermute | solution.py:12
  14.8 0.8 copy-start
  17.4 1.0 %copy-start.1 = (f32[3,64,128]{2,1,0:T(8,128)S(1)}, f32[3,64,128]{2,1,0:T(8,128)}, u32[]{:S(2)}) copy-start(f32[3,64,128]{2,1,0:T(8,128)} %copy-done) | copy-start | bytes 294916
  17.5 1.0 %slice-start = ((f32[3,64,128]{2,1,0:T(8,128)}), f32[2,64,128]{2,1,0:T(8,128)S(1)}, s32[]{:S(2)}) async-start(f32[3,64,128]{2,1,0:T(8,128)} %copy-done), calls=%async_computation.3 | async-start | bytes 131072 | tf_op jit(solution)/shard_map/slice | solution.py:61
  24.8 24.7 %all-to-all-start = ((f32[8,360,128]{2,1,0:T(8,128)}), f32[8,360,128]{2,1,0:T(8,128)S(1)}, u32[]{:S(2)}, u32[]{:S(2)}) async-start(f32[8,360,128]{2,1,0:T(8,128)} %constant_dynamic-update-slice_fusion.15), calls=%async_computation | async-start | bytes 2949120 | tf_op jit(solution)/shard_map/all_to_all | solution.py:29
  49.8 7.4 %collective-permute-start.4 = (f32[23,12,128]{2,1,0:T(8,128)S(1)}, f32[23,12,128]{2,1,0:T(8,128)S(1)}, u32[]{:S(2)}, u32[]{:S(2)}) collective-permute-start(f32[23,12,128]{2,1,0:T(8,128)S(1)} %get-tuple-element.112), channel_id=1, source_target_pairs={{1,16},{2,17},{3,18},{4,19},{5,20},{6,21},{7,22},{8,23},{9,24},{10... | collective-permute-start | bytes 423944 | tf_op jit(solution)/shard_map/ppermute | solution.py:23
  54.0 3.3 %collective-permute-start.5 = (f32[23,12,128]{2,1,0:T(8,128)S(1)}, f32[23,12,128]{2,1,0:T(8,128)S(1)}, u32[]{:S(2)}, u32[]{:S(2)}) collective-permute-start(f32[23,12,128]{2,1,0:T(8,128)S(1)} %get-tuple-element.111), channel_id=1, source_target_pairs={{0,16},{16,0},{32,48},{48,32},{64,80},{80,64},{96,112},{112,96},{1... | collective-permute-start | bytes 423944 | tf_op jit(solution)/shard_map/ppermute | solution.py:12
  70.2 1.8 %collective-permute-start.6 = (f32[8,13,8,128]{3,2,1,0:T(8,128)S(1)}, f32[8,13,8,128]{3,2,1,0:T(8,128)S(1)}, u32[]{:S(2)}, u32[]{:S(2)}) collective-permute-start(f32[8,13,8,128]{3,2,1,0:T(8,128)S(1)} %all_to_all.15), channel_id=1, source_target_pairs={{0,16},{16,0},{32,48},{48,32},{64,80},{80,64},{96,112},{112,96},{1... | collective-permute-start | bytes 1277960 | tf_op jit(solution)/shard_map/ppermute | solution.py:12
  72.6 20.2 %all-to-all-start.2 = ((f32[16,8,128]{2,1,0:T(8,128)}), f32[16,8,128]{2,1,0:T(8,128)S(1)}, u32[]{:S(2)}, u32[]{:S(2)}) async-start(f32[16,8,128]{2,1,0:T(8,128)} %broadcast_in_dim.49), calls=%async_computation.2 | async-start | bytes 131072 | tf_op jit(solution)/shard_map/all_to_all | solution.py:178

commit v3 on v0

v3 whole, which is shorter than its diff:
```python
import functools

import jax
import jax.numpy as jnp
from jax import lax
from jax.experimental import pallas as pl
from jax.experimental.pallas import tpu as pltpu
from jax.sharding import PartitionSpec as P

DAMPING = 0.05
ROWS = 8
VMEM_BYTES = 12 << 20

NAMES = ("zr", "zi", "zyr", "zyi", "zxr", "zxi", "rr", "ri", None, None, None, "d", "yr", "yi", "xr", "xi", "yxr", "yxi", None, None)
MAIN = {name: k for k, name in enumerate(NAMES) if name}
AROUND = {
    8: (("zyr", 0, 1, 2), ("zyi", 3, 1, 2), ("zr", 6, 1, 1)),
    9: (("zi", 0, 1, 1), ("zxr", 2, 1, 1), ("zxi", 4, 1, 1), ("xi", 6, 1, 1)),
    10: (("rr", 0, 2, 2), ("ri", 4, 2, 2)),
    18: (("yr", 0, 1, 2), ("yi", 3, 1, 2), ("d", 6, 1, 1)),
    19: (("yxr", 0, 1, 2), ("yxi", 3, 1, 2), ("xr", 6, 1, 1)),
}
PLANE = len(NAMES)
BEYOND = 11


def swap_cores(array):
    pairs = [(i, i ^ 1) for i in range(lax.axis_size("freq"))]
    return lax.ppermute(array, "freq", pairs)


def to_slabs(array, first_up, cross):
    peers, slabs = lax.axis_size("freq"), lax.axis_size("gz")
    pairs = []
    for f in range(peers):
        for g in range(slabs):
            to = g + 1 if f % 2 == first_up else g - 1
            if 0 <= to < slabs:
                pairs.append((f * slabs + g, (f ^ cross) * slabs + to))
    return lax.ppermute(array, ("freq", "gz"), pairs)


def over_chips(parts):
    peers = lax.axis_size("freq")
    groups = [list(range(core, peers, 2)) for core in range(2)]
    return lax.all_to_all(parts, "freq", split_axis=0, concat_axis=0, tiled=True, axis_index_groups=groups)


def rows_of(shape, dim):
    return lax.broadcasted_iota(jnp.int32, shape, dim)


def nxt(x, dim):
    size = x.shape[dim]
    return jnp.where(rows_of(x.shape, dim) == size - 1, 0.0, pltpu.roll(x, size - 1, dim))


def prv(x, dim):
    return jnp.where(rows_of(x.shape, dim) == 0, 0.0, pltpu.roll(x, 1, dim))


def stencil_kernel(place, kappas, field, tissue, same, cross, mid, out, acc):
    core, bottom = place[0], place[1]
    low, floor = core == 0, place[1] == 1
    ny, nx = field.shape[-2:]
    shape = (ny, nx)

    def cell(group, part, comp, k):
        flat = part * 3 + comp
        if group == 0:
            own, edge = field, same
            if 1 <= k <= 2:
                return own[part, comp, 2 * core + k - 1]
            inside = own[part, comp, 1 if k == 0 else 2]
        else:
            edge = cross
            if 1 <= k <= 2:
                return mid[flat * 3 + core + k - 1]
            inside = mid[flat * 3 + (0 if k == 0 else 2)]
        outside = edge[flat]
        if k == 0:
            outside = jnp.where(floor, cell(group, part, comp, 1), outside)
            return jnp.where(low, outside, inside)
        return jnp.where(low, inside, outside)

    masks = [tissue[2 * core + k].astype(jnp.float32) for k in range(2)]
    masks.append(jnp.where(low, tissue[2].astype(jnp.float32), same[6]))
    other_kappa = mid[18]

    for plane in range(2):
        here, above = masks[plane], masks[plane + 1]
        here_y, here_x = nxt(here, 0), nxt(here, 1)
        for group in range(2):
            kappa = kappas[0] if group == 0 else other_kappa
            scales = [m * kappa for m in (here, above, here_y, here_x)]
            for comp in range(3):
                u, gz, gp, gy, gx, hy, hx, s, t = ([] for _ in range(9))
                for part in range(2):
                    below, mine, up = (cell(group, part, comp, plane + k) for k in range(3))
                    right_y, right_x = nxt(mine, 0), nxt(mine, 1)
                    gz.append(up - mine)
                    gp.append(mine - below)
                    gy.append(right_y - mine)
                    gx.append(right_x - mine)
                    hy.append(prv(gy[-1], 0))
                    hx.append(prv(gx[-1], 1))
                    s.append(gz[-1] + gy[-1] + gx[-1])
                    t.append([mine * scales[0], up * scales[1], right_y * scales[2], right_x * scales[3]])

                def re(a, b):
                    return a[0] * b[0] + a[1] * b[1]

                def im(a, b):
                    return a[0] * b[1] - a[1] * b[0]

                new = [re(s, s), re(gz, gz), re(gy, gy), re(gx, gx)]
                for a, b in ((s, gp), (s, hy), (s, hx), (gp, hy), (gp, hx), (hy, hx)):
                    new += [re(a, b), im(a, b)]
                ts = [[t[0][k], t[1][k]] for k in range(4)]
                for f in (re, im):
                    new.append(f(gz, ts[1]) + f(gy, ts[2]) + f(gx, ts[3]) - f(s, ts[0]))
                first = group == 0 and comp == 0
                for k, value in enumerate(new):
                    acc[k] = value if first else acc[k] + value
        done = {"d": here * acc[0] + above * acc[1] + here_y * acc[2] + here_x * acc[3]}
        for k, name in enumerate(("z", "y", "x", "zy", "zx", "yx")):
            signed = -here if k < 3 else here
            done[name + "r"] = signed * acc[4 + 2 * k]
            done[name + "i"] = signed * acc[5 + 2 * k]
        done["rr"], done["ri"] = acc[16], acc[17]
        row = rows_of(shape, 0)
        lane = row % ROWS
        for name, k in MAIN.items():
            out[:, plane * PLANE + k] = done[name].reshape(ny // ROWS, ROWS, nx)
        for k, parts in AROUND.items():
            tile = jnp.zeros(shape, jnp.float32)
            for name, start, before, after in parts:
                moved = pltpu.roll(done[name], start + before, 0)
                back = pltpu.roll(moved, ny - ROWS, 0)
                moved = jnp.where(row < ROWS, 0.0, moved)
                back = jnp.where(row >= ny - ROWS, 0.0, back)
                tile = jnp.where((lane >= start) & (lane < start + before), moved, tile)
                tile = jnp.where((lane >= start + before) & (lane < start + before + after), back, tile)
            out[:, plane * PLANE + k] = tile.reshape(ny // ROWS, ROWS, nx)


def around_of(name):
    for tile, parts in AROUND.items():
        for other, start, before, after in parts:
            if other == name:
                return tile, start, before, after
    raise KeyError(name)


def vectors_kernel(place, mine, near, far, out):
    low = place[0] == 0
    nx = mine.shape[-1]
    half = rows_of((ROWS, nx), 0)

    def spread(get, name):
        tile, start, before, after = around_of(name)
        main = pltpu.roll(get(MAIN[name]), 4, 0)
        side = get(tile)
        turn = (4 - before - start) % ROWS
        side = pltpu.roll(side, turn, 0) if turn else side
        head = jnp.where(half >= 4, main, jnp.where(half >= 4 - before, side, 0.0))
        tail = jnp.where(half < 4, main, jnp.where(half < 4 + after, side, 0.0))
        return jnp.concatenate([head, tail])

    def below(k):
        return jnp.where(low, far[k], near[k])

    def above(k):
        return jnp.where(low, near[k], far[k])

    sources = {
        -2: lambda k: below(PLANE + k),
        -1: below,
        0: lambda k: mine[0, k],
        1: lambda k: mine[1, k],
        2: above,
        3: lambda k: above(PLANE + k),
    }
    couplings = ("z", "zy", "zx", "y", "x", "yx")
    coefs = {}
    for p in range(-1, 4):
        names = couplings[:3] if p == 3 else couplings
        coefs[p] = {n: (spread(sources[p], n + "r"), spread(sources[p], n + "i")) for n in names}
        if p < 3:
            coefs[p]["d"] = spread(sources[p], "d") + DAMPING
    v0 = {p: (spread(sources[p], "rr"), spread(sources[p], "ri")) for p in range(-2, 4)}

    def mul(c, m):
        return c[0] * m[0] - c[1] * m[1], c[0] * m[1] + c[1] * m[0]

    def conj(c, m):
        return c[0] * m[0] + c[1] * m[1], c[0] * m[1] - c[1] * m[0]

    def plus(*terms):
        return tuple(functools.reduce(lambda a, b: a + b, part) for part in zip(*terms))

    def ahead_y(x):
        return pltpu.roll(x, 2 * ROWS - 1, 0)

    def behind_y(x):
        return pltpu.roll(x, 1, 0)

    def apply(field, planes):
        stepped = {}
        flat = {}
        for p in planes + [planes[-1] + 1]:
            c, m = coefs[p], field[p]
            back = field.get(p - 1)
            my = tuple(behind_y(v) for v in m)
            mx = tuple(prv(v, 1) for v in m)
            stepped[p] = plus(conj(c["z"], m), mul(c["zy"], my), mul(c["zx"], mx))
            if p > planes[-1]:
                continue
            ys = plus(conj(c["y"], m), conj(c["zy"], back), mul(c["yx"], mx))
            xs = plus(conj(c["x"], m), conj(c["zx"], back), conj(c["yx"], my))
            flat[p] = plus(
                tuple(c["d"] * v for v in m),
                mul(c["z"], back),
                mul(c["y"], my),
                mul(c["x"], mx),
                tuple(ahead_y(v) for v in ys),
                tuple(nxt(v, 1) for v in xs),
            )
        return {p: plus(flat[p], stepped[p + 1]) for p in planes}

    v1 = apply(v0, [-1, 0, 1, 2])
    v2 = apply(v1, [0, 1])

    def own(x):
        return jnp.where(half < 4, pltpu.roll(x[:ROWS], 4, 0), pltpu.roll(x[ROWS:], 4, 0))

    held = [[[own(v[p][part]) for p in range(2)] for part in range(2)] for v in (v0, v1, v2)]
    note = jnp.zeros((ROWS, nx), jnp.float32)
    for k, (a, b) in enumerate(((0, 0), (0, 1), (1, 1), (1, 2))):
        total = sum(held[a][part][p] * held[b][part][p] for part in range(2) for p in range(2))
        note = jnp.where(half == k, jnp.sum(total, axis=0, keepdims=True), note)
    tiles = [tile for vector in held for parts in vector for tile in parts] + [note]
    for k, tile in enumerate(tiles):
        for chip in range(out.shape[0]):
            out[chip, k] = tile


def outputs_kernel(place, sums, gathered, others, modulus, residual):
    core = place[0]
    chips = gathered.shape[0]
    total = sums[0]
    for k in range(1, sums.shape[0]):
        total = total + sums[k]
    total = jnp.broadcast_to(jnp.sum(total, axis=1, keepdims=True), total.shape)
    m0, m1, m2, m3 = (total[k : k + 1] for k in range(4))
    step = m0 / m1
    norm = step * step * m2 - m0
    grown = 1.0 + norm / m0
    curve = grown * grown * m1 - 2.0 * step * grown * m2 + step * step * m3
    second = norm / curve
    shape = (chips, ROWS, total.shape[-1])
    p = jnp.broadcast_to((step + second * grown).reshape(1, 1, -1), shape)
    q = jnp.broadcast_to((step * second).reshape(1, 1, -1), shape)
    for source, first in ((gathered, 2 * core), (others, 2 - 2 * core)):
        for part in range(2):
            for plane in range(2):
                v0, v1, v2 = (source[:, 4 * k + 2 * part + plane] for k in range(3))
                flat = (chips * ROWS, shape[-1])
                modulus[part, first + plane] = (p * v0 - q * v1).reshape(flat)
                residual[part, first + plane] = (v0 - p * v1 + q * v2).reshape(flat)


def run(kernel, shapes, place, *arrays, scratch=(), scalars=1):
    vmem = pl.BlockSpec(memory_space=pltpu.VMEM)
    smem = pl.BlockSpec(memory_space=pltpu.SMEM)
    return pl.pallas_call(
        kernel,
        out_shape=shapes,
        in_specs=[smem] * scalars + [vmem] * (len(arrays) + 1 - scalars),
        out_specs=jax.tree.map(lambda _: vmem, shapes),
        scratch_shapes=list(scratch),
        compiler_params=pltpu.CompilerParams(vmem_limit_bytes=VMEM_BYTES),
    )(place, *arrays)


def body(displacement, freq_index, tissue):
    core = lax.axis_index("freq") % 2
    chips = lax.axis_size("freq") // 2
    slabs = lax.axis_size("gz")
    low = core == 0
    field = displacement[0]
    ny, nx = field.shape[-2:]
    tile = (ROWS, nx)
    kappa = 0.2 * (freq_index + 1).astype(jnp.float32)
    place = jnp.stack([core, (low & (lax.axis_index("gz") == 0)).astype(jnp.int32)])

    def shape(*dims):
        return jax.ShapeDtypeStruct(dims, jnp.float32)

    first = jnp.concatenate([field[:, :, 0].reshape(6, ny, nx), tissue[0:1].astype(jnp.float32)])
    last = jnp.concatenate([field[:, :, 3].reshape(6, ny, nx), tissue[3:4].astype(jnp.float32)])
    same = to_slabs(jnp.where(low, last, first), 0, 0)
    cross = to_slabs(jnp.where(low, first, last), 1, 1)
    sent = jnp.where(low, field[:, :, 1:], field[:, :, :3]).reshape(18, ny, nx)
    mid = swap_cores(jnp.concatenate([sent, jnp.broadcast_to(kappa[0], (1, ny, nx))]))

    parts = run(
        stencil_kernel,
        shape(chips, 2 * PLANE, *tile),
        place,
        kappa,
        field,
        tissue,
        same,
        cross,
        mid,
        scratch=[pltpu.VMEM((18, ny, nx), jnp.float32)],
        scalars=2,
    )
    mine = over_chips(parts).sum(axis=0).reshape(2, PLANE, *tile)

    down = jnp.concatenate([mine[0], mine[1, :BEYOND]])
    up = jnp.concatenate([mine[1], mine[0, :BEYOND]])
    near = swap_cores(jnp.where(low, up, down))
    far = to_slabs(jnp.where(low, down, up), 1, 1)
    tiles = run(vectors_kernel, shape(chips, 13, *tile), place, mine, near, far)

    gathered = over_chips(tiles)
    others = swap_cores(gathered)
    sums = (gathered[:, 12] + others[:, 12]).sum(axis=0)
    sums = lax.all_to_all(jnp.broadcast_to(sums, (slabs, *tile)), "gz", split_axis=0, concat_axis=0, tiled=True)
    result = shape(2, 4, ny, nx)
    return tuple(run(outputs_kernel, (result, result), place, sums, gathered, others))


def solution(mesh):
    placed = (P("freq", None, None, "gz", None, None), P("freq"), P("gz", None, None))
    return jax.shard_map(
        body,
        mesh=mesh,
        in_specs=placed,
        out_specs=(P(None, "gz", None, None), P(None, "gz", None, None)),
        check_vma=False,
    )
```

time: 204 us -> 84.3 us (0.41)
  blocking collectives: 130 us -> 54 us
  waiting for transfers between devices: 34.8 us -> 10.6 us
  other arithmetic: 10.9 us -> 1.63 us
  local copies, waits for them, and re-layouts: 7.18 us -> 0.13 us
  Pallas kernels: 0 us -> 5.26 us
  between operations: 5.75 us -> 1.43 us
  starting transfers between devices: 14.4 us -> 11 us
    all_to_all x9 -> x3, blocking collectives: 130 us -> 54 us  [the longest x2 33.6 us: over_chips(): lax.all_to_all(parts, 'freq', split_axis=0, concat_axis=0, tiled=True, ax...]
    ppermute x6, waiting for transfers between devices: 26.7 us -> 10.6 us  [the longest x3 8.98 us: to_slabs(): return lax.ppermute(array, ('freq', 'gz'), pairs)]
    all_to_all x1 -> x0, waiting for transfers between devices: 8.07 us -> none  [copy_for_each(): return lax.all_to_all(copies, axis, split_axis=0, concat_axis=0, tiled=True)]
    reduce_sum x18 -> x2, other arithmetic: 6.2 us -> 0.08 us  [the longest x1 0.07 us: body(): mine = over_chips(parts).sum(axis=0).reshape(2, PLANE, *tile)]
    pallas_call x0 -> x3, Pallas kernels: none -> 5.26 us  [run(): pl.pallas_call(kernel, out_shape=shapes, in_specs=[smem] * scalars + [vme...]
    slice x17 -> x2, local copies, waits for them, and re-layouts: 3.75 us -> 0.04 us  [the longest x1 0.03 us: body(): field[:, :, 3].reshape(6, ny, nx)]
    all_to_all x1 -> x0, starting transfers between devices: 3.47 us -> none  [copy_for_each(): return lax.all_to_all(copies, axis, split_axis=0, concat_axis=0, tiled=True)]
    broadcast_in_dim x7 -> x1, local copies, waits for them, and re-layouts: 3.25 us -> 0.01 us  [body(): jnp.broadcast_to(sums, (slabs, *tile))]
  transfers between devices with their start and end apart: 7 -> 6, of which waited for: 7 -> 4; matrix products, arithmetic and copies ran while one was open for 2% -> 0% of each run, Pallas kernels for 0% -> 0%
where the time goes in v3:
time: 84.3 us; the launch traced here: 84 us
  blocking collectives  54 us (64%)
  starting transfers between devices  11 us (13%)
  waiting for transfers between devices  10.6 us (13%)
  Pallas kernels  5.26 us (6%)
  other arithmetic  1.63 us (2%)
  between operations  1.43 us (2%)
    all_to_all x2, blocking collectives, over_chips(): lax.all_to_all(parts, 'freq', split_axis=0, concat_axis=0, tiled=True, ax...  33.6 us
    all_to_all x1, blocking collectives, body(): lax.all_to_all(jnp.broadcast_to(sums, (slabs, *tile)), 'gz', split_axis=0...  20.4 us
    ppermute x3, waiting for transfers between devices, to_slabs(): return lax.ppermute(array, ('freq', 'gz'), pairs)  8.98 us
    ppermute x3, starting transfers between devices, to_slabs(): return lax.ppermute(array, ('freq', 'gz'), pairs)  7.38 us
    pallas_call x3, Pallas kernels, run(): pl.pallas_call(kernel, out_shape=shapes, in_specs=[smem] * scalars + [vme...  5.26 us
    ppermute x3, starting transfers between devices, swap_cores(): return lax.ppermute(array, 'freq', pairs)  3.62 us
  transfers between devices with their start and end apart: 6, of which 4 were waited for; matrix products, arithmetic and copies ran while one was open for 0% of the time, Pallas kernels for 0%

profile of v3, /device:TPU:1, one launch (start us, length us, event | category | flops | bytes accessed | tf_op | source)
XLA Modules:
  0.0 84.0 jit_solution(5853375426729461645)
XLA Ops:
  1.3 0.0 copy-start.1
  1.3 0.0 copy-start
  1.3 1.4 %slice_select_fusion = f32[2,3,3,64,128]{4,3,2,1,0:T(8,128)S(1)} fusion(f32[2,3,4,64,128]{4,3,2,1,0:T(8,128)} %bitcast.12, pred[]{:T(512)S(6)} %eq.8), kind=kLoop, calls=%fused_computation | loop fusion | flops 147456 | bytes 1769473 | tf_op jit(solution)/shard_map/jit(_where)/select_n | solution.py:304
  2.7 0.1 concatenate.17
  2.8 3.3 %collective-permute-start.2 = (f32[19,64,128]{2,1,0:T(8,128)S(1)}, f32[19,64,128]{2,1,0:T(8,128)S(1)}, u32[]{:S(2)}, u32[]{:S(2)}) collective-permute-start(f32[19,64,128]{2,1,0:T(8,128)S(1)} %concatenate.17), channel_id=1, source_target_pairs={{0,16},{16,0},{32,48},{48,32},{64,80},{80,64},{96,112},{112,96},{1... | collective-permute-start | bytes 1867784 | tf_op jit(solution)/shard_map/ppermute | solution.py:29
  6.1 0.0 copy-done.1
  6.1 0.0 copy-done
  6.2 1.9 %collective-permute-start.1 = (f32[7,64,128]{2,1,0:T(8,128)S(1)}, f32[7,64,128]{2,1,0:T(8,128)S(1)}, u32[]{:S(2)}, u32[]{:S(2)}) collective-permute-start(f32[7,64,128]{2,1,0:T(8,128)S(1)} %get-tuple-element.4), channel_id=1, source_target_pairs={{1,16},{2,17},{3,18},{4,19},{5,20},{6,21},{7,22},{8,23},{9,24},{10... | collective-permute-start | bytes 688136 | tf_op jit(solution)/shard_map/ppermute | solution.py:40
  8.1 1.3 %collective-permute-start = (f32[7,64,128]{2,1,0:T(8,128)S(1)}, f32[7,64,128]{2,1,0:T(8,128)S(1)}, u32[]{:S(2)}, u32[]{:S(2)}) collective-permute-start(f32[7,64,128]{2,1,0:T(8,128)S(1)} %get-tuple-element.5), channel_id=1, source_target_pairs={{0,1},{1,2},{2,3},{3,4},{4,5},{5,6},{6,7},{7,8},{8,9},{9,10},{10,1... | collective-permute-start | bytes 688136 | tf_op jit(solution)/shard_map/ppermute | solution.py:40
  9.4 0.1 pad_add_fusion.place
  9.5 5.1 %collective-permute-done.1.cross = f32[7,64,128]{2,1,0:T(8,128)S(1)} collective-permute-done((f32[7,64,128]{2,1,0:T(8,128)S(1)}, f32[7,64,128]{2,1,0:T(8,128)S(1)}, u32[]{:S(2)}, u32[]{:S(2)}) %collective-permute-start.1) | collective-permute-done | bytes 229408 | tf_op jit(solution)/shard_map/ppermute | solution.py:40
  14.6 1.4 %collective-permute-done.same = f32[7,64,128]{2,1,0:T(8,128)S(1)} collective-permute-done((f32[7,64,128]{2,1,0:T(8,128)S(1)}, f32[7,64,128]{2,1,0:T(8,128)S(1)}, u32[]{:S(2)}, u32[]{:S(2)}) %collective-permute-start) | collective-permute-done | bytes 229408 | tf_op jit(solution)/shard_map/ppermute | solution.py:40
  16.0 0.0 collective-permute-done.2.mid
  16.0 2.9 %shard_map.50 = f32[8,40,8,128]{3,2,1,0:T(8,128)S(1)} custom-call(s32[2]{0:T(128)S(1)} %pad_add_fusion.place, f32[1]{0:T(128)} %mul.3.kappas, f32[2,3,4,64,128]{4,3,2,1,0:T(8,128)S(1)} %bitcast.14, s32[4,64,128]{2,1,0:T(8,128)S(1)} %copy-done.1, f32[7,64,128]{2,1,0:T(8,128)S(1)} %collective-permute-done.same, ...), custom_call_target="tpu_custom_call" | custom-call | tf_op jit(solution)/shard_map/pallas_call | solution.py:276
  18.9 22.2 %all_to_all.15 = f32[8,40,8,128]{3,2,1,0:T(8,128)S(1)} all-to-all(f32[8,40,8,128]{3,2,1,0:T(8,128)S(1)} %shard_map.50), channel_id=1, replica_groups={{0,32,64,96,128,160,192,224},{16,48,80,112,144,176,208,240},{1,33,65,97..., dimensions={0} | all-to-all | bytes 2621440 | tf_op jit(solution)/shard_map/all_to_all | solution.py:46
  41.1 0.1 reduce_sum.18
  41.2 4.2 %collective-permute-start.4 = (f32[31,8,128]{2,1,0:T(8,128)S(1)}, f32[31,8,128]{2,1,0:T(8,128)S(1)}, u32[]{:S(2)}, u32[]{:S(2)}) collective-permute-start(f32[31,8,128]{2,1,0:T(8,128)S(1)} %get-tuple-element.6), channel_id=1, source_target_pairs={{1,16},{2,17},{3,18},{4,19},{5,20},{6,21},{7,22},{8,23},{9,24},{10... | collective-permute-start | bytes 380936 | tf_op jit(solution)/shard_map/ppermute | solution.py:40
  45.4 0.1 collective-permute-start.3
  45.5 2.5 %collective-permute-done.4.far = f32[31,8,128]{2,1,0:T(8,128)S(1)} collective-permute-done((f32[31,8,128]{2,1,0:T(8,128)S(1)}, f32[31,8,128]{2,1,0:T(8,128)S(1)}, u32[]{:S(2)}, u32[]{:S(2)}) %collective-permute-start.4) | collective-permute-done | bytes 127008 | tf_op jit(solution)/shard_map/ppermute | solution.py:40
  48.0 0.0 collective-permute-done.3.near
  48.0 0.8 shard_map.51
  48.8 11.5 %all_to_all.16.gathered = f32[8,13,8,128]{3,2,1,0:T(8,128)S(1)} all-to-all(f32[8,13,8,128]{3,2,1,0:T(8,128)S(1)} %shard_map.51), channel_id=1, replica_groups={{0,32,64,96,128,160,192,224},{16,48,80,112,144,176,208,240},{1,33,65,97..., dimensions={0} | all-to-all | bytes 851968 | tf_op jit(solution)/shard_map/all_to_all | solution.py:46
  60.3 0.2 collective-permute-start.5
  60.5 1.6 %collective-permute-done.5.others = f32[8,13,8,128]{3,2,1,0:T(8,128)S(1)} collective-permute-done((f32[8,13,8,128]{3,2,1,0:T(8,128)S(1)}, f32[8,13,8,128]{3,2,1,0:T(8,128)S(1)}, u32[]{:S(2)}, u32[]{:S(2)}) %collective-permute-start.5) | collective-permute-done | bytes 426016 | tf_op jit(solution)/shard_map/ppermute | solution.py:29
  62.1 20.4 %all_to_all.17.sums = f32[16,8,128]{2,1,0:T(8,128)S(1)} all-to-all(f32[16,8,128]{2,1,0:T(8,128)S(1)} %broadcast_in_dim.4), channel_id=1, replica_groups=mesh['freq'=16,'gz'=16] {'gz'}, dimensions={0} | all-to-all | bytes 131072 | tf_op jit(solution)/shard_map/all_to_all | solution.py:331
  82.5 1.5 %shard_map.52 = (f32[2,4,64,128]{3,2,1,0:T(8,128)}, f32[2,4,64,128]{3,2,1,0:T(8,128)}) custom-call(s32[2]{0:T(128)S(1)} %pad_add_fusion.place, f32[16,8,128]{2,1,0:T(8,128)S(1)} %all_to_all.17.sums, f32[8,13,8,128]{3,2,1,0:T(8,128)S(1)} %all_to_all.16.gathered, f32[8,13,8,128]{3,2,1,0:T(8,128)S(1)} %collective-permute-done.5.others), custom_call_target="tpu_custom_call" | custom-call | tf_op jit(solution)/shard_map/pallas_call | solution.py:276
  (8 shorter events, 0.1 us)
Async XLA Ops:
  1.3 4.8 %copy-start.1 = (s32[4,64,128]{2,1,0:T(8,128)S(1)}, s32[4,64,128]{2,1,0:T(8,128)}, u32[]{:S(2)}) copy-start(s32[4,64,128]{2,1,0:T(8,128)} %tissue.1) | copy-start | bytes 393220
  1.3 4.8 %copy-start = (f32[1,2,3,4,64,128]{5,4,3,2,1,0:T(8,128)S(1)}, f32[1,2,3,4,64,128]{5,4,3,2,1,0:T(8,128)}, u32[]{:S(2)}) copy-start(f32[1,2,3,4,64,128]{5,4,3,2,1,0:T(8,128)} %param.3) | copy-start | bytes 2359300
  2.8 13.2 %collective-permute-start.2 = (f32[19,64,128]{2,1,0:T(8,128)S(1)}, f32[19,64,128]{2,1,0:T(8,128)S(1)}, u32[]{:S(2)}, u32[]{:S(2)}) collective-permute-start(f32[19,64,128]{2,1,0:T(8,128)S(1)} %concatenate.17), channel_id=1, source_target_pairs={{0,16},{16,0},{32,48},{48,32},{64,80},{80,64},{96,112},{112,96},{1... | collective-permute-start | bytes 1867784 | tf_op jit(solution)/shard_map/ppermute | solution.py:29
  6.2 8.4 %collective-permute-start.1 = (f32[7,64,128]{2,1,0:T(8,128)S(1)}, f32[7,64,128]{2,1,0:T(8,128)S(1)}, u32[]{:S(2)}, u32[]{:S(2)}) collective-permute-start(f32[7,64,128]{2,1,0:T(8,128)S(1)} %get-tuple-element.4), channel_id=1, source_target_pairs={{1,16},{2,17},{3,18},{4,19},{5,20},{6,21},{7,22},{8,23},{9,24},{10... | collective-permute-start | bytes 688136 | tf_op jit(solution)/shard_map/ppermute | solution.py:40
  8.1 7.9 %collective-permute-start = (f32[7,64,128]{2,1,0:T(8,128)S(1)}, f32[7,64,128]{2,1,0:T(8,128)S(1)}, u32[]{:S(2)}, u32[]{:S(2)}) collective-permute-start(f32[7,64,128]{2,1,0:T(8,128)S(1)} %get-tuple-element.5), channel_id=1, source_target_pairs={{0,1},{1,2},{2,3},{3,4},{4,5},{5,6},{6,7},{7,8},{8,9},{9,10},{10,1... | collective-permute-start | bytes 688136 | tf_op jit(solution)/shard_map/ppermute | solution.py:40
  41.2 6.8 %collective-permute-start.4 = (f32[31,8,128]{2,1,0:T(8,128)S(1)}, f32[31,8,128]{2,1,0:T(8,128)S(1)}, u32[]{:S(2)}, u32[]{:S(2)}) collective-permute-start(f32[31,8,128]{2,1,0:T(8,128)S(1)} %get-tuple-element.6), channel_id=1, source_target_pairs={{1,16},{2,17},{3,18},{4,19},{5,20},{6,21},{7,22},{8,23},{9,24},{10... | collective-permute-start | bytes 380936 | tf_op jit(solution)/shard_map/ppermute | solution.py:40
  45.4 2.6 %collective-permute-start.3 = (f32[31,8,128]{2,1,0:T(8,128)S(1)}, f32[31,8,128]{2,1,0:T(8,128)S(1)}, u32[]{:S(2)}, u32[]{:S(2)}) collective-permute-start(f32[31,8,128]{2,1,0:T(8,128)S(1)} %get-tuple-element.7), channel_id=1, source_target_pairs={{0,16},{16,0},{32,48},{48,32},{64,80},{80,64},{96,112},{112,96},{1... | collective-permute-start | bytes 380936 | tf_op jit(solution)/shard_map/ppermute | solution.py:29
  60.3 1.8 %collective-permute-start.5 = (f32[8,13,8,128]{3,2,1,0:T(8,128)S(1)}, f32[8,13,8,128]{3,2,1,0:T(8,128)S(1)}, u32[]{:S(2)}, u32[]{:S(2)}) collective-permute-start(f32[8,13,8,128]{3,2,1,0:T(8,128)S(1)} %all_to_all.16.gathered), channel_id=1, source_target_pairs={{0,16},{16,0},{32,48},{48,32},{64,80},{80,64},{96,112},{112,96},{1... | collective-permute-start | bytes 1277960 | tf_op jit(solution)/shard_map/ppermute | solution.py:29

commit v4 on v3

--- a/solution.py
+++ b/solution.py
@@ -59,89 +59,91 @@
     return jnp.where(rows_of(x.shape, dim) == 0, 0.0, pltpu.roll(x, 1, dim))
 
 
-def stencil_kernel(place, kappas, field, tissue, same, cross, mid, out, acc):
-    core, bottom = place[0], place[1]
+def products(cell, kappas, here, above, out, first, acc):
+    shape = here.shape
+    ny, nx = shape
+    here_y, here_x = nxt(here, 0), nxt(here, 1)
+    for group in range(2):
+        scales = [m * kappas[group] for m in (here, above, here_y, here_x)]
+        for comp in range(3):
+            gz, gp, gy, gx, hy, hx, s, t = ([] for _ in range(8))
+            for part in range(2):
+                below, mine, up = cell(group, part, comp)
+                right_y, right_x = nxt(mine, 0), nxt(mine, 1)
+                gz.append(up - mine)
+                gp.append(mine - below)
+                gy.append(right_y - mine)
+                gx.append(right_x - mine)
+                hy.append(prv(gy[-1], 0))
+                hx.append(prv(gx[-1], 1))
+                s.append(gz[-1] + gy[-1] + gx[-1])
+                t.append([mine * scales[0], up * scales[1], right_y * scales[2], right_x * scales[3]])
+
+            def re(a, b):
+                return a[0] * b[0] + a[1] * b[1]
+
+            def im(a, b):
+                return a[0] * b[1] - a[1] * b[0]
+
+            new = [re(s, s), re(gz, gz), re(gy, gy), re(gx, gx)]
+            for a, b in ((s, gp), (s, hy), (s, hx), (gp, hy), (gp, hx), (hy, hx)):
+                new += [re(a, b), im(a, b)]
+            ts = [[t[0][k], t[1][k]] for k in range(4)]
+            for f in (re, im):
+                new.append(f(gz, ts[1]) + f(gy, ts[2]) + f(gx, ts[3]) - f(s, ts[0]))
+            for k, value in enumerate(new):
+                acc[k] = value if group == 0 and comp == 0 else acc[k] + value
+    done = {"d": here * acc[0] + above * acc[1] + here_y * acc[2] + here_x * acc[3]}
+    for k, name in enumerate(("z", "y", "x", "zy", "zx", "yx")):
+        signed = -here if k < 3 else here
+        done[name + "r"] = signed * acc[4 + 2 * k]
+        done[name + "i"] = signed * acc[5 + 2 * k]
+    done["rr"], done["ri"] = acc[16], acc[17]
+    row = rows_of(shape, 0)
+    lane = row % ROWS
+    for name, k in MAIN.items():
+        out[:, first + k] = done[name].reshape(ny // ROWS, ROWS, nx)
+    for k, parts in AROUND.items():
+        tile = jnp.zeros(shape, jnp.float32)
+        for name, start, before, after in parts:
+            moved = pltpu.roll(done[name], start + before, 0)
+            back = pltpu.roll(moved, ny - ROWS, 0)
+            moved = jnp.where(row < ROWS, 0.0, moved)
+            back = jnp.where(row >= ny - ROWS, 0.0, back)
+            tile = jnp.where((lane >= start) & (lane < start + before), moved, tile)
+            tile = jnp.where((lane >= start + before) & (lane < start + before + after), back, tile)
+        out[:, first + k] = tile.reshape(ny // ROWS, ROWS, nx)
+
+
+def kappa_of(index):
+    return 0.2 * (index[0] + 1).astype(jnp.float32)
+
+
+def inner_kernel(place, index, other_index, field, other, tissue, out, acc):
+    core = place[0]
+
+    def cell(group, part, comp):
+        source = field if group == 0 else other
+        return [source[part, comp, core + k] for k in range(3)]
+
+    here, above = (tissue[core + k].astype(jnp.float32) for k in (1, 2))
+    products(cell, (kappa_of(index), kappa_of(other_index)), here, above, out, 0, acc)
+
+
+def outer_kernel(place, index, other_index, field, other, tissue, edge, _, out, acc):
+    core = place[0]
     low, floor = core == 0, place[1] == 1
-    ny, nx = field.shape[-2:]
-    shape = (ny, nx)
-
-    def cell(group, part, comp, k):
-        flat = part * 3 + comp
-        if group == 0:
-            own, edge = field, same
-            if 1 <= k <= 2:
-                return own[part, comp, 2 * core + k - 1]
-            inside = own[part, comp, 1 if k == 0 else 2]
-        else:
-            edge = cross
-            if 1 <= k <= 2:
-                return mid[flat * 3 + core + k - 1]
-            inside = mid[flat * 3 + (0 if k == 0 else 2)]
-        outside = edge[flat]
-        if k == 0:
-            outside = jnp.where(floor, cell(group, part, comp, 1), outside)
-            return jnp.where(low, outside, inside)
-        return jnp.where(low, inside, outside)
-
-    masks = [tissue[2 * core + k].astype(jnp.float32) for k in range(2)]
-    masks.append(jnp.where(low, tissue[2].astype(jnp.float32), same[6]))
-    other_kappa = mid[18]
-
-    for plane in range(2):
-        here, above = masks[plane], masks[plane + 1]
-        here_y, here_x = nxt(here, 0), nxt(here, 1)
-        for group in range(2):
-            kappa = kappas[0] if group == 0 else other_kappa
-            scales = [m * kappa for m in (here, above, here_y, here_x)]
-            for comp in range(3):
-                u, gz, gp, gy, gx, hy, hx, s, t = ([] for _ in range(9))
-                for part in range(2):
-                    below, mine, up = (cell(group, part, comp, plane + k) for k in range(3))
-                    right_y, right_x = nxt(mine, 0), nxt(mine, 1)
-                    gz.append(up - mine)
-                    gp.append(mine - below)
-                    gy.append(right_y - mine)
-                    gx.append(right_x - mine)
-                    hy.append(prv(gy[-1], 0))
-                    hx.append(prv(gx[-1], 1))
-                    s.append(gz[-1] + gy[-1] + gx[-1])
-                    t.append([mine * scales[0], up * scales[1], right_y * scales[2], right_x * scales[3]])
-
-                def re(a, b):
-                    return a[0] * b[0] + a[1] * b[1]
-
-                def im(a, b):
-                    return a[0] * b[1] - a[1] * b[0]
-
-                new = [re(s, s), re(gz, gz), re(gy, gy), re(gx, gx)]
-                for a, b in ((s, gp), (s, hy), (s, hx), (gp, hy), (gp, hx), (hy, hx)):
-                    new += [re(a, b), im(a, b)]
-                ts = [[t[0][k], t[1][k]] for k in range(4)]
-                for f in (re, im):
-                    new.append(f(gz, ts[1]) + f(gy, ts[2]) + f(gx, ts[3]) - f(s, ts[0]))
-                first = group == 0 and comp == 0
-                for k, value in enumerate(new):
-                    acc[k] = value if first else acc[k] + value
-        done = {"d": here * acc[0] + above * acc[1] + here_y * acc[2] + here_x * acc[3]}
-        for k, name in enumerate(("z", "y", "x", "zy", "zx", "yx")):
-            signed = -here if k < 3 else here
-            done[name + "r"] = signed * acc[4 + 2 * k]
-            done[name + "i"] = signed * acc[5 + 2 * k]
-        done["rr"], done["ri"] = acc[16], acc[17]
-        row = rows_of(shape, 0)
-        lane = row % ROWS
-        for name, k in MAIN.items():
-            out[:, plane * PLANE + k] = done[name].reshape(ny // ROWS, ROWS, nx)
-        for k, parts in AROUND.items():
-            tile = jnp.zeros(shape, jnp.float32)
-            for name, start, before, after in parts:
-                moved = pltpu.roll(done[name], start + before, 0)
-                back = pltpu.roll(moved, ny - ROWS, 0)
-                moved = jnp.where(row < ROWS, 0.0, moved)
-                back = jnp.where(row >= ny - ROWS, 0.0, back)
-                tile = jnp.where((lane >= start) & (lane < start + before), moved, tile)
-                tile = jnp.where((lane >= start + before) & (lane < start + before + after), back, tile)
-            out[:, plane * PLANE + k] = tile.reshape(ny // ROWS, ROWS, nx)
+
+    def cell(group, part, comp):
+        source = field if group == 0 else other
+        outside = edge[6 * (1 - group) + 3 * part + comp]
+        mine, inside = source[part, comp, 3 * core], source[part, comp, 1 + core]
+        below = jnp.where(low, jnp.where(floor, mine, outside), inside)
+        return below, mine, jnp.where(low, inside, outside)
+
+    here = tissue[3 * core].astype(jnp.float32)
+    above = jnp.where(low, tissue[1].astype(jnp.float32), edge[12])
+    products(cell, (kappa_of(index), kappa_of(other_index)), here, above, out, PLANE, acc)
 
 
 def around_of(name):
@@ -153,7 +155,8 @@
 
 
 def vectors_kernel(place, mine, near, far, out):
-    low = place[0] == 0
+    core = place[0]
+    low = core == 0
     nx = mine.shape[-1]
     half = rows_of((ROWS, nx), 0)
 
@@ -176,8 +179,8 @@
     sources = {
         -2: lambda k: below(PLANE + k),
         -1: below,
-        0: lambda k: mine[0, k],
-        1: lambda k: mine[1, k],
+        0: lambda k: mine[1 - core, k],
+        1: lambda k: mine[core, k],
         2: above,
         3: lambda k: above(PLANE + k),
     }
@@ -270,17 +273,18 @@
                 residual[part, first + plane] = (v0 - p * v1 + q * v2).reshape(flat)
 
 
-def run(kernel, shapes, place, *arrays, scratch=(), scalars=1):
+def run(kernel, shapes, *arrays, scratch=(), scalars=1, aliases=None):
     vmem = pl.BlockSpec(memory_space=pltpu.VMEM)
     smem = pl.BlockSpec(memory_space=pltpu.SMEM)
     return pl.pallas_call(
         kernel,
         out_shape=shapes,
-        in_specs=[smem] * scalars + [vmem] * (len(arrays) + 1 - scalars),
+        in_specs=[smem] * scalars + [vmem] * (len(arrays) - scalars),
         out_specs=jax.tree.map(lambda _: vmem, shapes),
         scratch_shapes=list(scratch),
+        input_output_aliases=aliases or {},
         compiler_params=pltpu.CompilerParams(vmem_limit_bytes=VMEM_BYTES),
-    )(place, *arrays)
+    )(*arrays)
 
 
 def body(displacement, freq_index, tissue):
@@ -288,41 +292,34 @@
     chips = lax.axis_size("freq") // 2
     slabs = lax.axis_size("gz")
     low = core == 0
-    field = displacement[0]
-    ny, nx = field.shape[-2:]
+    ny, nx = displacement.shape[-2:]
     tile = (ROWS, nx)
-    kappa = 0.2 * (freq_index + 1).astype(jnp.float32)
     place = jnp.stack([core, (low & (lax.axis_index("gz") == 0)).astype(jnp.int32)])
 
     def shape(*dims):
         return jax.ShapeDtypeStruct(dims, jnp.float32)
 
-    first = jnp.concatenate([field[:, :, 0].reshape(6, ny, nx), tissue[0:1].astype(jnp.float32)])
-    last = jnp.concatenate([field[:, :, 3].reshape(6, ny, nx), tissue[3:4].astype(jnp.float32)])
-    same = to_slabs(jnp.where(low, last, first), 0, 0)
-    cross = to_slabs(jnp.where(low, first, last), 1, 1)
-    sent = jnp.where(low, field[:, :, 1:], field[:, :, :3]).reshape(18, ny, nx)
-    mid = swap_cores(jnp.concatenate([sent, jnp.broadcast_to(kappa[0], (1, ny, nx))]))
-
-    parts = run(
-        stencil_kernel,
-        shape(chips, 2 * PLANE, *tile),
-        place,
-        kappa,
-        field,
-        tissue,
-        same,
-        cross,
-        mid,
-        scratch=[pltpu.VMEM((18, ny, nx), jnp.float32)],
-        scalars=2,
+    other = swap_cores(displacement)[0]
+    other_index = swap_cores(freq_index)
+    field = displacement[0]
+
+    def plane(array, k):
+        return array[:, :, k].reshape(6, ny, nx)
+
+    first, last = (
+        jnp.concatenate([plane(field, k), plane(other, k), tissue[k : k + 1].astype(jnp.float32)]) for k in (0, 3)
     )
+    edge = to_slabs(jnp.where(low, first, last), 1, 1)
+
+    held = (place, freq_index, other_index, field, other, tissue)
+    scratch = [pltpu.VMEM((18, ny, nx), jnp.float32)]
+    message = shape(chips, 2 * PLANE, *tile)
+    parts = run(inner_kernel, message, *held, scratch=scratch, scalars=3)
+    parts = run(outer_kernel, message, *held, edge, parts, scratch=scratch, scalars=3, aliases={7: 0})
     mine = over_chips(parts).sum(axis=0).reshape(2, PLANE, *tile)
 
-    down = jnp.concatenate([mine[0], mine[1, :BEYOND]])
-    up = jnp.concatenate([mine[1], mine[0, :BEYOND]])
-    near = swap_cores(jnp.where(low, up, down))
-    far = to_slabs(jnp.where(low, down, up), 1, 1)
+    near = swap_cores(jnp.concatenate([mine[0], mine[1, :BEYOND]]))
+    far = to_slabs(jnp.concatenate([mine[1], mine[0, :BEYOND]]), 1, 1)
     tiles = run(vectors_kernel, shape(chips, 13, *tile), place, mine, near, far)
 
     gathered = over_chips(tiles)

time: 84.3 us -> 83.1 us (0.986)
  waiting for transfers between devices: 10.6 us -> 8.88 us
  Pallas kernels: 5.26 us -> 6.77 us
  blocking collectives: 54 us -> 52.9 us
  local copies, waits for them, and re-layouts: 0.13 us -> 1.2 us
    all_to_all x2, blocking collectives: 33.6 us -> 30.7 us  [over_chips(): lax.all_to_all(parts, 'freq', split_axis=0, concat_axis=0, tiled=True, ax...]
    ppermute x3 -> x2, waiting for transfers between devices: 8.98 us -> 6.28 us  [to_slabs(): return lax.ppermute(array, ('freq', 'gz'), pairs)]
    all_to_all x1, blocking collectives: 20.4 us -> 22.1 us  [body(): lax.all_to_all(jnp.broadcast_to(sums, (slabs, *tile)), 'gz', split_axis=0...]
    pallas_call x3 -> x4, Pallas kernels: 5.26 us -> 6.77 us  [run(): pl.pallas_call(kernel, out_shape=shapes, in_specs=[smem] * scalars + [vme...]
    select_n x3 -> x1, other arithmetic: 1.46 us -> 0.05 us  [body(): edge = to_slabs(jnp.where(low, first, last), 1, 1)]
    slice x2 -> x3, local copies, waits for them, and re-layouts: 0.04 us -> 1.17 us  [the longest x2 1.16 us: plane(): return array[:, :, k].reshape(6, ny, nx)]
    ppermute x3 -> x4, waiting for transfers between devices: 1.58 us -> 2.61 us  [swap_cores(): return lax.ppermute(array, 'freq', pairs)]
    ppermute x3 -> x2, starting transfers between devices: 7.38 us -> 7.15 us  [to_slabs(): return lax.ppermute(array, ('freq', 'gz'), pairs)]
  transfers between devices with their start and end apart: 6 -> 6, of which waited for: 4 -> 5; matrix products, arithmetic and copies ran while one was open for 0% -> 2% of each run, Pallas kernels for 0% -> 3%
where the time goes in v4:
time: 83.1 us; the launch traced here: 82.8 us
  blocking collectives  52.9 us (64%)
  starting transfers between devices  10.7 us (13%)
  waiting for transfers between devices  8.88 us (11%)
  Pallas kernels  6.77 us (8%)
  between operations  1.41 us (2%)
  local copies, waits for them, and re-layouts  1.2 us (1%)
  other arithmetic  1.01 us (1%)
    all_to_all x2, blocking collectives, over_chips(): lax.all_to_all(parts, 'freq', split_axis=0, concat_axis=0, tiled=True, ax...  30.7 us
    all_to_all x1, blocking collectives, body(): lax.all_to_all(jnp.broadcast_to(sums, (slabs, *tile)), 'gz', split_axis=0...  22.1 us
    ppermute x2, starting transfers between devices, to_slabs(): return lax.ppermute(array, ('freq', 'gz'), pairs)  7.15 us
    pallas_call x4, Pallas kernels, run(): pl.pallas_call(kernel, out_shape=shapes, in_specs=[smem] * scalars + [vme...  6.77 us
    ppermute x2, waiting for transfers between devices, to_slabs(): return lax.ppermute(array, ('freq', 'gz'), pairs)  6.28 us
    ppermute x4, starting transfers between devices, swap_cores(): return lax.ppermute(array, 'freq', pairs)  3.52 us
    ppermute x4, waiting for transfers between devices, swap_cores(): return lax.ppermute(array, 'freq', pairs)  2.61 us
  transfers between devices with their start and end apart: 6, of which 5 were waited for; matrix products, arithmetic and copies ran while one was open for 2% of the time, Pallas kernels for 3%

profile of v4, /device:TPU:1, one launch (start us, length us, event | category | flops | bytes accessed | tf_op | source)
XLA Modules:
  0.0 82.8 jit_solution(4626243742675777814)
XLA Ops:
  0.6 3.3 %collective-permute-start.1 = (f32[1,2,3,4,64,128]{5,4,3,2,1,0:T(8,128)}, f32[1,2,3,4,64,128]{5,4,3,2,1,0:T(8,128)S(1)}, u32[]{:S(2)}, u32[]{:S(2)}) collective-permute-start(f32[1,2,3,4,64,128]{5,4,3,2,1,0:T(8,128)} %param.3), channel_id=1, source_target_pairs={{0,16},{16,0},{32,48},{48,32},{64,80},{80,64},{96,112},{112,96},{1... | collective-permute-start | bytes 2359304 | tf_op jit(solution)/shard_map/ppermute | solution.py:29
  4.0 0.8 slice_convert_fusion
  4.7 0.0 copy-start
  4.7 0.0 copy-start.1
  4.7 1.1 %fusion.1 = (f32[2,3,1,64,128]{4,3,2,1,0:T(8,128)S(1)}, f32[2,3,1,64,128]{4,3,2,1,0:T(8,128)S(1)}) fusion(f32[2,3,4,64,128]{4,3,2,1,0:T(8,128)} %bitcast.13), kind=kLoop, calls=%fused_computation.10 | loop fusion | bytes 786432 | tf_op jit(solution)/shard_map/slice | solution.py:307
  5.9 0.2 collective-permute-done.1
  6.1 0.1 maximum_select_fusion
  6.2 2.1 %collective-permute-start.2 = (f32[13,64,128]{2,1,0:T(8,128)S(1)}, f32[13,64,128]{2,1,0:T(8,128)S(1)}, u32[]{:S(2)}, u32[]{:S(2)}) collective-permute-start(f32[13,64,128]{2,1,0:T(8,128)S(1)} %maximum_select_fusion), channel_id=1, source_target_pairs={{1,16},{2,17},{3,18},{4,19},{5,20},{6,21},{7,22},{8,23},{9,24},{10... | collective-permute-start | bytes 1277960 | tf_op jit(solution)/shard_map/ppermute | solution.py:40
  8.2 0.1 collective-permute-start
  9.0 0.1 pad_add_fusion.place
  9.1 0.6 collective-permute-done.other_index
  9.7 0.0 copy-done
  9.7 0.0 copy-done.1
  9.7 2.2 %shard_map.50._ = f32[8,40,8,128]{3,2,1,0:T(8,128)S(1)} custom-call(s32[2]{0:T(128)S(1)} %pad_add_fusion.place, s32[1]{0:T(128)S(6)} %copy.7.index, s32[1]{0:T(128)} %collective-permute-done.other_index, f32[2,3,4,64,128]{4,3,2,1,0:T(8,128)S(1)} %bitcast.14, f32[2,3,4,64,128]{4,3,2,1,0:T(8,128)S(1)} %bitcast.17, s32[4,64,128]{2,1,0:T(8,128)S(1)} %copy-done.1), custom_call_target="tpu_custom_call" | custom-call | tf_op jit(solution)/shard_map/pallas_call | solution.py:279
  11.9 3.7 %collective-permute-done.2.edge = f32[13,64,128]{2,1,0:T(8,128)S(1)} collective-permute-done((f32[13,64,128]{2,1,0:T(8,128)S(1)}, f32[13,64,128]{2,1,0:T(8,128)S(1)}, u32[]{:S(2)}, u32[]{:S(2)}) %collective-permute-start.2) | collective-permute-done | bytes 426016 | tf_op jit(solution)/shard_map/ppermute | solution.py:40
  15.6 2.2 %shard_map.51 = f32[8,40,8,128]{3,2,1,0:T(8,128)S(1)} custom-call(s32[2]{0:T(128)S(1)} %pad_add_fusion.place, s32[1]{0:T(128)S(6)} %copy.7.index, s32[1]{0:T(128)} %collective-permute-done.other_index, f32[2,3,4,64,128]{4,3,2,1,0:T(8,128)S(1)} %bitcast.15, f32[2,3,4,64,128]{4,3,2,1,0:T(8,128)S(1)} %bitcast.18, ...), custom_call_target="tpu_custom_call", output_to_operand_aliasing={{}: (7, {})} | custom-call | tf_op jit(solution)/shard_map/pallas_call | solution.py:279
  17.9 21.1 %all_to_all.15 = f32[8,40,8,128]{3,2,1,0:T(8,128)S(1)} all-to-all(f32[8,40,8,128]{3,2,1,0:T(8,128)S(1)} %shard_map.51), channel_id=1, replica_groups={{0,32,64,96,128,160,192,224},{16,48,80,112,144,176,208,240},{1,33,65,97..., dimensions={0} | all-to-all | bytes 2621440 | tf_op jit(solution)/shard_map/all_to_all | solution.py:46
  38.9 0.1 reduce_sum.18
  39.1 0.1 collective-permute-start.3
  39.2 5.1 %collective-permute-start.4 = (f32[31,8,128]{2,1,0:T(8,128)S(1)}, f32[31,8,128]{2,1,0:T(8,128)S(1)}, u32[]{:S(2)}, u32[]{:S(2)}) collective-permute-start(f32[31,8,128]{2,1,0:T(8,128)S(1)} %pad_maximum_fusion.1), channel_id=1, source_target_pairs={{1,16},{2,17},{3,18},{4,19},{5,20},{6,21},{7,22},{8,23},{9,24},{10... | collective-permute-start | bytes 380936 | tf_op jit(solution)/shard_map/ppermute | solution.py:40
  44.3 0.0 collective-permute-done.3.near
  44.3 2.6 %collective-permute-done.4.far = f32[31,8,128]{2,1,0:T(8,128)S(1)} collective-permute-done((f32[31,8,128]{2,1,0:T(8,128)S(1)}, f32[31,8,128]{2,1,0:T(8,128)S(1)}, u32[]{:S(2)}, u32[]{:S(2)}) %collective-permute-start.4) | collective-permute-done | bytes 127008 | tf_op jit(solution)/shard_map/ppermute | solution.py:40
  46.9 0.8 %shard_map.52 = f32[8,13,8,128]{3,2,1,0:T(8,128)S(1)} custom-call(s32[2]{0:T(128)S(1)} %pad_add_fusion.place, f32[2,20,8,128]{3,2,1,0:T(8,128)S(1)} %bitcast.20, f32[31,8,128]{2,1,0:T(8,128)S(1)} %collective-permute-done.3.near, f32[31,8,128]{2,1,0:T(8,128)S(1)} %collective-permute-done.4.far), custom_call_target="tpu_custom_call" | custom-call | tf_op jit(solution)/shard_map/pallas_call | solution.py:279
  47.7 9.6 %all_to_all.16.gathered = f32[8,13,8,128]{3,2,1,0:T(8,128)S(1)} all-to-all(f32[8,13,8,128]{3,2,1,0:T(8,128)S(1)} %shard_map.52), channel_id=1, replica_groups={{0,32,64,96,128,160,192,224},{16,48,80,112,144,176,208,240},{1,33,65,97..., dimensions={0} | all-to-all | bytes 851968 | tf_op jit(solution)/shard_map/all_to_all | solution.py:46
  57.3 0.0 collective-permute-start.5
  57.4 1.8 %collective-permute-done.5.others = f32[8,13,8,128]{3,2,1,0:T(8,128)S(1)} collective-permute-done((f32[8,13,8,128]{3,2,1,0:T(8,128)S(1)}, f32[8,13,8,128]{3,2,1,0:T(8,128)S(1)}, u32[]{:S(2)}, u32[]{:S(2)}) %collective-permute-start.5) | collective-permute-done | bytes 426016 | tf_op jit(solution)/shard_map/ppermute | solution.py:29
  59.1 22.1 %all_to_all.17.sums = f32[16,8,128]{2,1,0:T(8,128)S(1)} all-to-all(f32[16,8,128]{2,1,0:T(8,128)S(1)} %broadcast_in_dim.3), channel_id=1, replica_groups=mesh['freq'=16,'gz'=16] {'gz'}, dimensions={0} | all-to-all | bytes 131072 | tf_op jit(solution)/shard_map/all_to_all | solution.py:328
  81.3 1.5 %shard_map.53 = (f32[2,4,64,128]{3,2,1,0:T(8,128)}, f32[2,4,64,128]{3,2,1,0:T(8,128)}) custom-call(s32[2]{0:T(128)S(1)} %pad_add_fusion.place, f32[16,8,128]{2,1,0:T(8,128)S(1)} %all_to_all.17.sums, f32[8,13,8,128]{3,2,1,0:T(8,128)S(1)} %all_to_all.16.gathered, f32[8,13,8,128]{3,2,1,0:T(8,128)S(1)} %collective-permute-done.5.others), custom_call_target="tpu_custom_call" | custom-call | tf_op jit(solution)/shard_map/pallas_call | solution.py:279
  (7 shorter events, 0.1 us)
Async XLA Ops:
  0.6 5.5 %collective-permute-start.1 = (f32[1,2,3,4,64,128]{5,4,3,2,1,0:T(8,128)}, f32[1,2,3,4,64,128]{5,4,3,2,1,0:T(8,128)S(1)}, u32[]{:S(2)}, u32[]{:S(2)}) collective-permute-start(f32[1,2,3,4,64,128]{5,4,3,2,1,0:T(8,128)} %param.3), channel_id=1, source_target_pairs={{0,16},{16,0},{32,48},{48,32},{64,80},{80,64},{96,112},{112,96},{1... | collective-permute-start | bytes 2359304 | tf_op jit(solution)/shard_map/ppermute | solution.py:29
  4.7 5.0 %copy-start = (f32[1,2,3,4,64,128]{5,4,3,2,1,0:T(8,128)S(1)}, f32[1,2,3,4,64,128]{5,4,3,2,1,0:T(8,128)}, u32[]{:S(2)}) copy-start(f32[1,2,3,4,64,128]{5,4,3,2,1,0:T(8,128)} %param.3) | copy-start | bytes 2359300
  4.7 5.0 %copy-start.1 = (s32[4,64,128]{2,1,0:T(8,128)S(1)}, s32[4,64,128]{2,1,0:T(8,128)}, u32[]{:S(2)}) copy-start(s32[4,64,128]{2,1,0:T(8,128)} %tissue.3) | copy-start | bytes 393220
  6.2 9.4 %collective-permute-start.2 = (f32[13,64,128]{2,1,0:T(8,128)S(1)}, f32[13,64,128]{2,1,0:T(8,128)S(1)}, u32[]{:S(2)}, u32[]{:S(2)}) collective-permute-start(f32[13,64,128]{2,1,0:T(8,128)S(1)} %maximum_select_fusion), channel_id=1, source_target_pairs={{1,16},{2,17},{3,18},{4,19},{5,20},{6,21},{7,22},{8,23},{9,24},{10... | collective-permute-start | bytes 1277960 | tf_op jit(solution)/shard_map/ppermute | solution.py:40
  8.2 1.5 %collective-permute-start = (s32[1]{0:T(128)}, s32[1]{0:T(128)}, u32[]{:S(2)}, u32[]{:S(2)}) collective-permute-start(s32[1]{0:T(128)} %param.4), channel_id=1, source_target_pairs={{0,16},{16,0},{32,48},{48,32},{64,80},{80,64},{96,112},{112,96},{1... | collective-permute-start | bytes 20 | tf_op jit(solution)/shard_map/ppermute | solution.py:29
  39.1 5.2 %collective-permute-start.3 = (f32[31,8,128]{2,1,0:T(8,128)S(1)}, f32[31,8,128]{2,1,0:T(8,128)S(1)}, u32[]{:S(2)}, u32[]{:S(2)}) collective-permute-start(f32[31,8,128]{2,1,0:T(8,128)S(1)} %pad_maximum_fusion), channel_id=1, source_target_pairs={{0,16},{16,0},{32,48},{48,32},{64,80},{80,64},{96,112},{112,96},{1... | collective-permute-start | bytes 380936 | tf_op jit(solution)/shard_map/ppermute | solution.py:29
  39.2 7.7 %collective-permute-start.4 = (f32[31,8,128]{2,1,0:T(8,128)S(1)}, f32[31,8,128]{2,1,0:T(8,128)S(1)}, u32[]{:S(2)}, u32[]{:S(2)}) collective-permute-start(f32[31,8,128]{2,1,0:T(8,128)S(1)} %pad_maximum_fusion.1), channel_id=1, source_target_pairs={{1,16},{2,17},{3,18},{4,19},{5,20},{6,21},{7,22},{8,23},{9,24},{10... | collective-permute-start | bytes 380936 | tf_op jit(solution)/shard_map/ppermute | solution.py:40
  57.3 1.8 %collective-permute-start.5 = (f32[8,13,8,128]{3,2,1,0:T(8,128)S(1)}, f32[8,13,8,128]{3,2,1,0:T(8,128)S(1)}, u32[]{:S(2)}, u32[]{:S(2)}) collective-permute-start(f32[8,13,8,128]{3,2,1,0:T(8,128)S(1)} %all_to_all.16.gathered), channel_id=1, source_target_pairs={{0,16},{16,0},{32,48},{48,32},{64,80},{80,64},{96,112},{112,96},{1... | collective-permute-start | bytes 1277960 | tf_op jit(solution)/shard_map/ppermute | solution.py:29

commit v5 on v4

--- a/solution.py
+++ b/solution.py
@@ -59,91 +59,130 @@
     return jnp.where(rows_of(x.shape, dim) == 0, 0.0, pltpu.roll(x, 1, dim))
 
 
-def products(cell, kappas, here, above, out, first, acc):
-    shape = here.shape
-    ny, nx = shape
-    here_y, here_x = nxt(here, 0), nxt(here, 1)
-    for group in range(2):
-        scales = [m * kappas[group] for m in (here, above, here_y, here_x)]
-        for comp in range(3):
-            gz, gp, gy, gx, hy, hx, s, t = ([] for _ in range(8))
-            for part in range(2):
-                below, mine, up = cell(group, part, comp)
-                right_y, right_x = nxt(mine, 0), nxt(mine, 1)
-                gz.append(up - mine)
-                gp.append(mine - below)
-                gy.append(right_y - mine)
-                gx.append(right_x - mine)
-                hy.append(prv(gy[-1], 0))
-                hx.append(prv(gx[-1], 1))
-                s.append(gz[-1] + gy[-1] + gx[-1])
-                t.append([mine * scales[0], up * scales[1], right_y * scales[2], right_x * scales[3]])
-
-            def re(a, b):
-                return a[0] * b[0] + a[1] * b[1]
-
-            def im(a, b):
-                return a[0] * b[1] - a[1] * b[0]
-
-            new = [re(s, s), re(gz, gz), re(gy, gy), re(gx, gx)]
-            for a, b in ((s, gp), (s, hy), (s, hx), (gp, hy), (gp, hx), (hy, hx)):
-                new += [re(a, b), im(a, b)]
-            ts = [[t[0][k], t[1][k]] for k in range(4)]
-            for f in (re, im):
-                new.append(f(gz, ts[1]) + f(gy, ts[2]) + f(gx, ts[3]) - f(s, ts[0]))
-            for k, value in enumerate(new):
-                acc[k] = value if group == 0 and comp == 0 else acc[k] + value
-    done = {"d": here * acc[0] + above * acc[1] + here_y * acc[2] + here_x * acc[3]}
-    for k, name in enumerate(("z", "y", "x", "zy", "zx", "yx")):
-        signed = -here if k < 3 else here
-        done[name + "r"] = signed * acc[4 + 2 * k]
-        done[name + "i"] = signed * acc[5 + 2 * k]
-    done["rr"], done["ri"] = acc[16], acc[17]
-    row = rows_of(shape, 0)
-    lane = row % ROWS
-    for name, k in MAIN.items():
-        out[:, first + k] = done[name].reshape(ny // ROWS, ROWS, nx)
-    for k, parts in AROUND.items():
-        tile = jnp.zeros(shape, jnp.float32)
-        for name, start, before, after in parts:
-            moved = pltpu.roll(done[name], start + before, 0)
-            back = pltpu.roll(moved, ny - ROWS, 0)
-            moved = jnp.where(row < ROWS, 0.0, moved)
-            back = jnp.where(row >= ny - ROWS, 0.0, back)
-            tile = jnp.where((lane >= start) & (lane < start + before), moved, tile)
-            tile = jnp.where((lane >= start + before) & (lane < start + before + after), back, tile)
-        out[:, first + k] = tile.reshape(ny // ROWS, ROWS, nx)
+def products(cell, kappas, masks, out, first, rows):
+    nx = out.shape[-1]
+    ny = out.shape[0] * ROWS
+    tile = (ROWS, nx)
+    line, lane = rows_of(tile, 0), rows_of(tile, 1)
+    blank = jnp.zeros(tile, jnp.float32)
+
+    def at(read, j):
+        return read(pl.ds(ROWS * j, ROWS))
+
+    def next_y(read, j):
+        if ROWS * j + ROWS < ny:
+            return read(pl.ds(ROWS * j + 1, ROWS))
+        return jnp.where(line == ROWS - 1, 0.0, pltpu.roll(at(read, j), ROWS - 1, 0))
+
+    def prev_y(read, j):
+        if j:
+            return read(pl.ds(ROWS * j - 1, ROWS))
+        return pltpu.roll(at(read, j), 1, 0)
+
+    def re(a, b):
+        return a[0] * b[0] + a[1] * b[1]
+
+    def im(a, b):
+        return a[0] * b[1] - a[1] * b[0]
+
+    names = [name for name in NAMES if name]
+    for k in range(len(names)):
+        rows[k, :ROWS] = blank
+        rows[k, ROWS + ny :] = blank
+    for j in range(ny // ROWS):
+        here, above = (at(mask, j) for mask in masks)
+        here_y, here_x = next_y(masks[0], j), nxt(here, 1)
+        sums = None
+        for group in range(2):
+            scales = [m * kappas[group] for m in (here, above, here_y, here_x)]
+            for comp in range(3):
+                gz, gp, gy, gx, hy, hx, s, t = ([] for _ in range(8))
+                for part in range(2):
+                    below, mine, up = cell(group, part, comp)
+                    u, uz = at(mine, j), at(up, j)
+                    uy, ux = next_y(mine, j), nxt(u, 1)
+                    gz.append(uz - u)
+                    gp.append(u - at(below, j))
+                    gy.append(uy - u)
+                    gx.append(ux - u)
+                    step = u - prev_y(mine, j)
+                    hy.append(step if j else jnp.where(line == 0, 0.0, step))
+                    hx.append(jnp.where(lane == 0, 0.0, u - pltpu.roll(u, 1, 1)))
+                    s.append(gz[-1] + gy[-1] + gx[-1])
+                    t.append([u * scales[0], uz * scales[1], uy * scales[2], ux * scales[3]])
+                new = [re(s, s), re(gz, gz), re(gy, gy), re(gx, gx)]
+                for a, b in ((s, gp), (s, hy), (s, hx), (gp, hy), (gp, hx), (hy, hx)):
+                    new += [re(a, b), im(a, b)]
+                ts = [[t[0][k], t[1][k]] for k in range(4)]
+                for f in (re, im):
+                    new.append(f(gz, ts[1]) + f(gy, ts[2]) + f(gx, ts[3]) - f(s, ts[0]))
+                sums = new if sums is None else [old + value for old, value in zip(sums, new)]
+        done = {"d": here * sums[0] + above * sums[1] + here_y * sums[2] + here_x * sums[3]}
+        for k, name in enumerate(("z", "y", "x", "zy", "zx", "yx")):
+            signed = -here if k < 3 else here
+            done[name + "r"] = signed * sums[4 + 2 * k]
+            done[name + "i"] = signed * sums[5 + 2 * k]
+        done["rr"], done["ri"] = sums[16], sums[17]
+        for k, name in enumerate(names):
+            out[j, first + MAIN[name]] = done[name]
+            rows[k, ROWS + ROWS * j : 2 * ROWS + ROWS * j] = done[name]
+    for j in range(ny // ROWS):
+        for k, parts in AROUND.items():
+            packed = blank
+            for name, start, before, after in parts:
+                kept = names.index(name)
+                middle = start + before
+                head = rows[kept, pl.ds(ROWS + ROWS * j - middle, ROWS)]
+                tail = rows[kept, pl.ds(2 * ROWS + ROWS * j - middle, ROWS)]
+                packed = jnp.where((line >= start) & (line < middle), head, packed)
+                packed = jnp.where((line >= middle) & (line < middle + after), tail, packed)
+            out[j, first + k] = packed
 
 
 def kappa_of(index):
     return 0.2 * (index[0] + 1).astype(jnp.float32)
 
 
-def inner_kernel(place, index, other_index, field, other, tissue, out, acc):
+def inner_kernel(place, index, other_index, field, other, tissue, out, rows):
     core = place[0]
 
     def cell(group, part, comp):
         source = field if group == 0 else other
-        return [source[part, comp, core + k] for k in range(3)]
-
-    here, above = (tissue[core + k].astype(jnp.float32) for k in (1, 2))
-    products(cell, (kappa_of(index), kappa_of(other_index)), here, above, out, 0, acc)
-
-
-def outer_kernel(place, index, other_index, field, other, tissue, edge, _, out, acc):
+        return [lambda at, k=k: source[part, comp, core + k, at] for k in range(3)]
+
+    masks = [lambda at, k=k: tissue[core + k, at].astype(jnp.float32) for k in (1, 2)]
+    products(cell, (kappa_of(index), kappa_of(other_index)), masks, out, 0, rows)
+
+
+def outer_kernel(place, index, other_index, field, other, tissue, edge, inner, out, rows):
     core = place[0]
     low, floor = core == 0, place[1] == 1
+    out[:, :PLANE] = inner[...]
 
     def cell(group, part, comp):
         source = field if group == 0 else other
-        outside = edge[6 * (1 - group) + 3 * part + comp]
-        mine, inside = source[part, comp, 3 * core], source[part, comp, 1 + core]
-        below = jnp.where(low, jnp.where(floor, mine, outside), inside)
-        return below, mine, jnp.where(low, inside, outside)
-
-    here = tissue[3 * core].astype(jnp.float32)
-    above = jnp.where(low, tissue[1].astype(jnp.float32), edge[12])
-    products(cell, (kappa_of(index), kappa_of(other_index)), here, above, out, PLANE, acc)
+
+        def outside(at):
+            return edge[6 * (1 - group) + 3 * part + comp, at]
+
+        def mine(at):
+            return source[part, comp, 3 * core, at]
+
+        def inside(at):
+            return source[part, comp, 1 + core, at]
+
+        def below(at):
+            return jnp.where(low, jnp.where(floor, mine(at), outside(at)), inside(at))
+
+        return below, mine, lambda at: jnp.where(low, inside(at), outside(at))
+
+    def here(at):
+        return tissue[3 * core, at].astype(jnp.float32)
+
+    def above(at):
+        return jnp.where(low, tissue[1, at].astype(jnp.float32), edge[12, at])
+
+    products(cell, (kappa_of(index), kappa_of(other_index)), (here, above), out, PLANE, rows)
 
 
 def around_of(name):
@@ -273,7 +312,7 @@
                 residual[part, first + plane] = (v0 - p * v1 + q * v2).reshape(flat)
 
 
-def run(kernel, shapes, *arrays, scratch=(), scalars=1, aliases=None):
+def run(kernel, shapes, *arrays, scratch=(), scalars=1):
     vmem = pl.BlockSpec(memory_space=pltpu.VMEM)
     smem = pl.BlockSpec(memory_space=pltpu.SMEM)
     return pl.pallas_call(
@@ -282,7 +321,6 @@
         in_specs=[smem] * scalars + [vmem] * (len(arrays) - scalars),
         out_specs=jax.tree.map(lambda _: vmem, shapes),
         scratch_shapes=list(scratch),
-        input_output_aliases=aliases or {},
         compiler_params=pltpu.CompilerParams(vmem_limit_bytes=VMEM_BYTES),
     )(*arrays)
 
@@ -312,10 +350,9 @@
     edge = to_slabs(jnp.where(low, first, last), 1, 1)
 
     held = (place, freq_index, other_index, field, other, tissue)
-    scratch = [pltpu.VMEM((18, ny, nx), jnp.float32)]
-    message = shape(chips, 2 * PLANE, *tile)
-    parts = run(inner_kernel, message, *held, scratch=scratch, scalars=3)
-    parts = run(outer_kernel, message, *held, edge, parts, scratch=scratch, scalars=3, aliases={7: 0})
+    scratch = [pltpu.VMEM((15, ny + 2 * ROWS, nx), jnp.float32)]
+    inner = run(inner_kernel, shape(chips, PLANE, *tile), *held, scratch=scratch, scalars=3)
+    parts = run(outer_kernel, shape(chips, 2 * PLANE, *tile), *held, edge, inner, scratch=scratch, scalars=3)
     mine = over_chips(parts).sum(axis=0).reshape(2, PLANE, *tile)
 
     near = swap_cores(jnp.concatenate([mine[0], mine[1, :BEYOND]]))
@@ -324,7 +361,8 @@
 
     gathered = over_chips(tiles)
     others = swap_cores(gathered)
-    sums = (gathered[:, 12] + others[:, 12]).sum(axis=0)
+    sums = gathered[:, 12].sum(axis=0)
+    sums = sums + swap_cores(sums)
     sums = lax.all_to_all(jnp.broadcast_to(sums, (slabs, *tile)), "gz", split_axis=0, concat_axis=0, tiled=True)
     result = shape(2, 4, ny, nx)
     return tuple(run(outputs_kernel, (result, result), place, sums, gathered, others))

time: 83.1 us -> 83.2 us (level)
    ppermute x4 -> x5, waiting for transfers between devices: 2.61 us -> 1.94 us  [swap_cores(): return lax.ppermute(array, 'freq', pairs)]
    ppermute x4 -> x5, starting transfers between devices: 3.52 us -> 4.03 us  [swap_cores(): return lax.ppermute(array, 'freq', pairs)]
  transfers between devices with their start and end apart: 6 -> 7, of which waited for: 5 -> 5; matrix products, arithmetic and copies ran while one was open for 2% -> 2% of each run, Pallas kernels for 3% -> 3%
where the time goes in v5:
time: 83.2 us; the launch traced here: 82.8 us
  blocking collectives  52.4 us (63%)
  starting transfers between devices  11.3 us (14%)
  waiting for transfers between devices  8.68 us (10%)
  Pallas kernels  6.76 us (8%)
  between operations  1.41 us (2%)
  local copies, waits for them, and re-layouts  1.2 us (1%)
  other arithmetic  1.01 us (1%)
    all_to_all x2, blocking collectives, over_chips(): lax.all_to_all(parts, 'freq', split_axis=0, concat_axis=0, tiled=True, ax...  30.3 us
    all_to_all x1, blocking collectives, body(): lax.all_to_all(jnp.broadcast_to(sums, (slabs, *tile)), 'gz', split_axis=0...  22.1 us
    ppermute x2, starting transfers between devices, to_slabs(): return lax.ppermute(array, ('freq', 'gz'), pairs)  7.29 us
    pallas_call x4, Pallas kernels, run(): pl.pallas_call(kernel, out_shape=shapes, in_specs=[smem] * scalars + [vme...  6.76 us
    ppermute x2, waiting for transfers between devices, to_slabs(): return lax.ppermute(array, ('freq', 'gz'), pairs)  6.74 us
    ppermute x5, starting transfers between devices, swap_cores(): return lax.ppermute(array, 'freq', pairs)  4.03 us
    ppermute x5, waiting for transfers between devices, swap_cores(): return lax.ppermute(array, 'freq', pairs)  1.94 us
  transfers between devices with their start and end apart: 7, of which 5 were waited for; matrix products, arithmetic and copies ran while one was open for 2% of the time, Pallas kernels for 3%

profile of v5, /device:TPU:1, one launch (start us, length us, event | category | flops | bytes accessed | tf_op | source)
XLA Modules:
  0.0 82.8 jit_solution(118020299640393070)
XLA Ops:
  0.6 3.3 %collective-permute-start.1 = (f32[1,2,3,4,64,128]{5,4,3,2,1,0:T(8,128)}, f32[1,2,3,4,64,128]{5,4,3,2,1,0:T(8,128)S(1)}, u32[]{:S(2)}, u32[]{:S(2)}) collective-permute-start(f32[1,2,3,4,64,128]{5,4,3,2,1,0:T(8,128)} %param.3), channel_id=1, source_target_pairs={{0,16},{16,0},{32,48},{48,32},{64,80},{80,64},{96,112},{112,96},{1... | collective-permute-start | bytes 2359304 | tf_op jit(solution)/shard_map/ppermute | solution.py:29
  4.0 0.8 slice_convert_fusion
  4.7 0.0 copy-start
  4.7 0.0 copy-start.1
  4.7 1.1 %fusion = (f32[2,3,1,64,128]{4,3,2,1,0:T(8,128)S(1)}, f32[2,3,1,64,128]{4,3,2,1,0:T(8,128)S(1)}) fusion(f32[2,3,4,64,128]{4,3,2,1,0:T(8,128)} %bitcast.13), kind=kLoop, calls=%fused_computation.9 | loop fusion | bytes 786432 | tf_op jit(solution)/shard_map/slice | solution.py:345
  5.9 0.2 collective-permute-done.1
  6.1 0.1 maximum_select_fusion
  6.2 2.1 %collective-permute-start.2 = (f32[13,64,128]{2,1,0:T(8,128)S(1)}, f32[13,64,128]{2,1,0:T(8,128)S(1)}, u32[]{:S(2)}, u32[]{:S(2)}) collective-permute-start(f32[13,64,128]{2,1,0:T(8,128)S(1)} %maximum_select_fusion), channel_id=1, source_target_pairs={{1,16},{2,17},{3,18},{4,19},{5,20},{6,21},{7,22},{8,23},{9,24},{10... | collective-permute-start | bytes 1277960 | tf_op jit(solution)/shard_map/ppermute | solution.py:40
  8.2 0.1 collective-permute-start
  9.0 0.1 pad_add_fusion.place
  9.1 0.5 collective-permute-done.other_index
  9.6 0.0 copy-done
  9.6 0.0 copy-done.1
  9.6 2.2 %shard_map.50.inner = f32[8,20,8,128]{3,2,1,0:T(8,128)S(1)} custom-call(s32[2]{0:T(128)S(1)} %pad_add_fusion.place, s32[1]{0:T(128)S(6)} %copy.5.index, s32[1]{0:T(128)} %collective-permute-done.other_index, f32[2,3,4,64,128]{4,3,2,1,0:T(8,128)S(1)} %bitcast.14, f32[2,3,4,64,128]{4,3,2,1,0:T(8,128)S(1)} %bitcast.17, s32[4,64,128]{2,1,0:T(8,128)S(1)} %copy-done.1), custom_call_target="tpu_custom_call" | custom-call | tf_op jit(solution)/shard_map/pallas_call | solution.py:318
  11.8 3.9 %collective-permute-done.2.edge = f32[13,64,128]{2,1,0:T(8,128)S(1)} collective-permute-done((f32[13,64,128]{2,1,0:T(8,128)S(1)}, f32[13,64,128]{2,1,0:T(8,128)S(1)}, u32[]{:S(2)}, u32[]{:S(2)}) %collective-permute-start.2) | collective-permute-done | bytes 426016 | tf_op jit(solution)/shard_map/ppermute | solution.py:40
  15.6 2.2 %shard_map.51 = f32[8,40,8,128]{3,2,1,0:T(8,128)S(1)} custom-call(s32[2]{0:T(128)S(1)} %pad_add_fusion.place, s32[1]{0:T(128)S(6)} %copy.5.index, s32[1]{0:T(128)} %collective-permute-done.other_index, f32[2,3,4,64,128]{4,3,2,1,0:T(8,128)S(1)} %bitcast.15, f32[2,3,4,64,128]{4,3,2,1,0:T(8,128)S(1)} %bitcast.18, s32[4,64,128]{2,1,0:T(8,128)S(1)} %copy-done.1, ...), custom_call_target="tpu_custom_call" | custom-call | tf_op jit(solution)/shard_map/pallas_call | solution.py:318
  17.9 20.9 %all_to_all.15 = f32[8,40,8,128]{3,2,1,0:T(8,128)S(1)} all-to-all(f32[8,40,8,128]{3,2,1,0:T(8,128)S(1)} %shard_map.51), channel_id=1, replica_groups={{0,32,64,96,128,160,192,224},{16,48,80,112,144,176,208,240},{1,33,65,97..., dimensions={0} | all-to-all | bytes 2621440 | tf_op jit(solution)/shard_map/all_to_all | solution.py:46
  38.8 0.1 reduce_sum.18
  38.9 0.1 collective-permute-start.3
  39.0 5.2 %collective-permute-start.4 = (f32[31,8,128]{2,1,0:T(8,128)S(1)}, f32[31,8,128]{2,1,0:T(8,128)S(1)}, u32[]{:S(2)}, u32[]{:S(2)}) collective-permute-start(f32[31,8,128]{2,1,0:T(8,128)S(1)} %pad_maximum_fusion.1), channel_id=1, source_target_pairs={{1,16},{2,17},{3,18},{4,19},{5,20},{6,21},{7,22},{8,23},{9,24},{10... | collective-permute-start | bytes 380936 | tf_op jit(solution)/shard_map/ppermute | solution.py:40
  44.3 0.0 collective-permute-done.3.near
  44.3 2.9 %collective-permute-done.4.far = f32[31,8,128]{2,1,0:T(8,128)S(1)} collective-permute-done((f32[31,8,128]{2,1,0:T(8,128)S(1)}, f32[31,8,128]{2,1,0:T(8,128)S(1)}, u32[]{:S(2)}, u32[]{:S(2)}) %collective-permute-start.4) | collective-permute-done | bytes 127008 | tf_op jit(solution)/shard_map/ppermute | solution.py:40
  47.2 0.8 %shard_map.52 = f32[8,13,8,128]{3,2,1,0:T(8,128)S(1)} custom-call(s32[2]{0:T(128)S(1)} %pad_add_fusion.place, f32[2,20,8,128]{3,2,1,0:T(8,128)S(1)} %bitcast.20, f32[31,8,128]{2,1,0:T(8,128)S(1)} %collective-permute-done.3.near, f32[31,8,128]{2,1,0:T(8,128)S(1)} %collective-permute-done.4.far), custom_call_target="tpu_custom_call" | custom-call | tf_op jit(solution)/shard_map/pallas_call | solution.py:318
  48.0 9.4 %all_to_all.16.gathered = f32[8,13,8,128]{3,2,1,0:T(8,128)S(1)} all-to-all(f32[8,13,8,128]{3,2,1,0:T(8,128)S(1)} %shard_map.52), channel_id=1, replica_groups={{0,32,64,96,128,160,192,224},{16,48,80,112,144,176,208,240},{1,33,65,97..., dimensions={0} | all-to-all | bytes 851968 | tf_op jit(solution)/shard_map/all_to_all | solution.py:46
  57.4 0.0 collective-permute-start.6
  57.4 0.5 collective-permute-start.5
  57.9 1.3 %collective-permute-done.5 = f32[8,128]{1,0:T(8,128)S(1)} collective-permute-done((f32[8,128]{1,0:T(8,128)S(1)}, f32[8,128]{1,0:T(8,128)S(1)}, u32[]{:S(2)}, u32[]{:S(2)}) %collective-permute-start.5) | collective-permute-done | bytes 4128 | tf_op jit(solution)/shard_map/ppermute | solution.py:29
  59.2 22.1 %all_to_all.17.sums = f32[16,8,128]{2,1,0:T(8,128)S(1)} all-to-all(f32[16,8,128]{2,1,0:T(8,128)S(1)} %broadcast_in_dim.3), channel_id=1, replica_groups=mesh['freq'=16,'gz'=16] {'gz'}, dimensions={0} | all-to-all | bytes 131072 | tf_op jit(solution)/shard_map/all_to_all | solution.py:366
  81.3 0.0 collective-permute-done.6.others
  81.3 1.5 %shard_map.53 = (f32[2,4,64,128]{3,2,1,0:T(8,128)}, f32[2,4,64,128]{3,2,1,0:T(8,128)}) custom-call(s32[2]{0:T(128)S(1)} %pad_add_fusion.place, f32[16,8,128]{2,1,0:T(8,128)S(1)} %all_to_all.17.sums, f32[8,13,8,128]{3,2,1,0:T(8,128)S(1)} %all_to_all.16.gathered, f32[8,13,8,128]{3,2,1,0:T(8,128)S(1)} %collective-permute-done.6.others), custom_call_target="tpu_custom_call" | custom-call | tf_op jit(solution)/shard_map/pallas_call | solution.py:318
  (8 shorter events, 0.1 us)
Async XLA Ops:
  0.6 5.5 %collective-permute-start.1 = (f32[1,2,3,4,64,128]{5,4,3,2,1,0:T(8,128)}, f32[1,2,3,4,64,128]{5,4,3,2,1,0:T(8,128)S(1)}, u32[]{:S(2)}, u32[]{:S(2)}) collective-permute-start(f32[1,2,3,4,64,128]{5,4,3,2,1,0:T(8,128)} %param.3), channel_id=1, source_target_pairs={{0,16},{16,0},{32,48},{48,32},{64,80},{80,64},{96,112},{112,96},{1... | collective-permute-start | bytes 2359304 | tf_op jit(solution)/shard_map/ppermute | solution.py:29
  4.7 4.8 %copy-start = (f32[1,2,3,4,64,128]{5,4,3,2,1,0:T(8,128)S(1)}, f32[1,2,3,4,64,128]{5,4,3,2,1,0:T(8,128)}, u32[]{:S(2)}) copy-start(f32[1,2,3,4,64,128]{5,4,3,2,1,0:T(8,128)} %param.3) | copy-start | bytes 2359300
  4.7 4.8 %copy-start.1 = (s32[4,64,128]{2,1,0:T(8,128)S(1)}, s32[4,64,128]{2,1,0:T(8,128)}, u32[]{:S(2)}) copy-start(s32[4,64,128]{2,1,0:T(8,128)} %tissue.3) | copy-start | bytes 393220
  6.2 9.4 %collective-permute-start.2 = (f32[13,64,128]{2,1,0:T(8,128)S(1)}, f32[13,64,128]{2,1,0:T(8,128)S(1)}, u32[]{:S(2)}, u32[]{:S(2)}) collective-permute-start(f32[13,64,128]{2,1,0:T(8,128)S(1)} %maximum_select_fusion), channel_id=1, source_target_pairs={{1,16},{2,17},{3,18},{4,19},{5,20},{6,21},{7,22},{8,23},{9,24},{10... | collective-permute-start | bytes 1277960 | tf_op jit(solution)/shard_map/ppermute | solution.py:40
  8.2 1.3 %collective-permute-start = (s32[1]{0:T(128)}, s32[1]{0:T(128)}, u32[]{:S(2)}, u32[]{:S(2)}) collective-permute-start(s32[1]{0:T(128)} %param.4), channel_id=1, source_target_pairs={{0,16},{16,0},{32,48},{48,32},{64,80},{80,64},{96,112},{112,96},{1... | collective-permute-start | bytes 20 | tf_op jit(solution)/shard_map/ppermute | solution.py:29
  38.9 5.4 %collective-permute-start.3 = (f32[31,8,128]{2,1,0:T(8,128)S(1)}, f32[31,8,128]{2,1,0:T(8,128)S(1)}, u32[]{:S(2)}, u32[]{:S(2)}) collective-permute-start(f32[31,8,128]{2,1,0:T(8,128)S(1)} %pad_maximum_fusion), channel_id=1, source_target_pairs={{0,16},{16,0},{32,48},{48,32},{64,80},{80,64},{96,112},{112,96},{1... | collective-permute-start | bytes 380936 | tf_op jit(solution)/shard_map/ppermute | solution.py:29
  39.0 8.1 %collective-permute-start.4 = (f32[31,8,128]{2,1,0:T(8,128)S(1)}, f32[31,8,128]{2,1,0:T(8,128)S(1)}, u32[]{:S(2)}, u32[]{:S(2)}) collective-permute-start(f32[31,8,128]{2,1,0:T(8,128)S(1)} %pad_maximum_fusion.1), channel_id=1, source_target_pairs={{1,16},{2,17},{3,18},{4,19},{5,20},{6,21},{7,22},{8,23},{9,24},{10... | collective-permute-start | bytes 380936 | tf_op jit(solution)/shard_map/ppermute | solution.py:40
  57.4 23.9 %collective-permute-start.6 = (f32[8,13,8,128]{3,2,1,0:T(8,128)S(1)}, f32[8,13,8,128]{3,2,1,0:T(8,128)S(1)}, u32[]{:S(2)}, u32[]{:S(2)}) collective-permute-start(f32[8,13,8,128]{3,2,1,0:T(8,128)S(1)} %all_to_all.16.gathered), channel_id=1, source_target_pairs={{0,16},{16,0},{32,48},{48,32},{64,80},{80,64},{96,112},{112,96},{1... | collective-permute-start | bytes 1277960 | tf_op jit(solution)/shard_map/ppermute | solution.py:29
  57.4 1.8 %collective-permute-start.5 = (f32[8,128]{1,0:T(8,128)S(1)}, f32[8,128]{1,0:T(8,128)S(1)}, u32[]{:S(2)}, u32[]{:S(2)}) collective-permute-start(f32[8,128]{1,0:T(8,128)S(1)} %slice_reduce_fusion), channel_id=1, source_target_pairs={{0,16},{16,0},{32,48},{48,32},{64,80},{80,64},{96,112},{112,96},{1... | collective-permute-start | bytes 12296 | tf_op jit(solution)/shard_map/ppermute | solution.py:29

commit v6 on v5

--- a/solution.py
+++ b/solution.py
@@ -66,18 +66,18 @@
     line, lane = rows_of(tile, 0), rows_of(tile, 1)
     blank = jnp.zeros(tile, jnp.float32)
 
+    last = ny // ROWS - 1
+
     def at(read, j):
-        return read(pl.ds(ROWS * j, ROWS))
-
-    def next_y(read, j):
-        if ROWS * j + ROWS < ny:
-            return read(pl.ds(ROWS * j + 1, ROWS))
-        return jnp.where(line == ROWS - 1, 0.0, pltpu.roll(at(read, j), ROWS - 1, 0))
-
-    def prev_y(read, j):
-        if j:
-            return read(pl.ds(ROWS * j - 1, ROWS))
-        return pltpu.roll(at(read, j), 1, 0)
+        return read(pl.ds(pl.multiple_of(ROWS * j, ROWS), ROWS))
+
+    def next_y(read, j, own):
+        after = jnp.where(j == last, 0.0, at(read, jnp.minimum(j + 1, last)))
+        return pltpu.roll(jnp.where(line == 0, after, own), ROWS - 1, 0)
+
+    def prev_y(read, j, own):
+        before = at(read, jnp.maximum(j - 1, 0))
+        return pltpu.roll(jnp.where(line == ROWS - 1, before, own), 1, 0)
 
     def re(a, b):
         return a[0] * b[0] + a[1] * b[1]
@@ -89,9 +89,10 @@
     for k in range(len(names)):
         rows[k, :ROWS] = blank
         rows[k, ROWS + ny :] = blank
-    for j in range(ny // ROWS):
+    def chunk(j, _):
         here, above = (at(mask, j) for mask in masks)
-        here_y, here_x = next_y(masks[0], j), nxt(here, 1)
+        here_y, here_x = next_y(masks[0], j, here), nxt(here, 1)
+        bottom = (line == 0) & (j == 0)
         sums = None
         for group in range(2):
             scales = [m * kappas[group] for m in (here, above, here_y, here_x)]
@@ -100,13 +101,12 @@
                 for part in range(2):
                     below, mine, up = cell(group, part, comp)
                     u, uz = at(mine, j), at(up, j)
-                    uy, ux = next_y(mine, j), nxt(u, 1)
+                    uy, ux = next_y(mine, j, u), nxt(u, 1)
                     gz.append(uz - u)
                     gp.append(u - at(below, j))
                     gy.append(uy - u)
                     gx.append(ux - u)
-                    step = u - prev_y(mine, j)
-                    hy.append(step if j else jnp.where(line == 0, 0.0, step))
+                    hy.append(jnp.where(bottom, 0.0, u - prev_y(mine, j, u)))
                     hx.append(jnp.where(lane == 0, 0.0, u - pltpu.roll(u, 1, 1)))
                     s.append(gz[-1] + gy[-1] + gx[-1])
                     t.append([u * scales[0], uz * scales[1], uy * scales[2], ux * scales[3]])
@@ -125,18 +125,26 @@
         done["rr"], done["ri"] = sums[16], sums[17]
         for k, name in enumerate(names):
             out[j, first + MAIN[name]] = done[name]
-            rows[k, ROWS + ROWS * j : 2 * ROWS + ROWS * j] = done[name]
-    for j in range(ny // ROWS):
+            rows[k, pl.ds(pl.multiple_of(ROWS * j + ROWS, ROWS), ROWS)] = done[name]
+        return 0
+
+    lax.fori_loop(0, ny // ROWS, chunk, 0)
+
+    def surround(j, _):
+        def tile_of(name, k):
+            return rows[names.index(name), pl.ds(pl.multiple_of(ROWS * (j + k), ROWS), ROWS)]
+
         for k, parts in AROUND.items():
             packed = blank
             for name, start, before, after in parts:
-                kept = names.index(name)
                 middle = start + before
-                head = rows[kept, pl.ds(ROWS + ROWS * j - middle, ROWS)]
-                tail = rows[kept, pl.ds(2 * ROWS + ROWS * j - middle, ROWS)]
-                packed = jnp.where((line >= start) & (line < middle), head, packed)
-                packed = jnp.where((line >= middle) & (line < middle + after), tail, packed)
+                both = jnp.where(line < after, tile_of(name, 2), tile_of(name, 0))
+                both = pltpu.roll(both, middle % ROWS, 0) if middle % ROWS else both
+                packed = jnp.where((line >= start) & (line < middle + after), both, packed)
             out[j, first + k] = packed
+        return 0
+
+    lax.fori_loop(0, ny // ROWS, surround, 0)
 
 
 def kappa_of(index):
@@ -360,9 +368,9 @@
     tiles = run(vectors_kernel, shape(chips, 13, *tile), place, mine, near, far)
 
     gathered = over_chips(tiles)
+    sums = gathered[:, 12].sum(axis=0)
+    sums, gathered = lax.optimization_barrier((sums + swap_cores(sums), gathered))
     others = swap_cores(gathered)
-    sums = gathered[:, 12].sum(axis=0)
-    sums = sums + swap_cores(sums)
     sums = lax.all_to_all(jnp.broadcast_to(sums, (slabs, *tile)), "gz", split_axis=0, concat_axis=0, tiled=True)
     result = shape(2, 4, ny, nx)
     return tuple(run(outputs_kernel, (result, result), place, sums, gathered, others))

time: 83.2 us -> 83.2 us (level)
  no operation moved by 1% of the time
where the time goes in v6:
time: 83.2 us; the launch traced here: 82.8 us
  blocking collectives  53 us (64%)
  starting transfers between devices  10.9 us (13%)
  waiting for transfers between devices  8.03 us (10%)
  Pallas kernels  7.26 us (9%)
  between operations  1.41 us (2%)
  local copies, waits for them, and re-layouts  1.19 us (1%)
  other arithmetic  1.01 us (1%)
    all_to_all x2, blocking collectives, over_chips(): lax.all_to_all(parts, 'freq', split_axis=0, concat_axis=0, tiled=True, ax...  30.4 us
    all_to_all x1, blocking collectives, body(): lax.all_to_all(jnp.broadcast_to(sums, (slabs, *tile)), 'gz', split_axis=0...  22.6 us
    pallas_call x4, Pallas kernels, run(): pl.pallas_call(kernel, out_shape=shapes, in_specs=[smem] * scalars + [vme...  7.26 us
    ppermute x2, starting transfers between devices, to_slabs(): return lax.ppermute(array, ('freq', 'gz'), pairs)  7.21 us
    ppermute x2, waiting for transfers between devices, to_slabs(): return lax.ppermute(array, ('freq', 'gz'), pairs)  6.19 us
    ppermute x5, starting transfers between devices, swap_cores(): return lax.ppermute(array, 'freq', pairs)  3.69 us
    ppermute x5, waiting for transfers between devices, swap_cores(): return lax.ppermute(array, 'freq', pairs)  1.85 us
  transfers between devices with their start and end apart: 7, of which 5 were waited for; matrix products, arithmetic and copies ran while one was open for 2% of the time, Pallas kernels for 3%

profile of v6, /device:TPU:1, one launch (start us, length us, event | category | flops | bytes accessed | tf_op | source)
XLA Modules:
  0.0 82.8 jit_solution(16707493531447290190)
XLA Ops:
  0.6 3.3 %collective-permute-start.1 = (f32[1,2,3,4,64,128]{5,4,3,2,1,0:T(8,128)}, f32[1,2,3,4,64,128]{5,4,3,2,1,0:T(8,128)S(1)}, u32[]{:S(2)}, u32[]{:S(2)}) collective-permute-start(f32[1,2,3,4,64,128]{5,4,3,2,1,0:T(8,128)} %param.3), channel_id=1, source_target_pairs={{0,16},{16,0},{32,48},{48,32},{64,80},{80,64},{96,112},{112,96},{1... | collective-permute-start | bytes 2359304 | tf_op jit(solution)/shard_map/ppermute | solution.py:29
  4.0 0.8 slice_convert_fusion
  4.7 0.0 copy-start
  4.7 0.0 copy-start.1
  4.7 1.1 %fusion = (f32[2,3,1,64,128]{4,3,2,1,0:T(8,128)S(1)}, f32[2,3,1,64,128]{4,3,2,1,0:T(8,128)S(1)}) fusion(f32[2,3,4,64,128]{4,3,2,1,0:T(8,128)} %bitcast.13), kind=kLoop, calls=%fused_computation.9 | loop fusion | bytes 786432 | tf_op jit(solution)/shard_map/slice | solution.py:353
  5.9 0.2 collective-permute-done.1
  6.1 0.1 maximum_select_fusion
  6.2 2.1 %collective-permute-start.2 = (f32[13,64,128]{2,1,0:T(8,128)S(1)}, f32[13,64,128]{2,1,0:T(8,128)S(1)}, u32[]{:S(2)}, u32[]{:S(2)}) collective-permute-start(f32[13,64,128]{2,1,0:T(8,128)S(1)} %maximum_select_fusion), channel_id=1, source_target_pairs={{1,16},{2,17},{3,18},{4,19},{5,20},{6,21},{7,22},{8,23},{9,24},{10... | collective-permute-start | bytes 1277960 | tf_op jit(solution)/shard_map/ppermute | solution.py:40
  8.2 0.1 collective-permute-start
  9.0 0.1 pad_add_fusion.place
  9.1 0.5 collective-permute-done.other_index
  9.6 0.0 copy-done
  9.6 0.0 copy-done.1
  9.6 2.4 %shard_map.50.inner = f32[8,20,8,128]{3,2,1,0:T(8,128)S(1)} custom-call(s32[2]{0:T(128)S(1)} %pad_add_fusion.place, s32[1]{0:T(128)S(6)} %copy.5.index, s32[1]{0:T(128)} %collective-permute-done.other_index, f32[2,3,4,64,128]{4,3,2,1,0:T(8,128)S(1)} %bitcast.14, f32[2,3,4,64,128]{4,3,2,1,0:T(8,128)S(1)} %bitcast.17, s32[4,64,128]{2,1,0:T(8,128)S(1)} %copy-done.1), custom_call_target="tpu_custom_call" | custom-call | tf_op jit(solution)/shard_map/pallas_call | solution.py:326
  12.0 3.6 %collective-permute-done.2.edge = f32[13,64,128]{2,1,0:T(8,128)S(1)} collective-permute-done((f32[13,64,128]{2,1,0:T(8,128)S(1)}, f32[13,64,128]{2,1,0:T(8,128)S(1)}, u32[]{:S(2)}, u32[]{:S(2)}) %collective-permute-start.2) | collective-permute-done | bytes 426016 | tf_op jit(solution)/shard_map/ppermute | solution.py:40
  15.6 2.5 %shard_map.51 = f32[8,40,8,128]{3,2,1,0:T(8,128)S(1)} custom-call(s32[2]{0:T(128)S(1)} %pad_add_fusion.place, s32[1]{0:T(128)S(6)} %copy.5.index, s32[1]{0:T(128)} %collective-permute-done.other_index, f32[2,3,4,64,128]{4,3,2,1,0:T(8,128)S(1)} %bitcast.15, f32[2,3,4,64,128]{4,3,2,1,0:T(8,128)S(1)} %bitcast.18, s32[4,64,128]{2,1,0:T(8,128)S(1)} %copy-done.1, ...), custom_call_target="tpu_custom_call" | custom-call | tf_op jit(solution)/shard_map/pallas_call | solution.py:326
  18.1 21.0 %all_to_all.15 = f32[8,40,8,128]{3,2,1,0:T(8,128)S(1)} all-to-all(f32[8,40,8,128]{3,2,1,0:T(8,128)S(1)} %shard_map.51), channel_id=1, replica_groups={{0,32,64,96,128,160,192,224},{16,48,80,112,144,176,208,240},{1,33,65,97..., dimensions={0} | all-to-all | bytes 2621440 | tf_op jit(solution)/shard_map/all_to_all | solution.py:46
  39.1 0.1 reduce_sum.18
  39.2 0.1 collective-permute-start.3
  39.4 5.1 %collective-permute-start.4 = (f32[31,8,128]{2,1,0:T(8,128)S(1)}, f32[31,8,128]{2,1,0:T(8,128)S(1)}, u32[]{:S(2)}, u32[]{:S(2)}) collective-permute-start(f32[31,8,128]{2,1,0:T(8,128)S(1)} %pad_maximum_fusion.1), channel_id=1, source_target_pairs={{1,16},{2,17},{3,18},{4,19},{5,20},{6,21},{7,22},{8,23},{9,24},{10... | collective-permute-start | bytes 380936 | tf_op jit(solution)/shard_map/ppermute | solution.py:40
  44.5 0.0 collective-permute-done.3.near
  44.5 2.6 %collective-permute-done.4.far = f32[31,8,128]{2,1,0:T(8,128)S(1)} collective-permute-done((f32[31,8,128]{2,1,0:T(8,128)S(1)}, f32[31,8,128]{2,1,0:T(8,128)S(1)}, u32[]{:S(2)}, u32[]{:S(2)}) %collective-permute-start.4) | collective-permute-done | bytes 127008 | tf_op jit(solution)/shard_map/ppermute | solution.py:40
  47.1 0.8 %shard_map.52 = f32[8,13,8,128]{3,2,1,0:T(8,128)S(1)} custom-call(s32[2]{0:T(128)S(1)} %pad_add_fusion.place, f32[2,20,8,128]{3,2,1,0:T(8,128)S(1)} %bitcast.20, f32[31,8,128]{2,1,0:T(8,128)S(1)} %collective-permute-done.3.near, f32[31,8,128]{2,1,0:T(8,128)S(1)} %collective-permute-done.4.far), custom_call_target="tpu_custom_call" | custom-call | tf_op jit(solution)/shard_map/pallas_call | solution.py:326
  48.0 9.4 %all_to_all.16.gathered = f32[8,13,8,128]{3,2,1,0:T(8,128)S(1)} all-to-all(f32[8,13,8,128]{3,2,1,0:T(8,128)S(1)} %shard_map.52), channel_id=1, replica_groups={{0,32,64,96,128,160,192,224},{16,48,80,112,144,176,208,240},{1,33,65,97..., dimensions={0} | all-to-all | bytes 851968 | tf_op jit(solution)/shard_map/all_to_all | solution.py:46
  57.4 0.0 collective-permute-start.5
  57.4 1.2 %collective-permute-done.5 = f32[8,128]{1,0:T(8,128)S(1)} collective-permute-done((f32[8,128]{1,0:T(8,128)S(1)}, f32[8,128]{1,0:T(8,128)S(1)}, u32[]{:S(2)}, u32[]{:S(2)}) %collective-permute-start.5) | collective-permute-done | bytes 4128 | tf_op jit(solution)/shard_map/ppermute | solution.py:29
  58.5 0.2 collective-permute-start.6
  58.7 22.6 %all_to_all.17.sums = f32[16,8,128]{2,1,0:T(8,128)S(1)} all-to-all(f32[16,8,128]{2,1,0:T(8,128)S(1)} %broadcast_in_dim.3), channel_id=1, replica_groups=mesh['freq'=16,'gz'=16] {'gz'}, dimensions={0} | all-to-all | bytes 131072 | tf_op jit(solution)/shard_map/all_to_all | solution.py:374
  81.3 0.0 collective-permute-done.6.others
  81.3 1.5 %shard_map.53 = (f32[2,4,64,128]{3,2,1,0:T(8,128)}, f32[2,4,64,128]{3,2,1,0:T(8,128)}) custom-call(s32[2]{0:T(128)S(1)} %pad_add_fusion.place, f32[16,8,128]{2,1,0:T(8,128)S(1)} %all_to_all.17.sums, f32[8,13,8,128]{3,2,1,0:T(8,128)S(1)} %all_to_all.16.gathered, f32[8,13,8,128]{3,2,1,0:T(8,128)S(1)} %collective-permute-done.6.others), custom_call_target="tpu_custom_call" | custom-call | tf_op jit(solution)/shard_map/pallas_call | solution.py:326
  (8 shorter events, 0.1 us)
Async XLA Ops:
  0.6 5.5 %collective-permute-start.1 = (f32[1,2,3,4,64,128]{5,4,3,2,1,0:T(8,128)}, f32[1,2,3,4,64,128]{5,4,3,2,1,0:T(8,128)S(1)}, u32[]{:S(2)}, u32[]{:S(2)}) collective-permute-start(f32[1,2,3,4,64,128]{5,4,3,2,1,0:T(8,128)} %param.3), channel_id=1, source_target_pairs={{0,16},{16,0},{32,48},{48,32},{64,80},{80,64},{96,112},{112,96},{1... | collective-permute-start | bytes 2359304 | tf_op jit(solution)/shard_map/ppermute | solution.py:29
  4.7 4.8 %copy-start = (f32[1,2,3,4,64,128]{5,4,3,2,1,0:T(8,128)S(1)}, f32[1,2,3,4,64,128]{5,4,3,2,1,0:T(8,128)}, u32[]{:S(2)}) copy-start(f32[1,2,3,4,64,128]{5,4,3,2,1,0:T(8,128)} %param.3) | copy-start | bytes 2359300
  4.7 4.8 %copy-start.1 = (s32[4,64,128]{2,1,0:T(8,128)S(1)}, s32[4,64,128]{2,1,0:T(8,128)}, u32[]{:S(2)}) copy-start(s32[4,64,128]{2,1,0:T(8,128)} %tissue.3) | copy-start | bytes 393220
  6.2 9.4 %collective-permute-start.2 = (f32[13,64,128]{2,1,0:T(8,128)S(1)}, f32[13,64,128]{2,1,0:T(8,128)S(1)}, u32[]{:S(2)}, u32[]{:S(2)}) collective-permute-start(f32[13,64,128]{2,1,0:T(8,128)S(1)} %maximum_select_fusion), channel_id=1, source_target_pairs={{1,16},{2,17},{3,18},{4,19},{5,20},{6,21},{7,22},{8,23},{9,24},{10... | collective-permute-start | bytes 1277960 | tf_op jit(solution)/shard_map/ppermute | solution.py:40
  8.2 1.3 %collective-permute-start = (s32[1]{0:T(128)}, s32[1]{0:T(128)}, u32[]{:S(2)}, u32[]{:S(2)}) collective-permute-start(s32[1]{0:T(128)} %param.4), channel_id=1, source_target_pairs={{0,16},{16,0},{32,48},{48,32},{64,80},{80,64},{96,112},{112,96},{1... | collective-permute-start | bytes 20 | tf_op jit(solution)/shard_map/ppermute | solution.py:29
  39.2 5.3 %collective-permute-start.3 = (f32[31,8,128]{2,1,0:T(8,128)S(1)}, f32[31,8,128]{2,1,0:T(8,128)S(1)}, u32[]{:S(2)}, u32[]{:S(2)}) collective-permute-start(f32[31,8,128]{2,1,0:T(8,128)S(1)} %pad_maximum_fusion), channel_id=1, source_target_pairs={{0,16},{16,0},{32,48},{48,32},{64,80},{80,64},{96,112},{112,96},{1... | collective-permute-start | bytes 380936 | tf_op jit(solution)/shard_map/ppermute | solution.py:29
  39.4 7.7 %collective-permute-start.4 = (f32[31,8,128]{2,1,0:T(8,128)S(1)}, f32[31,8,128]{2,1,0:T(8,128)S(1)}, u32[]{:S(2)}, u32[]{:S(2)}) collective-permute-start(f32[31,8,128]{2,1,0:T(8,128)S(1)} %pad_maximum_fusion.1), channel_id=1, source_target_pairs={{1,16},{2,17},{3,18},{4,19},{5,20},{6,21},{7,22},{8,23},{9,24},{10... | collective-permute-start | bytes 380936 | tf_op jit(solution)/shard_map/ppermute | solution.py:40
  57.4 1.2 %collective-permute-start.5 = (f32[8,128]{1,0:T(8,128)S(1)}, f32[8,128]{1,0:T(8,128)S(1)}, u32[]{:S(2)}, u32[]{:S(2)}) collective-permute-start(f32[8,128]{1,0:T(8,128)S(1)} %slice_reduce_fusion), channel_id=1, source_target_pairs={{0,16},{16,0},{32,48},{48,32},{64,80},{80,64},{96,112},{112,96},{1... | collective-permute-start | bytes 12296 | tf_op jit(solution)/shard_map/ppermute | solution.py:29
  58.5 22.7 %collective-permute-start.6 = (f32[8,13,8,128]{3,2,1,0:T(8,128)S(1)}, f32[8,13,8,128]{3,2,1,0:T(8,128)S(1)}, u32[]{:S(2)}, u32[]{:S(2)}) collective-permute-start(f32[8,13,8,128]{3,2,1,0:T(8,128)S(1)} %all_to_all.16.gathered), channel_id=1, source_target_pairs={{0,16},{16,0},{32,48},{48,32},{64,80},{80,64},{96,112},{112,96},{1... | collective-permute-start | bytes 1277960 | tf_op jit(solution)/shard_map/ppermute | solution.py:29

commit v7 on v6

--- a/solution.py
+++ b/solution.py
@@ -41,8 +41,9 @@
 
 
 def over_chips(parts):
-    peers = lax.axis_size("freq")
-    groups = [list(range(core, peers, 2)) for core in range(2)]
+    chips = lax.axis_size("freq") // 2
+    ring = [*range(chips // 2), *reversed(range(chips // 2, chips))]
+    groups = [[2 * chip + core for chip in ring] for core in range(2)]
     return lax.all_to_all(parts, "freq", split_axis=0, concat_axis=0, tiled=True, axis_index_groups=groups)
 
 

time: 83.2 us -> 83.2 us (level)
  no operation moved by 1% of the time
where the time goes in v7:
time: 83.2 us; the launch traced here: 82.9 us
  blocking collectives  53 us (64%)
  starting transfers between devices  10.9 us (13%)
  waiting for transfers between devices  8.03 us (10%)
  Pallas kernels  7.26 us (9%)
  between operations  1.41 us (2%)
  local copies, waits for them, and re-layouts  1.19 us (1%)
  other arithmetic  1.01 us (1%)
    all_to_all x2, blocking collectives, over_chips(): lax.all_to_all(parts, 'freq', split_axis=0, concat_axis=0, tiled=True, ax...  30.5 us
    all_to_all x1, blocking collectives, body(): lax.all_to_all(jnp.broadcast_to(sums, (slabs, *tile)), 'gz', split_axis=0...  22.5 us
    pallas_call x4, Pallas kernels, run(): pl.pallas_call(kernel, out_shape=shapes, in_specs=[smem] * scalars + [vme...  7.26 us
    ppermute x2, starting transfers between devices, to_slabs(): return lax.ppermute(array, ('freq', 'gz'), pairs)  7.24 us
    ppermute x2, waiting for transfers between devices, to_slabs(): return lax.ppermute(array, ('freq', 'gz'), pairs)  6.19 us
    ppermute x5, starting transfers between devices, swap_cores(): return lax.ppermute(array, 'freq', pairs)  3.69 us
    ppermute x5, waiting for transfers between devices, swap_cores(): return lax.ppermute(array, 'freq', pairs)  1.85 us
  transfers between devices with their start and end apart: 7, of which 5 were waited for; matrix products, arithmetic and copies ran while one was open for 2% of the time, Pallas kernels for 3%

profile of v7, /device:TPU:1, one launch (start us, length us, event | category | flops | bytes accessed | tf_op | source)
XLA Modules:
  0.0 82.9 jit_solution(8495179102827821929)
XLA Ops:
  0.6 3.3 %collective-permute-start.1 = (f32[1,2,3,4,64,128]{5,4,3,2,1,0:T(8,128)}, f32[1,2,3,4,64,128]{5,4,3,2,1,0:T(8,128)S(1)}, u32[]{:S(2)}, u32[]{:S(2)}) collective-permute-start(f32[1,2,3,4,64,128]{5,4,3,2,1,0:T(8,128)} %param.3), channel_id=1, source_target_pairs={{0,16},{16,0},{32,48},{48,32},{64,80},{80,64},{96,112},{112,96},{1... | collective-permute-start | bytes 2359304 | tf_op jit(solution)/shard_map/ppermute | solution.py:29
  4.0 0.8 slice_convert_fusion
  4.7 0.0 copy-start
  4.7 0.0 copy-start.1
  4.7 1.1 %fusion = (f32[2,3,1,64,128]{4,3,2,1,0:T(8,128)S(1)}, f32[2,3,1,64,128]{4,3,2,1,0:T(8,128)S(1)}) fusion(f32[2,3,4,64,128]{4,3,2,1,0:T(8,128)} %bitcast.13), kind=kLoop, calls=%fused_computation.9 | loop fusion | bytes 786432 | tf_op jit(solution)/shard_map/slice | solution.py:354
  5.9 0.2 collective-permute-done.1
  6.1 0.1 maximum_select_fusion
  6.2 2.1 %collective-permute-start.2 = (f32[13,64,128]{2,1,0:T(8,128)S(1)}, f32[13,64,128]{2,1,0:T(8,128)S(1)}, u32[]{:S(2)}, u32[]{:S(2)}) collective-permute-start(f32[13,64,128]{2,1,0:T(8,128)S(1)} %maximum_select_fusion), channel_id=1, source_target_pairs={{1,16},{2,17},{3,18},{4,19},{5,20},{6,21},{7,22},{8,23},{9,24},{10... | collective-permute-start | bytes 1277960 | tf_op jit(solution)/shard_map/ppermute | solution.py:40
  8.2 0.1 collective-permute-start
  9.0 0.1 pad_add_fusion.place
  9.1 0.5 collective-permute-done.other_index
  9.6 0.0 copy-done
  9.6 0.0 copy-done.1
  9.6 2.4 %shard_map.50.inner = f32[8,20,8,128]{3,2,1,0:T(8,128)S(1)} custom-call(s32[2]{0:T(128)S(1)} %pad_add_fusion.place, s32[1]{0:T(128)S(6)} %copy.5.index, s32[1]{0:T(128)} %collective-permute-done.other_index, f32[2,3,4,64,128]{4,3,2,1,0:T(8,128)S(1)} %bitcast.14, f32[2,3,4,64,128]{4,3,2,1,0:T(8,128)S(1)} %bitcast.17, s32[4,64,128]{2,1,0:T(8,128)S(1)} %copy-done.1), custom_call_target="tpu_custom_call" | custom-call | tf_op jit(solution)/shard_map/pallas_call | solution.py:327
  12.0 3.6 %collective-permute-done.2.edge = f32[13,64,128]{2,1,0:T(8,128)S(1)} collective-permute-done((f32[13,64,128]{2,1,0:T(8,128)S(1)}, f32[13,64,128]{2,1,0:T(8,128)S(1)}, u32[]{:S(2)}, u32[]{:S(2)}) %collective-permute-start.2) | collective-permute-done | bytes 426016 | tf_op jit(solution)/shard_map/ppermute | solution.py:40
  15.6 2.5 %shard_map.51 = f32[8,40,8,128]{3,2,1,0:T(8,128)S(1)} custom-call(s32[2]{0:T(128)S(1)} %pad_add_fusion.place, s32[1]{0:T(128)S(6)} %copy.5.index, s32[1]{0:T(128)} %collective-permute-done.other_index, f32[2,3,4,64,128]{4,3,2,1,0:T(8,128)S(1)} %bitcast.15, f32[2,3,4,64,128]{4,3,2,1,0:T(8,128)S(1)} %bitcast.18, s32[4,64,128]{2,1,0:T(8,128)S(1)} %copy-done.1, ...), custom_call_target="tpu_custom_call" | custom-call | tf_op jit(solution)/shard_map/pallas_call | solution.py:327
  18.1 21.1 %all_to_all.15 = f32[8,40,8,128]{3,2,1,0:T(8,128)S(1)} all-to-all(f32[8,40,8,128]{3,2,1,0:T(8,128)S(1)} %shard_map.51), channel_id=1, replica_groups={{0,32,64,96,224,192,160,128},{16,48,80,112,240,208,176,144},{1,33,65,97..., dimensions={0} | all-to-all | bytes 2621440 | tf_op jit(solution)/shard_map/all_to_all | solution.py:47
  39.2 0.1 reduce_sum.18
  39.3 0.1 collective-permute-start.3
  39.4 5.2 %collective-permute-start.4 = (f32[31,8,128]{2,1,0:T(8,128)S(1)}, f32[31,8,128]{2,1,0:T(8,128)S(1)}, u32[]{:S(2)}, u32[]{:S(2)}) collective-permute-start(f32[31,8,128]{2,1,0:T(8,128)S(1)} %pad_maximum_fusion.1), channel_id=1, source_target_pairs={{1,16},{2,17},{3,18},{4,19},{5,20},{6,21},{7,22},{8,23},{9,24},{10... | collective-permute-start | bytes 380936 | tf_op jit(solution)/shard_map/ppermute | solution.py:40
  44.6 0.0 collective-permute-done.3.near
  44.6 2.6 %collective-permute-done.4.far = f32[31,8,128]{2,1,0:T(8,128)S(1)} collective-permute-done((f32[31,8,128]{2,1,0:T(8,128)S(1)}, f32[31,8,128]{2,1,0:T(8,128)S(1)}, u32[]{:S(2)}, u32[]{:S(2)}) %collective-permute-start.4) | collective-permute-done | bytes 127008 | tf_op jit(solution)/shard_map/ppermute | solution.py:40
  47.2 0.8 %shard_map.52 = f32[8,13,8,128]{3,2,1,0:T(8,128)S(1)} custom-call(s32[2]{0:T(128)S(1)} %pad_add_fusion.place, f32[2,20,8,128]{3,2,1,0:T(8,128)S(1)} %bitcast.20, f32[31,8,128]{2,1,0:T(8,128)S(1)} %collective-permute-done.3.near, f32[31,8,128]{2,1,0:T(8,128)S(1)} %collective-permute-done.4.far), custom_call_target="tpu_custom_call" | custom-call | tf_op jit(solution)/shard_map/pallas_call | solution.py:327
  48.0 9.4 %all_to_all.16.gathered = f32[8,13,8,128]{3,2,1,0:T(8,128)S(1)} all-to-all(f32[8,13,8,128]{3,2,1,0:T(8,128)S(1)} %shard_map.52), channel_id=1, replica_groups={{0,32,64,96,224,192,160,128},{16,48,80,112,240,208,176,144},{1,33,65,97..., dimensions={0} | all-to-all | bytes 851968 | tf_op jit(solution)/shard_map/all_to_all | solution.py:47
  57.4 0.0 collective-permute-start.5
  57.5 1.2 %collective-permute-done.5 = f32[8,128]{1,0:T(8,128)S(1)} collective-permute-done((f32[8,128]{1,0:T(8,128)S(1)}, f32[8,128]{1,0:T(8,128)S(1)}, u32[]{:S(2)}, u32[]{:S(2)}) %collective-permute-start.5) | collective-permute-done | bytes 4128 | tf_op jit(solution)/shard_map/ppermute | solution.py:29
  58.6 0.2 collective-permute-start.6
  58.8 22.5 %all_to_all.17.sums = f32[16,8,128]{2,1,0:T(8,128)S(1)} all-to-all(f32[16,8,128]{2,1,0:T(8,128)S(1)} %broadcast_in_dim.3), channel_id=1, replica_groups=mesh['freq'=16,'gz'=16] {'gz'}, dimensions={0} | all-to-all | bytes 131072 | tf_op jit(solution)/shard_map/all_to_all | solution.py:375
  81.3 0.0 collective-permute-done.6.others
  81.3 1.5 %shard_map.53 = (f32[2,4,64,128]{3,2,1,0:T(8,128)}, f32[2,4,64,128]{3,2,1,0:T(8,128)}) custom-call(s32[2]{0:T(128)S(1)} %pad_add_fusion.place, f32[16,8,128]{2,1,0:T(8,128)S(1)} %all_to_all.17.sums, f32[8,13,8,128]{3,2,1,0:T(8,128)S(1)} %all_to_all.16.gathered, f32[8,13,8,128]{3,2,1,0:T(8,128)S(1)} %collective-permute-done.6.others), custom_call_target="tpu_custom_call" | custom-call | tf_op jit(solution)/shard_map/pallas_call | solution.py:327
  (8 shorter events, 0.1 us)
Async XLA Ops:
  0.6 5.5 %collective-permute-start.1 = (f32[1,2,3,4,64,128]{5,4,3,2,1,0:T(8,128)}, f32[1,2,3,4,64,128]{5,4,3,2,1,0:T(8,128)S(1)}, u32[]{:S(2)}, u32[]{:S(2)}) collective-permute-start(f32[1,2,3,4,64,128]{5,4,3,2,1,0:T(8,128)} %param.3), channel_id=1, source_target_pairs={{0,16},{16,0},{32,48},{48,32},{64,80},{80,64},{96,112},{112,96},{1... | collective-permute-start | bytes 2359304 | tf_op jit(solution)/shard_map/ppermute | solution.py:29
  4.7 4.8 %copy-start = (f32[1,2,3,4,64,128]{5,4,3,2,1,0:T(8,128)S(1)}, f32[1,2,3,4,64,128]{5,4,3,2,1,0:T(8,128)}, u32[]{:S(2)}) copy-start(f32[1,2,3,4,64,128]{5,4,3,2,1,0:T(8,128)} %param.3) | copy-start | bytes 2359300
  4.7 4.8 %copy-start.1 = (s32[4,64,128]{2,1,0:T(8,128)S(1)}, s32[4,64,128]{2,1,0:T(8,128)}, u32[]{:S(2)}) copy-start(s32[4,64,128]{2,1,0:T(8,128)} %tissue.3) | copy-start | bytes 393220
  6.2 9.4 %collective-permute-start.2 = (f32[13,64,128]{2,1,0:T(8,128)S(1)}, f32[13,64,128]{2,1,0:T(8,128)S(1)}, u32[]{:S(2)}, u32[]{:S(2)}) collective-permute-start(f32[13,64,128]{2,1,0:T(8,128)S(1)} %maximum_select_fusion), channel_id=1, source_target_pairs={{1,16},{2,17},{3,18},{4,19},{5,20},{6,21},{7,22},{8,23},{9,24},{10... | collective-permute-start | bytes 1277960 | tf_op jit(solution)/shard_map/ppermute | solution.py:40
  8.2 1.3 %collective-permute-start = (s32[1]{0:T(128)}, s32[1]{0:T(128)}, u32[]{:S(2)}, u32[]{:S(2)}) collective-permute-start(s32[1]{0:T(128)} %param.4), channel_id=1, source_target_pairs={{0,16},{16,0},{32,48},{48,32},{64,80},{80,64},{96,112},{112,96},{1... | collective-permute-start | bytes 20 | tf_op jit(solution)/shard_map/ppermute | solution.py:29
  39.3 5.3 %collective-permute-start.3 = (f32[31,8,128]{2,1,0:T(8,128)S(1)}, f32[31,8,128]{2,1,0:T(8,128)S(1)}, u32[]{:S(2)}, u32[]{:S(2)}) collective-permute-start(f32[31,8,128]{2,1,0:T(8,128)S(1)} %pad_maximum_fusion), channel_id=1, source_target_pairs={{0,16},{16,0},{32,48},{48,32},{64,80},{80,64},{96,112},{112,96},{1... | collective-permute-start | bytes 380936 | tf_op jit(solution)/shard_map/ppermute | solution.py:29
  39.4 7.8 %collective-permute-start.4 = (f32[31,8,128]{2,1,0:T(8,128)S(1)}, f32[31,8,128]{2,1,0:T(8,128)S(1)}, u32[]{:S(2)}, u32[]{:S(2)}) collective-permute-start(f32[31,8,128]{2,1,0:T(8,128)S(1)} %pad_maximum_fusion.1), channel_id=1, source_target_pairs={{1,16},{2,17},{3,18},{4,19},{5,20},{6,21},{7,22},{8,23},{9,24},{10... | collective-permute-start | bytes 380936 | tf_op jit(solution)/shard_map/ppermute | solution.py:40
  57.4 1.2 %collective-permute-start.5 = (f32[8,128]{1,0:T(8,128)S(1)}, f32[8,128]{1,0:T(8,128)S(1)}, u32[]{:S(2)}, u32[]{:S(2)}) collective-permute-start(f32[8,128]{1,0:T(8,128)S(1)} %slice_reduce_fusion), channel_id=1, source_target_pairs={{0,16},{16,0},{32,48},{48,32},{64,80},{80,64},{96,112},{112,96},{1... | collective-permute-start | bytes 12296 | tf_op jit(solution)/shard_map/ppermute | solution.py:29
  58.6 22.7 %collective-permute-start.6 = (f32[8,13,8,128]{3,2,1,0:T(8,128)S(1)}, f32[8,13,8,128]{3,2,1,0:T(8,128)S(1)}, u32[]{:S(2)}, u32[]{:S(2)}) collective-permute-start(f32[8,13,8,128]{3,2,1,0:T(8,128)S(1)} %all_to_all.16.gathered), channel_id=1, source_target_pairs={{0,16},{16,0},{32,48},{48,32},{64,80},{80,64},{96,112},{112,96},{1... | collective-permute-start | bytes 1277960 | tf_op jit(solution)/shard_map/ppermute | solution.py:29

commit v8 on v5

--- a/solution.py
+++ b/solution.py
@@ -154,7 +154,7 @@
     products(cell, (kappa_of(index), kappa_of(other_index)), masks, out, 0, rows)
 
 
-def outer_kernel(place, index, other_index, field, other, tissue, edge, inner, out, rows):
+def outer_kernel(place, index, other_index, field, other, tissue, same, cross, inner, out, rows):
     core = place[0]
     low, floor = core == 0, place[1] == 1
     out[:, :PLANE] = inner[...]
@@ -163,7 +163,7 @@
         source = field if group == 0 else other
 
         def outside(at):
-            return edge[6 * (1 - group) + 3 * part + comp, at]
+            return (same, cross)[group][3 * part + comp, at]
 
         def mine(at):
             return source[part, comp, 3 * core, at]
@@ -180,7 +180,7 @@
         return tissue[3 * core, at].astype(jnp.float32)
 
     def above(at):
-        return jnp.where(low, tissue[1, at].astype(jnp.float32), edge[12, at])
+        return jnp.where(low, tissue[1, at].astype(jnp.float32), cross[6, at])
 
     products(cell, (kappa_of(index), kappa_of(other_index)), (here, above), out, PLANE, rows)
 
@@ -337,22 +337,17 @@
     def shape(*dims):
         return jax.ShapeDtypeStruct(dims, jnp.float32)
 
+    field = displacement[0]
+    first, last = (field[:, :, k].reshape(6, ny, nx) for k in (0, 3))
+    same = to_slabs(jnp.where(low, last, first), 0, 0)
+    cross = to_slabs(jnp.concatenate([jnp.where(low, first, last), tissue[:1].astype(jnp.float32)]), 1, 1)
     other = swap_cores(displacement)[0]
     other_index = swap_cores(freq_index)
-    field = displacement[0]
-
-    def plane(array, k):
-        return array[:, :, k].reshape(6, ny, nx)
-
-    first, last = (
-        jnp.concatenate([plane(field, k), plane(other, k), tissue[k : k + 1].astype(jnp.float32)]) for k in (0, 3)
-    )
-    edge = to_slabs(jnp.where(low, first, last), 1, 1)
 
     held = (place, freq_index, other_index, field, other, tissue)
     scratch = [pltpu.VMEM((15, ny + 2 * ROWS, nx), jnp.float32)]
     inner = run(inner_kernel, shape(chips, PLANE, *tile), *held, scratch=scratch, scalars=3)
-    parts = run(outer_kernel, shape(chips, 2 * PLANE, *tile), *held, edge, inner, scratch=scratch, scalars=3)
+    parts = run(outer_kernel, shape(chips, 2 * PLANE, *tile), *held, same, cross, inner, scratch=scratch, scalars=3)
     mine = over_chips(parts).sum(axis=0).reshape(2, PLANE, *tile)
 
     near = swap_cores(jnp.concatenate([mine[0], mine[1, :BEYOND]]))
@@ -360,9 +355,9 @@
     tiles = run(vectors_kernel, shape(chips, 13, *tile), place, mine, near, far)
 
     gathered = over_chips(tiles)
+    sums = gathered[:, 12].sum(axis=0)
+    sums, gathered = lax.optimization_barrier((sums + swap_cores(sums), gathered))
     others = swap_cores(gathered)
-    sums = gathered[:, 12].sum(axis=0)
-    sums = sums + swap_cores(sums)
     sums = lax.all_to_all(jnp.broadcast_to(sums, (slabs, *tile)), "gz", split_axis=0, concat_axis=0, tiled=True)
     result = shape(2, 4, ny, nx)
     return tuple(run(outputs_kernel, (result, result), place, sums, gathered, others))

time: 83.2 us -> 82.8 us (level)
  waiting for transfers between devices: 8.68 us -> 4.64 us
  starting transfers between devices: 11.3 us -> 13.8 us
  blocking collectives: 52.4 us -> 54 us
  local copies, waits for them, and re-layouts: 1.2 us -> 0.04 us
  other arithmetic: 1.01 us -> 2.01 us
    ppermute x2 -> x3, waiting for transfers between devices: 6.74 us -> 3.12 us  [to_slabs(): return lax.ppermute(array, ('freq', 'gz'), pairs)]
    ppermute x5, starting transfers between devices: 4.03 us -> 7.22 us  [swap_cores(): return lax.ppermute(array, 'freq', pairs)]
    all_to_all x2, blocking collectives: 30.3 us -> 31.8 us  [over_chips(): lax.all_to_all(parts, 'freq', split_axis=0, concat_axis=0, tiled=True, ax...]
    slice x2 -> x0, local copies, waits for them, and re-layouts: 1.16 us -> none  [plane(): return array[:, :, k].reshape(6, ny, nx)]
    select_n x1, other arithmetic: 0.05 us -> 1.05 us  [body(): jnp.where(low, first, last)]
    ppermute x2 -> x3, starting transfers between devices: 7.29 us -> 6.54 us  [to_slabs(): return lax.ppermute(array, ('freq', 'gz'), pairs)]
  transfers between devices with their start and end apart: 7 -> 8, of which waited for: 5 -> 4; matrix products, arithmetic and copies ran while one was open for 2% -> 2% of each run, Pallas kernels for 3% -> 2%
where the time goes in v8:
time: 82.8 us; the launch traced here: 82.4 us
  blocking collectives  54 us (65%)
  starting transfers between devices  13.8 us (17%)
  Pallas kernels  6.52 us (8%)
  waiting for transfers between devices  4.64 us (6%)
  other arithmetic  2.01 us (2%)
  between operations  1.41 us (2%)
    all_to_all x2, blocking collectives, over_chips(): lax.all_to_all(parts, 'freq', split_axis=0, concat_axis=0, tiled=True, ax...  31.8 us
    all_to_all x1, blocking collectives, body(): lax.all_to_all(jnp.broadcast_to(sums, (slabs, *tile)), 'gz', split_axis=0...  22.2 us
    ppermute x5, starting transfers between devices, swap_cores(): return lax.ppermute(array, 'freq', pairs)  7.22 us
    ppermute x3, starting transfers between devices, to_slabs(): return lax.ppermute(array, ('freq', 'gz'), pairs)  6.54 us
    pallas_call x4, Pallas kernels, run(): pl.pallas_call(kernel, out_shape=shapes, in_specs=[smem] * scalars + [vme...  6.52 us
    ppermute x3, waiting for transfers between devices, to_slabs(): return lax.ppermute(array, ('freq', 'gz'), pairs)  3.12 us
  transfers between devices with their start and end apart: 8, of which 4 were waited for; matrix products, arithmetic and copies ran while one was open for 2% of the time, Pallas kernels for 2%

profile of v8, /device:TPU:1, one launch (start us, length us, event | category | flops | bytes accessed | tf_op | source)
XLA Modules:
  0.0 82.4 jit_solution(7999688449820584465)
XLA Ops:
  0.6 0.0 copy-start
  0.6 0.0 copy-start.1
  0.7 3.3 %collective-permute-start.1 = (f32[1,2,3,4,64,128]{5,4,3,2,1,0:T(8,128)}, f32[1,2,3,4,64,128]{5,4,3,2,1,0:T(8,128)S(1)}, u32[]{:S(2)}, u32[]{:S(2)}) collective-permute-start(f32[1,2,3,4,64,128]{5,4,3,2,1,0:T(8,128)} %param.3), channel_id=1, source_target_pairs={{0,16},{16,0},{32,48},{48,32},{64,80},{80,64},{96,112},{112,96},{1... | collective-permute-start | bytes 2359304 | tf_op jit(solution)/shard_map/ppermute | solution.py:29
  4.0 0.8 slice_convert_fusion
  4.7 1.1 %slice_select_fusion = (f32[2,3,1,64,128]{4,3,2,1,0:T(8,128)S(1)}, f32[2,3,1,64,128]{4,3,2,1,0:T(8,128)S(1)}) fusion(f32[2,3,4,64,128]{4,3,2,1,0:T(8,128)} %bitcast.11, pred[]{:T(512)S(6)} %eq.8), kind=kLoop, calls=%fused_computation.1 | loop fusion | flops 98304 | bytes 786433 | tf_op jit(solution)/shard_map/jit(_where)/select_n | solution.py:343
  5.8 1.9 %collective-permute-start.3 = (f32[7,64,128]{2,1,0:T(8,128)S(1)}, f32[7,64,128]{2,1,0:T(8,128)S(1)}, u32[]{:S(2)}, u32[]{:S(2)}) collective-permute-start(f32[7,64,128]{2,1,0:T(8,128)S(1)} %pad_maximum_fusion), channel_id=1, source_target_pairs={{1,16},{2,17},{3,18},{4,19},{5,20},{6,21},{7,22},{8,23},{9,24},{10... | collective-permute-start | bytes 688136 | tf_op jit(solution)/shard_map/ppermute | solution.py:40
  7.8 1.3 %collective-permute-start.2 = (f32[6,64,128]{2,1,0:T(8,128)S(1)}, f32[6,64,128]{2,1,0:T(8,128)S(1)}, u32[]{:S(2)}, u32[]{:S(2)}) collective-permute-start(f32[6,64,128]{2,1,0:T(8,128)S(1)} %bitcast.19), channel_id=1, source_target_pairs={{0,1},{1,2},{2,3},{3,4},{4,5},{5,6},{6,7},{7,8},{8,9},{9,10},{10,1... | collective-permute-start | bytes 589832 | tf_op jit(solution)/shard_map/ppermute | solution.py:40
  9.1 2.8 %collective-permute-start = (s32[1]{0:T(128)}, s32[1]{0:T(128)}, u32[]{:S(2)}, u32[]{:S(2)}) collective-permute-start(s32[1]{0:T(128)} %param.4), channel_id=1, source_target_pairs={{0,16},{16,0},{32,48},{48,32},{64,80},{80,64},{96,112},{112,96},{1... | collective-permute-start | bytes 20 | tf_op jit(solution)/shard_map/ppermute | solution.py:29
  12.6 0.1 pad_add_fusion.place
  12.6 0.4 collective-permute-done.other_index
  13.0 0.0 collective-permute-done.1
  13.0 0.0 copy-done
  13.0 0.0 copy-done.1
  13.0 2.0 %shard_map.50.inner = f32[8,20,8,128]{3,2,1,0:T(8,128)S(1)} custom-call(s32[2]{0:T(128)S(1)} %pad_add_fusion.place, s32[1]{0:T(128)S(6)} %copy.5.index, s32[1]{0:T(128)} %collective-permute-done.other_index, f32[2,3,4,64,128]{4,3,2,1,0:T(8,128)S(1)} %bitcast.12, f32[2,3,4,64,128]{4,3,2,1,0:T(8,128)S(1)} %bitcast.14, s32[4,64,128]{2,1,0:T(8,128)S(1)} %copy-done.1), custom_call_target="tpu_custom_call" | custom-call | tf_op jit(solution)/shard_map/pallas_call | solution.py:318
  15.0 0.2 collective-permute-done.2.same
  15.3 0.0 collective-permute-done.3.cross
  15.3 2.1 %shard_map.51 = f32[8,40,8,128]{3,2,1,0:T(8,128)S(1)} custom-call(s32[2]{0:T(128)S(1)} %pad_add_fusion.place, s32[1]{0:T(128)S(6)} %copy.5.index, s32[1]{0:T(128)} %collective-permute-done.other_index, f32[2,3,4,64,128]{4,3,2,1,0:T(8,128)S(1)} %bitcast.13, f32[2,3,4,64,128]{4,3,2,1,0:T(8,128)S(1)} %bitcast.15, s32[4,64,128]{2,1,0:T(8,128)S(1)} %copy-done.1, ...), custom_call_target="tpu_custom_call" | custom-call | tf_op jit(solution)/shard_map/pallas_call | solution.py:318
  17.4 22.3 %all_to_all.15 = f32[8,40,8,128]{3,2,1,0:T(8,128)S(1)} all-to-all(f32[8,40,8,128]{3,2,1,0:T(8,128)S(1)} %shard_map.51), channel_id=1, replica_groups={{0,32,64,96,128,160,192,224},{16,48,80,112,144,176,208,240},{1,33,65,97..., dimensions={0} | all-to-all | bytes 2621440 | tf_op jit(solution)/shard_map/all_to_all | solution.py:46
  39.7 0.1 reduce_sum.18
  39.8 0.9 %collective-permute-start.4 = (f32[31,8,128]{2,1,0:T(8,128)S(1)}, f32[31,8,128]{2,1,0:T(8,128)S(1)}, u32[]{:S(2)}, u32[]{:S(2)}) collective-permute-start(f32[31,8,128]{2,1,0:T(8,128)S(1)} %pad_maximum_fusion.1), channel_id=1, source_target_pairs={{0,16},{16,0},{32,48},{48,32},{64,80},{80,64},{96,112},{112,96},{1... | collective-permute-start | bytes 380936 | tf_op jit(solution)/shard_map/ppermute | solution.py:29
  40.7 3.3 %collective-permute-start.5 = (f32[31,8,128]{2,1,0:T(8,128)S(1)}, f32[31,8,128]{2,1,0:T(8,128)S(1)}, u32[]{:S(2)}, u32[]{:S(2)}) collective-permute-start(f32[31,8,128]{2,1,0:T(8,128)S(1)} %pad_maximum_fusion.2), channel_id=1, source_target_pairs={{1,16},{2,17},{3,18},{4,19},{5,20},{6,21},{7,22},{8,23},{9,24},{10... | collective-permute-start | bytes 380936 | tf_op jit(solution)/shard_map/ppermute | solution.py:40
  44.1 0.0 collective-permute-done.4.near
  44.1 2.9 %collective-permute-done.5.far = f32[31,8,128]{2,1,0:T(8,128)S(1)} collective-permute-done((f32[31,8,128]{2,1,0:T(8,128)S(1)}, f32[31,8,128]{2,1,0:T(8,128)S(1)}, u32[]{:S(2)}, u32[]{:S(2)}) %collective-permute-start.5) | collective-permute-done | bytes 127008 | tf_op jit(solution)/shard_map/ppermute | solution.py:40
  47.0 0.8 %shard_map.52 = f32[8,13,8,128]{3,2,1,0:T(8,128)S(1)} custom-call(s32[2]{0:T(128)S(1)} %pad_add_fusion.place, f32[2,20,8,128]{3,2,1,0:T(8,128)S(1)} %bitcast.17, f32[31,8,128]{2,1,0:T(8,128)S(1)} %collective-permute-done.4.near, f32[31,8,128]{2,1,0:T(8,128)S(1)} %collective-permute-done.5.far), custom_call_target="tpu_custom_call" | custom-call | tf_op jit(solution)/shard_map/pallas_call | solution.py:318
  47.8 9.5 %all_to_all.16.gathered = f32[8,13,8,128]{3,2,1,0:T(8,128)S(1)} all-to-all(f32[8,13,8,128]{3,2,1,0:T(8,128)S(1)} %shard_map.52), channel_id=1, replica_groups={{0,32,64,96,128,160,192,224},{16,48,80,112,144,176,208,240},{1,33,65,97..., dimensions={0} | all-to-all | bytes 851968 | tf_op jit(solution)/shard_map/all_to_all | solution.py:46
  57.3 0.0 collective-permute-start.6
  57.3 1.2 %collective-permute-done.6 = f32[8,128]{1,0:T(8,128)S(1)} collective-permute-done((f32[8,128]{1,0:T(8,128)S(1)}, f32[8,128]{1,0:T(8,128)S(1)}, u32[]{:S(2)}, u32[]{:S(2)}) %collective-permute-start.6) | collective-permute-done | bytes 4128 | tf_op jit(solution)/shard_map/ppermute | solution.py:29
  58.5 0.2 collective-permute-start.7
  58.7 22.2 %all_to_all.17.sums = f32[16,8,128]{2,1,0:T(8,128)S(1)} all-to-all(f32[16,8,128]{2,1,0:T(8,128)S(1)} %broadcast_in_dim.3), channel_id=1, replica_groups=mesh['freq'=16,'gz'=16] {'gz'}, dimensions={0} | all-to-all | bytes 131072 | tf_op jit(solution)/shard_map/all_to_all | solution.py:361
  80.9 0.0 collective-permute-done.7.others
  80.9 1.5 %shard_map.53 = (f32[2,4,64,128]{3,2,1,0:T(8,128)}, f32[2,4,64,128]{3,2,1,0:T(8,128)}) custom-call(s32[2]{0:T(128)S(1)} %pad_add_fusion.place, f32[16,8,128]{2,1,0:T(8,128)S(1)} %all_to_all.17.sums, f32[8,13,8,128]{3,2,1,0:T(8,128)S(1)} %all_to_all.16.gathered, f32[8,13,8,128]{3,2,1,0:T(8,128)S(1)} %collective-permute-done.7.others), custom_call_target="tpu_custom_call" | custom-call | tf_op jit(solution)/shard_map/pallas_call | solution.py:318
  (8 shorter events, 0.1 us)
Async XLA Ops:
  0.6 12.4 %copy-start = (f32[1,2,3,4,64,128]{5,4,3,2,1,0:T(8,128)S(1)}, f32[1,2,3,4,64,128]{5,4,3,2,1,0:T(8,128)}, u32[]{:S(2)}) copy-start(f32[1,2,3,4,64,128]{5,4,3,2,1,0:T(8,128)} %param.3) | copy-start | bytes 2359300
  0.6 12.3 %copy-start.1 = (s32[4,64,128]{2,1,0:T(8,128)S(1)}, s32[4,64,128]{2,1,0:T(8,128)}, u32[]{:S(2)}) copy-start(s32[4,64,128]{2,1,0:T(8,128)} %tissue.3) | copy-start | bytes 393220
  0.7 12.3 %collective-permute-start.1 = (f32[1,2,3,4,64,128]{5,4,3,2,1,0:T(8,128)}, f32[1,2,3,4,64,128]{5,4,3,2,1,0:T(8,128)S(1)}, u32[]{:S(2)}, u32[]{:S(2)}) collective-permute-start(f32[1,2,3,4,64,128]{5,4,3,2,1,0:T(8,128)} %param.3), channel_id=1, source_target_pairs={{0,16},{16,0},{32,48},{48,32},{64,80},{80,64},{96,112},{112,96},{1... | collective-permute-start | bytes 2359304 | tf_op jit(solution)/shard_map/ppermute | solution.py:29
  5.8 9.4 %collective-permute-start.3 = (f32[7,64,128]{2,1,0:T(8,128)S(1)}, f32[7,64,128]{2,1,0:T(8,128)S(1)}, u32[]{:S(2)}, u32[]{:S(2)}) collective-permute-start(f32[7,64,128]{2,1,0:T(8,128)S(1)} %pad_maximum_fusion), channel_id=1, source_target_pairs={{1,16},{2,17},{3,18},{4,19},{5,20},{6,21},{7,22},{8,23},{9,24},{10... | collective-permute-start | bytes 688136 | tf_op jit(solution)/shard_map/ppermute | solution.py:40
  7.8 7.5 %collective-permute-start.2 = (f32[6,64,128]{2,1,0:T(8,128)S(1)}, f32[6,64,128]{2,1,0:T(8,128)S(1)}, u32[]{:S(2)}, u32[]{:S(2)}) collective-permute-start(f32[6,64,128]{2,1,0:T(8,128)S(1)} %bitcast.19), channel_id=1, source_target_pairs={{0,1},{1,2},{2,3},{3,4},{4,5},{5,6},{6,7},{7,8},{8,9},{9,10},{10,1... | collective-permute-start | bytes 589832 | tf_op jit(solution)/shard_map/ppermute | solution.py:40
  9.1 3.9 %collective-permute-start = (s32[1]{0:T(128)}, s32[1]{0:T(128)}, u32[]{:S(2)}, u32[]{:S(2)}) collective-permute-start(s32[1]{0:T(128)} %param.4), channel_id=1, source_target_pairs={{0,16},{16,0},{32,48},{48,32},{64,80},{80,64},{96,112},{112,96},{1... | collective-permute-start | bytes 20 | tf_op jit(solution)/shard_map/ppermute | solution.py:29
  39.8 4.2 %collective-permute-start.4 = (f32[31,8,128]{2,1,0:T(8,128)S(1)}, f32[31,8,128]{2,1,0:T(8,128)S(1)}, u32[]{:S(2)}, u32[]{:S(2)}) collective-permute-start(f32[31,8,128]{2,1,0:T(8,128)S(1)} %pad_maximum_fusion.1), channel_id=1, source_target_pairs={{0,16},{16,0},{32,48},{48,32},{64,80},{80,64},{96,112},{112,96},{1... | collective-permute-start | bytes 380936 | tf_op jit(solution)/shard_map/ppermute | solution.py:29
  40.7 6.2 %collective-permute-start.5 = (f32[31,8,128]{2,1,0:T(8,128)S(1)}, f32[31,8,128]{2,1,0:T(8,128)S(1)}, u32[]{:S(2)}, u32[]{:S(2)}) collective-permute-start(f32[31,8,128]{2,1,0:T(8,128)S(1)} %pad_maximum_fusion.2), channel_id=1, source_target_pairs={{1,16},{2,17},{3,18},{4,19},{5,20},{6,21},{7,22},{8,23},{9,24},{10... | collective-permute-start | bytes 380936 | tf_op jit(solution)/shard_map/ppermute | solution.py:40
  57.3 1.2 %collective-permute-start.6 = (f32[8,128]{1,0:T(8,128)S(1)}, f32[8,128]{1,0:T(8,128)S(1)}, u32[]{:S(2)}, u32[]{:S(2)}) collective-permute-start(f32[8,128]{1,0:T(8,128)S(1)} %slice_reduce_fusion), channel_id=1, source_target_pairs={{0,16},{16,0},{32,48},{48,32},{64,80},{80,64},{96,112},{112,96},{1... | collective-permute-start | bytes 12296 | tf_op jit(solution)/shard_map/ppermute | solution.py:29
  58.5 22.4 %collective-permute-start.7 = (f32[8,13,8,128]{3,2,1,0:T(8,128)S(1)}, f32[8,13,8,128]{3,2,1,0:T(8,128)S(1)}, u32[]{:S(2)}, u32[]{:S(2)}) collective-permute-start(f32[8,13,8,128]{3,2,1,0:T(8,128)S(1)} %all_to_all.16.gathered), channel_id=1, source_target_pairs={{0,16},{16,0},{32,48},{48,32},{64,80},{80,64},{96,112},{112,96},{1... | collective-permute-start | bytes 1277960 | tf_op jit(solution)/shard_map/ppermute | solution.py:29

commit v9 on v8

--- a/solution.py
+++ b/solution.py
@@ -355,10 +355,10 @@
     tiles = run(vectors_kernel, shape(chips, 13, *tile), place, mine, near, far)
 
     gathered = over_chips(tiles)
-    sums = gathered[:, 12].sum(axis=0)
-    sums, gathered = lax.optimization_barrier((sums + swap_cores(sums), gathered))
     others = swap_cores(gathered)
-    sums = lax.all_to_all(jnp.broadcast_to(sums, (slabs, *tile)), "gz", split_axis=0, concat_axis=0, tiled=True)
+    members = [[(2 * chip + core) * slabs + g for core in range(2) for g in range(slabs)] for chip in range(chips)]
+    sums = jnp.broadcast_to(gathered[:, 12].sum(axis=0), (2 * slabs, *tile))
+    sums = lax.all_to_all(sums, ("freq", "gz"), split_axis=0, concat_axis=0, tiled=True, axis_index_groups=members)
     result = shape(2, 4, ny, nx)
     return tuple(run(outputs_kernel, (result, result), place, sums, gathered, others))
 

time: 82.8 us -> 83.8 us (1.012)
  blocking collectives: 54 us -> 56.2 us
  waiting for transfers between devices: 4.64 us -> 3.35 us
    all_to_all x1, blocking collectives: 22.2 us -> 24.4 us  [body(): lax.all_to_all(sums, ('freq', 'gz'), split_axis=0, concat_axis=0, tiled=T...]
    ppermute x5 -> x4, waiting for transfers between devices: 1.52 us -> 0.23 us  [swap_cores(): return lax.ppermute(array, 'freq', pairs)]
    ppermute x5 -> x4, starting transfers between devices: 7.22 us -> 7.03 us  [swap_cores(): return lax.ppermute(array, 'freq', pairs)]
  transfers between devices with their start and end apart: 8 -> 7, of which waited for: 4 -> 3; matrix products, arithmetic and copies ran while one was open for 2% -> 2% of each run, Pallas kernels for 2% -> 3%
where the time goes in v9:
time: 83.8 us; the launch traced here: 83.4 us
  blocking collectives  56.2 us (67%)
  starting transfers between devices  13.6 us (16%)
  Pallas kernels  6.8 us (8%)
  waiting for transfers between devices  3.35 us (4%)
  other arithmetic  2.01 us (2%)
  between operations  1.41 us (2%)
    all_to_all x2, blocking collectives, over_chips(): lax.all_to_all(parts, 'freq', split_axis=0, concat_axis=0, tiled=True, ax...  31.8 us
    all_to_all x1, blocking collectives, body(): lax.all_to_all(sums, ('freq', 'gz'), split_axis=0, concat_axis=0, tiled=T...  24.4 us
    ppermute x4, starting transfers between devices, swap_cores(): return lax.ppermute(array, 'freq', pairs)  7.03 us
    pallas_call x4, Pallas kernels, run(): pl.pallas_call(kernel, out_shape=shapes, in_specs=[smem] * scalars + [vme...  6.8 us
    ppermute x3, starting transfers between devices, to_slabs(): return lax.ppermute(array, ('freq', 'gz'), pairs)  6.54 us
    ppermute x3, waiting for transfers between devices, to_slabs(): return lax.ppermute(array, ('freq', 'gz'), pairs)  3.12 us
  transfers between devices with their start and end apart: 7, of which 3 were waited for; matrix products, arithmetic and copies ran while one was open for 2% of the time, Pallas kernels for 3%

profile of v9, /device:TPU:1, one launch (start us, length us, event | category | flops | bytes accessed | tf_op | source)
XLA Modules:
  0.0 83.4 jit_solution(5979912549056530951)
XLA Ops:
  0.6 0.0 copy-start
  0.6 0.0 copy-start.1
  0.7 3.3 %collective-permute-start.1 = (f32[1,2,3,4,64,128]{5,4,3,2,1,0:T(8,128)}, f32[1,2,3,4,64,128]{5,4,3,2,1,0:T(8,128)S(1)}, u32[]{:S(2)}, u32[]{:S(2)}) collective-permute-start(f32[1,2,3,4,64,128]{5,4,3,2,1,0:T(8,128)} %param.3), channel_id=1, source_target_pairs={{0,16},{16,0},{32,48},{48,32},{64,80},{80,64},{96,112},{112,96},{1... | collective-permute-start | bytes 2359304 | tf_op jit(solution)/shard_map/ppermute | solution.py:29
  4.0 0.8 slice_convert_fusion
  4.7 1.1 %slice_select_fusion = (f32[2,3,1,64,128]{4,3,2,1,0:T(8,128)S(1)}, f32[2,3,1,64,128]{4,3,2,1,0:T(8,128)S(1)}) fusion(f32[2,3,4,64,128]{4,3,2,1,0:T(8,128)} %bitcast.11, pred[]{:T(512)S(6)} %eq.8), kind=kLoop, calls=%fused_computation.1 | loop fusion | flops 98304 | bytes 786433 | tf_op jit(solution)/shard_map/jit(_where)/select_n | solution.py:343
  5.8 1.9 %collective-permute-start.3 = (f32[7,64,128]{2,1,0:T(8,128)S(1)}, f32[7,64,128]{2,1,0:T(8,128)S(1)}, u32[]{:S(2)}, u32[]{:S(2)}) collective-permute-start(f32[7,64,128]{2,1,0:T(8,128)S(1)} %pad_maximum_fusion), channel_id=1, source_target_pairs={{1,16},{2,17},{3,18},{4,19},{5,20},{6,21},{7,22},{8,23},{9,24},{10... | collective-permute-start | bytes 688136 | tf_op jit(solution)/shard_map/ppermute | solution.py:40
  7.8 1.3 %collective-permute-start.2 = (f32[6,64,128]{2,1,0:T(8,128)S(1)}, f32[6,64,128]{2,1,0:T(8,128)S(1)}, u32[]{:S(2)}, u32[]{:S(2)}) collective-permute-start(f32[6,64,128]{2,1,0:T(8,128)S(1)} %bitcast.19), channel_id=1, source_target_pairs={{0,1},{1,2},{2,3},{3,4},{4,5},{5,6},{6,7},{7,8},{8,9},{9,10},{10,1... | collective-permute-start | bytes 589832 | tf_op jit(solution)/shard_map/ppermute | solution.py:40
  9.1 2.8 %collective-permute-start = (s32[1]{0:T(128)}, s32[1]{0:T(128)}, u32[]{:S(2)}, u32[]{:S(2)}) collective-permute-start(s32[1]{0:T(128)} %param.4), channel_id=1, source_target_pairs={{0,16},{16,0},{32,48},{48,32},{64,80},{80,64},{96,112},{112,96},{1... | collective-permute-start | bytes 20 | tf_op jit(solution)/shard_map/ppermute | solution.py:29
  12.6 0.1 pad_add_fusion.place
  12.6 0.2 collective-permute-done.other_index
  12.8 0.0 collective-permute-done.1
  12.8 0.0 copy-done
  12.9 0.0 copy-done.1
  12.9 2.2 %shard_map.50.inner = f32[8,20,8,128]{3,2,1,0:T(8,128)S(1)} custom-call(s32[2]{0:T(128)S(1)} %pad_add_fusion.place, s32[1]{0:T(128)S(6)} %copy.5.index, s32[1]{0:T(128)} %collective-permute-done.other_index, f32[2,3,4,64,128]{4,3,2,1,0:T(8,128)S(1)} %bitcast.12, f32[2,3,4,64,128]{4,3,2,1,0:T(8,128)S(1)} %bitcast.14, s32[4,64,128]{2,1,0:T(8,128)S(1)} %copy-done.1), custom_call_target="tpu_custom_call" | custom-call | tf_op jit(solution)/shard_map/pallas_call | solution.py:318
  15.0 0.2 collective-permute-done.2.same
  15.3 0.0 collective-permute-done.3.cross
  15.3 2.3 %shard_map.51 = f32[8,40,8,128]{3,2,1,0:T(8,128)S(1)} custom-call(s32[2]{0:T(128)S(1)} %pad_add_fusion.place, s32[1]{0:T(128)S(6)} %copy.5.index, s32[1]{0:T(128)} %collective-permute-done.other_index, f32[2,3,4,64,128]{4,3,2,1,0:T(8,128)S(1)} %bitcast.13, f32[2,3,4,64,128]{4,3,2,1,0:T(8,128)S(1)} %bitcast.15, s32[4,64,128]{2,1,0:T(8,128)S(1)} %copy-done.1, ...), custom_call_target="tpu_custom_call" | custom-call | tf_op jit(solution)/shard_map/pallas_call | solution.py:318
  17.5 22.3 %all_to_all.15 = f32[8,40,8,128]{3,2,1,0:T(8,128)S(1)} all-to-all(f32[8,40,8,128]{3,2,1,0:T(8,128)S(1)} %shard_map.51), channel_id=1, replica_groups={{0,32,64,96,128,160,192,224},{16,48,80,112,144,176,208,240},{1,33,65,97..., dimensions={0} | all-to-all | bytes 2621440 | tf_op jit(solution)/shard_map/all_to_all | solution.py:46
  39.9 0.1 reduce_sum.18
  40.0 0.9 %collective-permute-start.4 = (f32[31,8,128]{2,1,0:T(8,128)S(1)}, f32[31,8,128]{2,1,0:T(8,128)S(1)}, u32[]{:S(2)}, u32[]{:S(2)}) collective-permute-start(f32[31,8,128]{2,1,0:T(8,128)S(1)} %pad_maximum_fusion.1), channel_id=1, source_target_pairs={{0,16},{16,0},{32,48},{48,32},{64,80},{80,64},{96,112},{112,96},{1... | collective-permute-start | bytes 380936 | tf_op jit(solution)/shard_map/ppermute | solution.py:29
  40.9 3.3 %collective-permute-start.5 = (f32[31,8,128]{2,1,0:T(8,128)S(1)}, f32[31,8,128]{2,1,0:T(8,128)S(1)}, u32[]{:S(2)}, u32[]{:S(2)}) collective-permute-start(f32[31,8,128]{2,1,0:T(8,128)S(1)} %pad_maximum_fusion.2), channel_id=1, source_target_pairs={{1,16},{2,17},{3,18},{4,19},{5,20},{6,21},{7,22},{8,23},{9,24},{10... | collective-permute-start | bytes 380936 | tf_op jit(solution)/shard_map/ppermute | solution.py:40
  44.2 0.0 collective-permute-done.4.near
  44.2 2.9 %collective-permute-done.5.far = f32[31,8,128]{2,1,0:T(8,128)S(1)} collective-permute-done((f32[31,8,128]{2,1,0:T(8,128)S(1)}, f32[31,8,128]{2,1,0:T(8,128)S(1)}, u32[]{:S(2)}, u32[]{:S(2)}) %collective-permute-start.5) | collective-permute-done | bytes 127008 | tf_op jit(solution)/shard_map/ppermute | solution.py:40
  47.1 0.8 %shard_map.52 = f32[8,13,8,128]{3,2,1,0:T(8,128)S(1)} custom-call(s32[2]{0:T(128)S(1)} %pad_add_fusion.place, f32[2,20,8,128]{3,2,1,0:T(8,128)S(1)} %bitcast.17, f32[31,8,128]{2,1,0:T(8,128)S(1)} %collective-permute-done.4.near, f32[31,8,128]{2,1,0:T(8,128)S(1)} %collective-permute-done.5.far), custom_call_target="tpu_custom_call" | custom-call | tf_op jit(solution)/shard_map/pallas_call | solution.py:318
  48.0 9.5 %all_to_all.16.gathered = f32[8,13,8,128]{3,2,1,0:T(8,128)S(1)} all-to-all(f32[8,13,8,128]{3,2,1,0:T(8,128)S(1)} %shard_map.52), channel_id=1, replica_groups={{0,32,64,96,128,160,192,224},{16,48,80,112,144,176,208,240},{1,33,65,97..., dimensions={0} | all-to-all | bytes 851968 | tf_op jit(solution)/shard_map/all_to_all | solution.py:46
  57.4 0.0 collective-permute-start.6
  57.5 24.4 %all_to_all.17.sums = f32[32,8,128]{2,1,0:T(8,128)S(1)} all-to-all(f32[32,8,128]{2,1,0:T(8,128)S(1)} %broadcast_in_dim.3), channel_id=1, replica_groups={{0,1,2,3,4,5,6,7,8,9,10,11,12,13,14,15,16,17,18,19,20,21,22,23,24,25,26..., dimensions={0} | all-to-all | bytes 262144 | tf_op jit(solution)/shard_map/all_to_all | solution.py:361
  81.9 0.0 collective-permute-done.6.others
  81.9 1.5 %shard_map.53 = (f32[2,4,64,128]{3,2,1,0:T(8,128)}, f32[2,4,64,128]{3,2,1,0:T(8,128)}) custom-call(s32[2]{0:T(128)S(1)} %pad_add_fusion.place, f32[32,8,128]{2,1,0:T(8,128)S(1)} %all_to_all.17.sums, f32[8,13,8,128]{3,2,1,0:T(8,128)S(1)} %all_to_all.16.gathered, f32[8,13,8,128]{3,2,1,0:T(8,128)S(1)} %collective-permute-done.6.others), custom_call_target="tpu_custom_call" | custom-call | tf_op jit(solution)/shard_map/pallas_call | solution.py:318
  (7 shorter events, 0.1 us)
Async XLA Ops:
  0.6 12.2 %copy-start = (f32[1,2,3,4,64,128]{5,4,3,2,1,0:T(8,128)S(1)}, f32[1,2,3,4,64,128]{5,4,3,2,1,0:T(8,128)}, u32[]{:S(2)}) copy-start(f32[1,2,3,4,64,128]{5,4,3,2,1,0:T(8,128)} %param.3) | copy-start | bytes 2359300
  0.6 12.2 %copy-start.1 = (s32[4,64,128]{2,1,0:T(8,128)S(1)}, s32[4,64,128]{2,1,0:T(8,128)}, u32[]{:S(2)}) copy-start(s32[4,64,128]{2,1,0:T(8,128)} %tissue.3) | copy-start | bytes 393220
  0.7 12.2 %collective-permute-start.1 = (f32[1,2,3,4,64,128]{5,4,3,2,1,0:T(8,128)}, f32[1,2,3,4,64,128]{5,4,3,2,1,0:T(8,128)S(1)}, u32[]{:S(2)}, u32[]{:S(2)}) collective-permute-start(f32[1,2,3,4,64,128]{5,4,3,2,1,0:T(8,128)} %param.3), channel_id=1, source_target_pairs={{0,16},{16,0},{32,48},{48,32},{64,80},{80,64},{96,112},{112,96},{1... | collective-permute-start | bytes 2359304 | tf_op jit(solution)/shard_map/ppermute | solution.py:29
  5.8 9.4 %collective-permute-start.3 = (f32[7,64,128]{2,1,0:T(8,128)S(1)}, f32[7,64,128]{2,1,0:T(8,128)S(1)}, u32[]{:S(2)}, u32[]{:S(2)}) collective-permute-start(f32[7,64,128]{2,1,0:T(8,128)S(1)} %pad_maximum_fusion), channel_id=1, source_target_pairs={{1,16},{2,17},{3,18},{4,19},{5,20},{6,21},{7,22},{8,23},{9,24},{10... | collective-permute-start | bytes 688136 | tf_op jit(solution)/shard_map/ppermute | solution.py:40
  7.8 7.5 %collective-permute-start.2 = (f32[6,64,128]{2,1,0:T(8,128)S(1)}, f32[6,64,128]{2,1,0:T(8,128)S(1)}, u32[]{:S(2)}, u32[]{:S(2)}) collective-permute-start(f32[6,64,128]{2,1,0:T(8,128)S(1)} %bitcast.19), channel_id=1, source_target_pairs={{0,1},{1,2},{2,3},{3,4},{4,5},{5,6},{6,7},{7,8},{8,9},{9,10},{10,1... | collective-permute-start | bytes 589832 | tf_op jit(solution)/shard_map/ppermute | solution.py:40
  9.1 3.8 %collective-permute-start = (s32[1]{0:T(128)}, s32[1]{0:T(128)}, u32[]{:S(2)}, u32[]{:S(2)}) collective-permute-start(s32[1]{0:T(128)} %param.4), channel_id=1, source_target_pairs={{0,16},{16,0},{32,48},{48,32},{64,80},{80,64},{96,112},{112,96},{1... | collective-permute-start | bytes 20 | tf_op jit(solution)/shard_map/ppermute | solution.py:29
  40.0 4.2 %collective-permute-start.4 = (f32[31,8,128]{2,1,0:T(8,128)S(1)}, f32[31,8,128]{2,1,0:T(8,128)S(1)}, u32[]{:S(2)}, u32[]{:S(2)}) collective-permute-start(f32[31,8,128]{2,1,0:T(8,128)S(1)} %pad_maximum_fusion.1), channel_id=1, source_target_pairs={{0,16},{16,0},{32,48},{48,32},{64,80},{80,64},{96,112},{112,96},{1... | collective-permute-start | bytes 380936 | tf_op jit(solution)/shard_map/ppermute | solution.py:29
  40.9 6.2 %collective-permute-start.5 = (f32[31,8,128]{2,1,0:T(8,128)S(1)}, f32[31,8,128]{2,1,0:T(8,128)S(1)}, u32[]{:S(2)}, u32[]{:S(2)}) collective-permute-start(f32[31,8,128]{2,1,0:T(8,128)S(1)} %pad_maximum_fusion.2), channel_id=1, source_target_pairs={{1,16},{2,17},{3,18},{4,19},{5,20},{6,21},{7,22},{8,23},{9,24},{10... | collective-permute-start | bytes 380936 | tf_op jit(solution)/shard_map/ppermute | solution.py:40
  57.4 24.4 %collective-permute-start.6 = (f32[8,13,8,128]{3,2,1,0:T(8,128)S(1)}, f32[8,13,8,128]{3,2,1,0:T(8,128)S(1)}, u32[]{:S(2)}, u32[]{:S(2)}) collective-permute-start(f32[8,13,8,128]{3,2,1,0:T(8,128)S(1)} %all_to_all.16.gathered), channel_id=1, source_target_pairs={{0,16},{16,0},{32,48},{48,32},{64,80},{80,64},{96,112},{112,96},{1... | collective-permute-start | bytes 1277960 | tf_op jit(solution)/shard_map/ppermute | solution.py:29

commit v10 on v8

--- a/solution.py
+++ b/solution.py
@@ -287,7 +287,7 @@
             out[chip, k] = tile
 
 
-def outputs_kernel(place, sums, gathered, others, modulus, residual):
+def outputs_kernel(place, sums, gathered, others, modulus, residual, held, sems):
     core = place[0]
     chips = gathered.shape[0]
     total = sums[0]
@@ -303,23 +303,29 @@
     shape = (chips, ROWS, total.shape[-1])
     p = jnp.broadcast_to((step + second * grown).reshape(1, 1, -1), shape)
     q = jnp.broadcast_to((step * second).reshape(1, 1, -1), shape)
+    copies = []
     for source, first in ((gathered, 2 * core), (others, 2 - 2 * core)):
         for part in range(2):
             for plane in range(2):
                 v0, v1, v2 = (source[:, 4 * k + 2 * part + plane] for k in range(3))
                 flat = (chips * ROWS, shape[-1])
-                modulus[part, first + plane] = (p * v0 - q * v1).reshape(flat)
-                residual[part, first + plane] = (v0 - p * v1 + q * v2).reshape(flat)
-
-
-def run(kernel, shapes, *arrays, scratch=(), scalars=1):
+                for out, value in ((modulus, p * v0 - q * v1), (residual, v0 - p * v1 + q * v2)):
+                    slot = len(copies)
+                    held[slot] = value.reshape(flat)
+                    copies.append(pltpu.make_async_copy(held.at[slot], out.at[part, first + plane], sems.at[slot]))
+                    copies[-1].start()
+    for copy in copies:
+        copy.wait()
+
+
+def run(kernel, shapes, *arrays, scratch=(), scalars=1, outs=None):
     vmem = pl.BlockSpec(memory_space=pltpu.VMEM)
     smem = pl.BlockSpec(memory_space=pltpu.SMEM)
     return pl.pallas_call(
         kernel,
         out_shape=shapes,
         in_specs=[smem] * scalars + [vmem] * (len(arrays) - scalars),
-        out_specs=jax.tree.map(lambda _: vmem, shapes),
+        out_specs=jax.tree.map(lambda _: outs or vmem, shapes),
         scratch_shapes=list(scratch),
         compiler_params=pltpu.CompilerParams(vmem_limit_bytes=VMEM_BYTES),
     )(*arrays)
@@ -337,12 +343,13 @@
     def shape(*dims):
         return jax.ShapeDtypeStruct(dims, jnp.float32)
 
+    other = swap_cores(displacement)[0]
+    other_index = swap_cores(freq_index)
+    displacement, tissue, other_index = lax.optimization_barrier((displacement, tissue, other_index))
     field = displacement[0]
     first, last = (field[:, :, k].reshape(6, ny, nx) for k in (0, 3))
     same = to_slabs(jnp.where(low, last, first), 0, 0)
     cross = to_slabs(jnp.concatenate([jnp.where(low, first, last), tissue[:1].astype(jnp.float32)]), 1, 1)
-    other = swap_cores(displacement)[0]
-    other_index = swap_cores(freq_index)
 
     held = (place, freq_index, other_index, field, other, tissue)
     scratch = [pltpu.VMEM((15, ny + 2 * ROWS, nx), jnp.float32)]
@@ -360,7 +367,9 @@
     others = swap_cores(gathered)
     sums = lax.all_to_all(jnp.broadcast_to(sums, (slabs, *tile)), "gz", split_axis=0, concat_axis=0, tiled=True)
     result = shape(2, 4, ny, nx)
-    return tuple(run(outputs_kernel, (result, result), place, sums, gathered, others))
+    scratch = [pltpu.VMEM((16, ny, nx), jnp.float32), pltpu.SemaphoreType.DMA((16,))]
+    outs = pl.BlockSpec(memory_space=pl.ANY)
+    return tuple(run(outputs_kernel, (result, result), place, sums, gathered, others, scratch=scratch, outs=outs))
 
 
 def solution(mesh):

time: 82.8 us -> 83.9 us (1.013)
  waiting for transfers between devices: 4.64 us -> 8.07 us
  starting transfers between devices: 13.8 us -> 11.6 us
    ppermute x5, starting transfers between devices: 7.22 us -> 3.99 us  [swap_cores(): return lax.ppermute(array, 'freq', pairs)]
    ppermute x3, waiting for transfers between devices: 3.12 us -> 5.92 us  [to_slabs(): return lax.ppermute(array, ('freq', 'gz'), pairs)]
    ppermute x3, starting transfers between devices: 6.54 us -> 7.65 us  [to_slabs(): return lax.ppermute(array, ('freq', 'gz'), pairs)]
where the time goes in v10:
time: 83.9 us; the launch traced here: 83.5 us
  blocking collectives  53.7 us (64%)
  starting transfers between devices  11.6 us (14%)
  waiting for transfers between devices  8.07 us (10%)
  Pallas kernels  6.59 us (8%)
  other arithmetic  2.01 us (2%)
  between operations  1.41 us (2%)
    all_to_all x2, blocking collectives, over_chips(): lax.all_to_all(parts, 'freq', split_axis=0, concat_axis=0, tiled=True, ax...  31.7 us
    all_to_all x1, blocking collectives, body(): lax.all_to_all(jnp.broadcast_to(sums, (slabs, *tile)), 'gz', split_axis=0...  22.1 us
    ppermute x3, starting transfers between devices, to_slabs(): return lax.ppermute(array, ('freq', 'gz'), pairs)  7.65 us
    pallas_call x4, Pallas kernels, run(): pl.pallas_call(kernel, out_shape=shapes, in_specs=[smem] * scalars + [vme...  6.59 us
    ppermute x3, waiting for transfers between devices, to_slabs(): return lax.ppermute(array, ('freq', 'gz'), pairs)  5.92 us
    ppermute x5, starting transfers between devices, swap_cores(): return lax.ppermute(array, 'freq', pairs)  3.99 us
    ppermute x5, waiting for transfers between devices, swap_cores(): return lax.ppermute(array, 'freq', pairs)  2.15 us
  transfers between devices with their start and end apart: 8, of which 4 were waited for; matrix products, arithmetic and copies ran while one was open for 2% of the time, Pallas kernels for 2%

profile of v10, /device:TPU:1, one launch (start us, length us, event | category | flops | bytes accessed | tf_op | source)
XLA Modules:
  0.0 83.5 jit_solution(9350082668051870510)
XLA Ops:
  0.6 0.0 copy-start
  0.6 0.0 copy-start.1
  0.7 3.3 %collective-permute-start = (s32[1]{0:T(128)}, s32[1]{0:T(128)}, u32[]{:S(2)}, u32[]{:S(2)}) collective-permute-start(s32[1]{0:T(128)} %param.4), channel_id=1, source_target_pairs={{0,16},{16,0},{32,48},{48,32},{64,80},{80,64},{96,112},{112,96},{1... | collective-permute-start | bytes 20 | tf_op jit(solution)/shard_map/ppermute | solution.py:29
  4.0 0.1 collective-permute-start.1
  4.1 1.0 %collective-permute-done.other_index = s32[1]{0:T(128)} collective-permute-done((s32[1]{0:T(128)}, s32[1]{0:T(128)}, u32[]{:S(2)}, u32[]{:S(2)}) %collective-permute-start) | collective-permute-done | bytes 36 | tf_op jit(solution)/shard_map/ppermute | solution.py:29
  5.1 0.8 slice_convert_fusion
  5.8 1.1 %slice_select_fusion = (f32[2,3,1,64,128]{4,3,2,1,0:T(8,128)S(1)}, f32[2,3,1,64,128]{4,3,2,1,0:T(8,128)S(1)}) fusion(f32[2,3,4,64,128]{4,3,2,1,0:T(8,128)} %bitcast.11, pred[]{:T(512)S(6)} %eq.8), kind=kLoop, calls=%fused_computation.1 | loop fusion | flops 98304 | bytes 786433 | tf_op jit(solution)/shard_map/jit(_where)/select_n | solution.py:352
  6.9 2.0 %collective-permute-start.3 = (f32[7,64,128]{2,1,0:T(8,128)S(1)}, f32[7,64,128]{2,1,0:T(8,128)S(1)}, u32[]{:S(2)}, u32[]{:S(2)}) collective-permute-start(f32[7,64,128]{2,1,0:T(8,128)S(1)} %pad_maximum_fusion), channel_id=1, source_target_pairs={{1,16},{2,17},{3,18},{4,19},{5,20},{6,21},{7,22},{8,23},{9,24},{10... | collective-permute-start | bytes 688136 | tf_op jit(solution)/shard_map/ppermute | solution.py:40
  8.9 1.3 %collective-permute-start.2 = (f32[6,64,128]{2,1,0:T(8,128)S(1)}, f32[6,64,128]{2,1,0:T(8,128)S(1)}, u32[]{:S(2)}, u32[]{:S(2)}) collective-permute-start(f32[6,64,128]{2,1,0:T(8,128)S(1)} %bitcast.19), channel_id=1, source_target_pairs={{0,1},{1,2},{2,3},{3,4},{4,5},{5,6},{6,7},{7,8},{8,9},{9,10},{10,1... | collective-permute-start | bytes 589832 | tf_op jit(solution)/shard_map/ppermute | solution.py:40
  10.9 0.1 pad_add_fusion.place
  10.9 0.0 collective-permute-done.1
  11.0 0.0 copy-done
  11.0 0.0 copy-done.1
  11.0 2.0 %shard_map.50.inner = f32[8,20,8,128]{3,2,1,0:T(8,128)S(1)} custom-call(s32[2]{0:T(128)S(1)} %pad_add_fusion.place, s32[1]{0:T(128)S(6)} %copy.5.index, s32[1]{0:T(128)} %collective-permute-done.other_index, f32[2,3,4,64,128]{4,3,2,1,0:T(8,128)S(1)} %bitcast.12, f32[2,3,4,64,128]{4,3,2,1,0:T(8,128)S(1)} %bitcast.14, s32[4,64,128]{2,1,0:T(8,128)S(1)} %copy-done.1), custom_call_target="tpu_custom_call" | custom-call | tf_op jit(solution)/shard_map/pallas_call | solution.py:324
  13.0 3.3 %collective-permute-done.2.same = f32[6,64,128]{2,1,0:T(8,128)S(1)} collective-permute-done((f32[6,64,128]{2,1,0:T(8,128)S(1)}, f32[6,64,128]{2,1,0:T(8,128)S(1)}, u32[]{:S(2)}, u32[]{:S(2)}) %collective-permute-start.2) | collective-permute-done | bytes 196640 | tf_op jit(solution)/shard_map/ppermute | solution.py:40
  16.4 0.0 collective-permute-done.3.cross
  16.4 2.1 %shard_map.51 = f32[8,40,8,128]{3,2,1,0:T(8,128)S(1)} custom-call(s32[2]{0:T(128)S(1)} %pad_add_fusion.place, s32[1]{0:T(128)S(6)} %copy.5.index, s32[1]{0:T(128)} %collective-permute-done.other_index, f32[2,3,4,64,128]{4,3,2,1,0:T(8,128)S(1)} %bitcast.13, f32[2,3,4,64,128]{4,3,2,1,0:T(8,128)S(1)} %bitcast.15, s32[4,64,128]{2,1,0:T(8,128)S(1)} %copy-done.1, ...), custom_call_target="tpu_custom_call" | custom-call | tf_op jit(solution)/shard_map/pallas_call | solution.py:324
  18.5 22.1 %all_to_all.15 = f32[8,40,8,128]{3,2,1,0:T(8,128)S(1)} all-to-all(f32[8,40,8,128]{3,2,1,0:T(8,128)S(1)} %shard_map.51), channel_id=1, replica_groups={{0,32,64,96,128,160,192,224},{16,48,80,112,144,176,208,240},{1,33,65,97..., dimensions={0} | all-to-all | bytes 2621440 | tf_op jit(solution)/shard_map/all_to_all | solution.py:46
  40.6 0.1 reduce_sum.18
  40.7 0.4 collective-permute-start.4
  41.1 4.4 %collective-permute-start.5 = (f32[31,8,128]{2,1,0:T(8,128)S(1)}, f32[31,8,128]{2,1,0:T(8,128)S(1)}, u32[]{:S(2)}, u32[]{:S(2)}) collective-permute-start(f32[31,8,128]{2,1,0:T(8,128)S(1)} %pad_maximum_fusion.2), channel_id=1, source_target_pairs={{1,16},{2,17},{3,18},{4,19},{5,20},{6,21},{7,22},{8,23},{9,24},{10... | collective-permute-start | bytes 380936 | tf_op jit(solution)/shard_map/ppermute | solution.py:40
  45.5 0.0 collective-permute-done.4.near
  45.5 2.6 %collective-permute-done.5.far = f32[31,8,128]{2,1,0:T(8,128)S(1)} collective-permute-done((f32[31,8,128]{2,1,0:T(8,128)S(1)}, f32[31,8,128]{2,1,0:T(8,128)S(1)}, u32[]{:S(2)}, u32[]{:S(2)}) %collective-permute-start.5) | collective-permute-done | bytes 127008 | tf_op jit(solution)/shard_map/ppermute | solution.py:40
  48.1 0.8 %shard_map.52 = f32[8,13,8,128]{3,2,1,0:T(8,128)S(1)} custom-call(s32[2]{0:T(128)S(1)} %pad_add_fusion.place, f32[2,20,8,128]{3,2,1,0:T(8,128)S(1)} %bitcast.17, f32[31,8,128]{2,1,0:T(8,128)S(1)} %collective-permute-done.4.near, f32[31,8,128]{2,1,0:T(8,128)S(1)} %collective-permute-done.5.far), custom_call_target="tpu_custom_call" | custom-call | tf_op jit(solution)/shard_map/pallas_call | solution.py:324
  48.9 9.6 %all_to_all.16.gathered = f32[8,13,8,128]{3,2,1,0:T(8,128)S(1)} all-to-all(f32[8,13,8,128]{3,2,1,0:T(8,128)S(1)} %shard_map.52), channel_id=1, replica_groups={{0,32,64,96,128,160,192,224},{16,48,80,112,144,176,208,240},{1,33,65,97..., dimensions={0} | all-to-all | bytes 851968 | tf_op jit(solution)/shard_map/all_to_all | solution.py:46
  58.5 0.0 collective-permute-start.6
  58.5 1.2 %collective-permute-done.6 = f32[8,128]{1,0:T(8,128)S(1)} collective-permute-done((f32[8,128]{1,0:T(8,128)S(1)}, f32[8,128]{1,0:T(8,128)S(1)}, u32[]{:S(2)}, u32[]{:S(2)}) %collective-permute-start.6) | collective-permute-done | bytes 4128 | tf_op jit(solution)/shard_map/ppermute | solution.py:29
  59.7 0.2 collective-permute-start.7
  59.8 22.1 %all_to_all.17.sums = f32[16,8,128]{2,1,0:T(8,128)S(1)} all-to-all(f32[16,8,128]{2,1,0:T(8,128)S(1)} %broadcast_in_dim.3), channel_id=1, replica_groups=mesh['freq'=16,'gz'=16] {'gz'}, dimensions={0} | all-to-all | bytes 131072 | tf_op jit(solution)/shard_map/all_to_all | solution.py:368
  81.9 0.0 collective-permute-done.7.others
  81.9 1.6 %shard_map.53 = (f32[2,4,64,128]{3,2,1,0:T(8,128)}, f32[2,4,64,128]{3,2,1,0:T(8,128)}) custom-call(s32[2]{0:T(128)S(1)} %pad_add_fusion.place, f32[16,8,128]{2,1,0:T(8,128)S(1)} %all_to_all.17.sums, f32[8,13,8,128]{3,2,1,0:T(8,128)S(1)} %all_to_all.16.gathered, f32[8,13,8,128]{3,2,1,0:T(8,128)S(1)} %collective-permute-done.7.others), custom_call_target="tpu_custom_call" | custom-call | tf_op jit(solution)/shard_map/pallas_call | solution.py:324
  (8 shorter events, 0.1 us)
Async XLA Ops:
  0.6 10.3 %copy-start = (f32[1,2,3,4,64,128]{5,4,3,2,1,0:T(8,128)S(1)}, f32[1,2,3,4,64,128]{5,4,3,2,1,0:T(8,128)}, u32[]{:S(2)}) copy-start(f32[1,2,3,4,64,128]{5,4,3,2,1,0:T(8,128)} %param.3) | copy-start | bytes 2359300
  0.6 10.3 %copy-start.1 = (s32[4,64,128]{2,1,0:T(8,128)S(1)}, s32[4,64,128]{2,1,0:T(8,128)}, u32[]{:S(2)}) copy-start(s32[4,64,128]{2,1,0:T(8,128)} %tissue.1) | copy-start | bytes 393220
  0.7 4.4 %collective-permute-start = (s32[1]{0:T(128)}, s32[1]{0:T(128)}, u32[]{:S(2)}, u32[]{:S(2)}) collective-permute-start(s32[1]{0:T(128)} %param.4), channel_id=1, source_target_pairs={{0,16},{16,0},{32,48},{48,32},{64,80},{80,64},{96,112},{112,96},{1... | collective-permute-start | bytes 20 | tf_op jit(solution)/shard_map/ppermute | solution.py:29
  4.0 7.0 %collective-permute-start.1 = (f32[1,2,3,4,64,128]{5,4,3,2,1,0:T(8,128)}, f32[1,2,3,4,64,128]{5,4,3,2,1,0:T(8,128)S(1)}, u32[]{:S(2)}, u32[]{:S(2)}) collective-permute-start(f32[1,2,3,4,64,128]{5,4,3,2,1,0:T(8,128)} %param.3), channel_id=1, source_target_pairs={{0,16},{16,0},{32,48},{48,32},{64,80},{80,64},{96,112},{112,96},{1... | collective-permute-start | bytes 2359304 | tf_op jit(solution)/shard_map/ppermute | solution.py:29
  6.9 9.4 %collective-permute-start.3 = (f32[7,64,128]{2,1,0:T(8,128)S(1)}, f32[7,64,128]{2,1,0:T(8,128)S(1)}, u32[]{:S(2)}, u32[]{:S(2)}) collective-permute-start(f32[7,64,128]{2,1,0:T(8,128)S(1)} %pad_maximum_fusion), channel_id=1, source_target_pairs={{1,16},{2,17},{3,18},{4,19},{5,20},{6,21},{7,22},{8,23},{9,24},{10... | collective-permute-start | bytes 688136 | tf_op jit(solution)/shard_map/ppermute | solution.py:40
  8.9 7.4 %collective-permute-start.2 = (f32[6,64,128]{2,1,0:T(8,128)S(1)}, f32[6,64,128]{2,1,0:T(8,128)S(1)}, u32[]{:S(2)}, u32[]{:S(2)}) collective-permute-start(f32[6,64,128]{2,1,0:T(8,128)S(1)} %bitcast.19), channel_id=1, source_target_pairs={{0,1},{1,2},{2,3},{3,4},{4,5},{5,6},{6,7},{7,8},{8,9},{9,10},{10,1... | collective-permute-start | bytes 589832 | tf_op jit(solution)/shard_map/ppermute | solution.py:40
  40.7 4.8 %collective-permute-start.4 = (f32[31,8,128]{2,1,0:T(8,128)S(1)}, f32[31,8,128]{2,1,0:T(8,128)S(1)}, u32[]{:S(2)}, u32[]{:S(2)}) collective-permute-start(f32[31,8,128]{2,1,0:T(8,128)S(1)} %pad_maximum_fusion.1), channel_id=1, source_target_pairs={{0,16},{16,0},{32,48},{48,32},{64,80},{80,64},{96,112},{112,96},{1... | collective-permute-start | bytes 380936 | tf_op jit(solution)/shard_map/ppermute | solution.py:29
  41.1 7.0 %collective-permute-start.5 = (f32[31,8,128]{2,1,0:T(8,128)S(1)}, f32[31,8,128]{2,1,0:T(8,128)S(1)}, u32[]{:S(2)}, u32[]{:S(2)}) collective-permute-start(f32[31,8,128]{2,1,0:T(8,128)S(1)} %pad_maximum_fusion.2), channel_id=1, source_target_pairs={{1,16},{2,17},{3,18},{4,19},{5,20},{6,21},{7,22},{8,23},{9,24},{10... | collective-permute-start | bytes 380936 | tf_op jit(solution)/shard_map/ppermute | solution.py:40
  58.5 1.2 %collective-permute-start.6 = (f32[8,128]{1,0:T(8,128)S(1)}, f32[8,128]{1,0:T(8,128)S(1)}, u32[]{:S(2)}, u32[]{:S(2)}) collective-permute-start(f32[8,128]{1,0:T(8,128)S(1)} %slice_reduce_fusion), channel_id=1, source_target_pairs={{0,16},{16,0},{32,48},{48,32},{64,80},{80,64},{96,112},{112,96},{1... | collective-permute-start | bytes 12296 | tf_op jit(solution)/shard_map/ppermute | solution.py:29
  59.7 22.2 %collective-permute-start.7 = (f32[8,13,8,128]{3,2,1,0:T(8,128)S(1)}, f32[8,13,8,128]{3,2,1,0:T(8,128)S(1)}, u32[]{:S(2)}, u32[]{:S(2)}) collective-permute-start(f32[8,13,8,128]{3,2,1,0:T(8,128)S(1)} %all_to_all.16.gathered), channel_id=1, source_target_pairs={{0,16},{16,0},{32,48},{48,32},{64,80},{80,64},{96,112},{112,96},{1... | collective-permute-start | bytes 1277960 | tf_op jit(solution)/shard_map/ppermute | solution.py:29

commit v11 on v8

--- a/solution.py
+++ b/solution.py
@@ -339,10 +339,12 @@
 
     field = displacement[0]
     first, last = (field[:, :, k].reshape(6, ny, nx) for k in (0, 3))
-    same = to_slabs(jnp.where(low, last, first), 0, 0)
-    cross = to_slabs(jnp.concatenate([jnp.where(low, first, last), tissue[:1].astype(jnp.float32)]), 1, 1)
     other = swap_cores(displacement)[0]
     other_index = swap_cores(freq_index)
+    same = jnp.where(low, last, first)
+    cross = jnp.concatenate([jnp.where(low, first, last), tissue[:1].astype(jnp.float32)])
+    same, cross, other_index = lax.optimization_barrier((same, cross, other_index))
+    same, cross = to_slabs(same, 0, 0), to_slabs(cross, 1, 1)
 
     held = (place, freq_index, other_index, field, other, tissue)
     scratch = [pltpu.VMEM((15, ny + 2 * ROWS, nx), jnp.float32)]

time: 82.8 us -> 82.8 us (level)
  waiting for transfers between devices: 4.64 us -> 6.99 us
  starting transfers between devices: 13.8 us -> 11.7 us
    ppermute x5, starting transfers between devices: 7.22 us -> 3.97 us  [swap_cores(): return lax.ppermute(array, 'freq', pairs)]
    ppermute x3, waiting for transfers between devices: 3.12 us -> 5.82 us  [to_slabs(): return lax.ppermute(array, ('freq', 'gz'), pairs)]
    ppermute x3, starting transfers between devices: 6.54 us -> 7.77 us  [to_slabs(): return lax.ppermute(array, ('freq', 'gz'), pairs)]
  transfers between devices with their start and end apart: 8 -> 8, of which waited for: 4 -> 3; matrix products, arithmetic and copies ran while one was open for 2% -> 2% of each run, Pallas kernels for 2% -> 2%
where the time goes in v11:
time: 82.8 us; the launch traced here: 82.5 us
  blocking collectives  53.7 us (65%)
  starting transfers between devices  11.7 us (14%)
  waiting for transfers between devices  6.99 us (8%)
  Pallas kernels  6.52 us (8%)
  other arithmetic  2.01 us (2%)
  between operations  1.42 us (2%)
    all_to_all x2, blocking collectives, over_chips(): lax.all_to_all(parts, 'freq', split_axis=0, concat_axis=0, tiled=True, ax...  31.8 us
    all_to_all x1, blocking collectives, body(): lax.all_to_all(jnp.broadcast_to(sums, (slabs, *tile)), 'gz', split_axis=0...  22 us
    ppermute x3, starting transfers between devices, to_slabs(): return lax.ppermute(array, ('freq', 'gz'), pairs)  7.77 us
    pallas_call x4, Pallas kernels, run(): pl.pallas_call(kernel, out_shape=shapes, in_specs=[smem] * scalars + [vme...  6.52 us
    ppermute x3, waiting for transfers between devices, to_slabs(): return lax.ppermute(array, ('freq', 'gz'), pairs)  5.82 us
    ppermute x5, starting transfers between devices, swap_cores(): return lax.ppermute(array, 'freq', pairs)  3.97 us
  transfers between devices with their start and end apart: 8, of which 3 were waited for; matrix products, arithmetic and copies ran while one was open for 2% of the time, Pallas kernels for 2%

profile of v11, /device:TPU:1, one launch (start us, length us, event | category | flops | bytes accessed | tf_op | source)
XLA Modules:
  0.0 82.5 jit_solution(7279942110170280502)
XLA Ops:
  0.6 0.0 copy-start
  0.6 0.0 copy-start.1
  0.7 3.3 %collective-permute-start = (s32[1]{0:T(128)}, s32[1]{0:T(128)}, u32[]{:S(2)}, u32[]{:S(2)}) collective-permute-start(s32[1]{0:T(128)} %param.4), channel_id=1, source_target_pairs={{0,16},{16,0},{32,48},{48,32},{64,80},{80,64},{96,112},{112,96},{1... | collective-permute-start | bytes 20 | tf_op jit(solution)/shard_map/ppermute | solution.py:29
  4.0 0.1 collective-permute-start.1
  4.1 0.8 slice_convert_fusion
  4.8 1.1 %slice_select_fusion = (f32[2,3,1,64,128]{4,3,2,1,0:T(8,128)S(1)}, f32[2,3,1,64,128]{4,3,2,1,0:T(8,128)S(1)}) fusion(f32[2,3,4,64,128]{4,3,2,1,0:T(8,128)} %bitcast.11, pred[]{:T(512)S(6)} %eq.8), kind=kLoop, calls=%fused_computation.1 | loop fusion | flops 98304 | bytes 786433 | tf_op jit(solution)/shard_map/jit(_where)/select_n | solution.py:345
  5.9 0.0 collective-permute-done.other_index
  5.9 2.1 %collective-permute-start.3 = (f32[7,64,128]{2,1,0:T(8,128)S(1)}, f32[7,64,128]{2,1,0:T(8,128)S(1)}, u32[]{:S(2)}, u32[]{:S(2)}) collective-permute-start(f32[7,64,128]{2,1,0:T(8,128)S(1)} %pad_maximum_fusion), channel_id=1, source_target_pairs={{1,16},{2,17},{3,18},{4,19},{5,20},{6,21},{7,22},{8,23},{9,24},{10... | collective-permute-start | bytes 688136 | tf_op jit(solution)/shard_map/ppermute | solution.py:40
  8.0 1.3 %collective-permute-start.2 = (f32[6,64,128]{2,1,0:T(8,128)S(1)}, f32[6,64,128]{2,1,0:T(8,128)S(1)}, u32[]{:S(2)}, u32[]{:S(2)}) collective-permute-start(f32[6,64,128]{2,1,0:T(8,128)S(1)} %bitcast.19), channel_id=1, source_target_pairs={{0,1},{1,2},{2,3},{3,4},{4,5},{5,6},{6,7},{7,8},{8,9},{9,10},{10,1... | collective-permute-start | bytes 589832 | tf_op jit(solution)/shard_map/ppermute | solution.py:40
  10.0 0.1 pad_add_fusion.place
  10.1 0.0 collective-permute-done.1
  10.1 0.0 copy-done
  10.1 0.0 copy-done.1
  10.1 2.0 %shard_map.50.inner = f32[8,20,8,128]{3,2,1,0:T(8,128)S(1)} custom-call(s32[2]{0:T(128)S(1)} %pad_add_fusion.place, s32[1]{0:T(128)S(6)} %copy.5.index, s32[1]{0:T(128)} %collective-permute-done.other_index, f32[2,3,4,64,128]{4,3,2,1,0:T(8,128)S(1)} %bitcast.12, f32[2,3,4,64,128]{4,3,2,1,0:T(8,128)S(1)} %bitcast.14, s32[4,64,128]{2,1,0:T(8,128)S(1)} %copy-done.1), custom_call_target="tpu_custom_call" | custom-call | tf_op jit(solution)/shard_map/pallas_call | solution.py:318
  12.1 3.2 %collective-permute-done.2.same = f32[6,64,128]{2,1,0:T(8,128)S(1)} collective-permute-done((f32[6,64,128]{2,1,0:T(8,128)S(1)}, f32[6,64,128]{2,1,0:T(8,128)S(1)}, u32[]{:S(2)}, u32[]{:S(2)}) %collective-permute-start.2) | collective-permute-done | bytes 196640 | tf_op jit(solution)/shard_map/ppermute | solution.py:40
  15.4 0.0 collective-permute-done.3.cross
  15.4 2.1 %shard_map.51 = f32[8,40,8,128]{3,2,1,0:T(8,128)S(1)} custom-call(s32[2]{0:T(128)S(1)} %pad_add_fusion.place, s32[1]{0:T(128)S(6)} %copy.5.index, s32[1]{0:T(128)} %collective-permute-done.other_index, f32[2,3,4,64,128]{4,3,2,1,0:T(8,128)S(1)} %bitcast.13, f32[2,3,4,64,128]{4,3,2,1,0:T(8,128)S(1)} %bitcast.15, s32[4,64,128]{2,1,0:T(8,128)S(1)} %copy-done.1, ...), custom_call_target="tpu_custom_call" | custom-call | tf_op jit(solution)/shard_map/pallas_call | solution.py:318
  17.5 22.2 %all_to_all.15 = f32[8,40,8,128]{3,2,1,0:T(8,128)S(1)} all-to-all(f32[8,40,8,128]{3,2,1,0:T(8,128)S(1)} %shard_map.51), channel_id=1, replica_groups={{0,32,64,96,128,160,192,224},{16,48,80,112,144,176,208,240},{1,33,65,97..., dimensions={0} | all-to-all | bytes 2621440 | tf_op jit(solution)/shard_map/all_to_all | solution.py:46
  39.7 0.1 reduce_sum.18
  39.9 0.4 collective-permute-start.4
  40.2 4.4 %collective-permute-start.5 = (f32[31,8,128]{2,1,0:T(8,128)S(1)}, f32[31,8,128]{2,1,0:T(8,128)S(1)}, u32[]{:S(2)}, u32[]{:S(2)}) collective-permute-start(f32[31,8,128]{2,1,0:T(8,128)S(1)} %pad_maximum_fusion.2), channel_id=1, source_target_pairs={{1,16},{2,17},{3,18},{4,19},{5,20},{6,21},{7,22},{8,23},{9,24},{10... | collective-permute-start | bytes 380936 | tf_op jit(solution)/shard_map/ppermute | solution.py:40
  44.6 0.0 collective-permute-done.4.near
  44.6 2.6 %collective-permute-done.5.far = f32[31,8,128]{2,1,0:T(8,128)S(1)} collective-permute-done((f32[31,8,128]{2,1,0:T(8,128)S(1)}, f32[31,8,128]{2,1,0:T(8,128)S(1)}, u32[]{:S(2)}, u32[]{:S(2)}) %collective-permute-start.5) | collective-permute-done | bytes 127008 | tf_op jit(solution)/shard_map/ppermute | solution.py:40
  47.2 0.8 %shard_map.52 = f32[8,13,8,128]{3,2,1,0:T(8,128)S(1)} custom-call(s32[2]{0:T(128)S(1)} %pad_add_fusion.place, f32[2,20,8,128]{3,2,1,0:T(8,128)S(1)} %bitcast.17, f32[31,8,128]{2,1,0:T(8,128)S(1)} %collective-permute-done.4.near, f32[31,8,128]{2,1,0:T(8,128)S(1)} %collective-permute-done.5.far), custom_call_target="tpu_custom_call" | custom-call | tf_op jit(solution)/shard_map/pallas_call | solution.py:318
  48.0 9.6 %all_to_all.16.gathered = f32[8,13,8,128]{3,2,1,0:T(8,128)S(1)} all-to-all(f32[8,13,8,128]{3,2,1,0:T(8,128)S(1)} %shard_map.52), channel_id=1, replica_groups={{0,32,64,96,128,160,192,224},{16,48,80,112,144,176,208,240},{1,33,65,97..., dimensions={0} | all-to-all | bytes 851968 | tf_op jit(solution)/shard_map/all_to_all | solution.py:46
  57.6 0.0 collective-permute-start.6
  57.6 1.2 %collective-permute-done.6 = f32[8,128]{1,0:T(8,128)S(1)} collective-permute-done((f32[8,128]{1,0:T(8,128)S(1)}, f32[8,128]{1,0:T(8,128)S(1)}, u32[]{:S(2)}, u32[]{:S(2)}) %collective-permute-start.6) | collective-permute-done | bytes 4128 | tf_op jit(solution)/shard_map/ppermute | solution.py:29
  58.8 0.2 collective-permute-start.7
  59.0 22.0 %all_to_all.17.sums = f32[16,8,128]{2,1,0:T(8,128)S(1)} all-to-all(f32[16,8,128]{2,1,0:T(8,128)S(1)} %broadcast_in_dim.3), channel_id=1, replica_groups=mesh['freq'=16,'gz'=16] {'gz'}, dimensions={0} | all-to-all | bytes 131072 | tf_op jit(solution)/shard_map/all_to_all | solution.py:363
  80.9 0.0 collective-permute-done.7.others
  80.9 1.5 %shard_map.53 = (f32[2,4,64,128]{3,2,1,0:T(8,128)}, f32[2,4,64,128]{3,2,1,0:T(8,128)}) custom-call(s32[2]{0:T(128)S(1)} %pad_add_fusion.place, f32[16,8,128]{2,1,0:T(8,128)S(1)} %all_to_all.17.sums, f32[8,13,8,128]{3,2,1,0:T(8,128)S(1)} %all_to_all.16.gathered, f32[8,13,8,128]{3,2,1,0:T(8,128)S(1)} %collective-permute-done.7.others), custom_call_target="tpu_custom_call" | custom-call | tf_op jit(solution)/shard_map/pallas_call | solution.py:318
  (8 shorter events, 0.1 us)
Async XLA Ops:
  0.6 9.5 %copy-start = (f32[1,2,3,4,64,128]{5,4,3,2,1,0:T(8,128)S(1)}, f32[1,2,3,4,64,128]{5,4,3,2,1,0:T(8,128)}, u32[]{:S(2)}) copy-start(f32[1,2,3,4,64,128]{5,4,3,2,1,0:T(8,128)} %param.3) | copy-start | bytes 2359300
  0.6 9.4 %copy-start.1 = (s32[4,64,128]{2,1,0:T(8,128)S(1)}, s32[4,64,128]{2,1,0:T(8,128)}, u32[]{:S(2)}) copy-start(s32[4,64,128]{2,1,0:T(8,128)} %tissue.3) | copy-start | bytes 393220
  0.7 5.3 %collective-permute-start = (s32[1]{0:T(128)}, s32[1]{0:T(128)}, u32[]{:S(2)}, u32[]{:S(2)}) collective-permute-start(s32[1]{0:T(128)} %param.4), channel_id=1, source_target_pairs={{0,16},{16,0},{32,48},{48,32},{64,80},{80,64},{96,112},{112,96},{1... | collective-permute-start | bytes 20 | tf_op jit(solution)/shard_map/ppermute | solution.py:29
  4.0 6.1 %collective-permute-start.1 = (f32[1,2,3,4,64,128]{5,4,3,2,1,0:T(8,128)}, f32[1,2,3,4,64,128]{5,4,3,2,1,0:T(8,128)S(1)}, u32[]{:S(2)}, u32[]{:S(2)}) collective-permute-start(f32[1,2,3,4,64,128]{5,4,3,2,1,0:T(8,128)} %param.3), channel_id=1, source_target_pairs={{0,16},{16,0},{32,48},{48,32},{64,80},{80,64},{96,112},{112,96},{1... | collective-permute-start | bytes 2359304 | tf_op jit(solution)/shard_map/ppermute | solution.py:29
  5.9 9.4 %collective-permute-start.3 = (f32[7,64,128]{2,1,0:T(8,128)S(1)}, f32[7,64,128]{2,1,0:T(8,128)S(1)}, u32[]{:S(2)}, u32[]{:S(2)}) collective-permute-start(f32[7,64,128]{2,1,0:T(8,128)S(1)} %pad_maximum_fusion), channel_id=1, source_target_pairs={{1,16},{2,17},{3,18},{4,19},{5,20},{6,21},{7,22},{8,23},{9,24},{10... | collective-permute-start | bytes 688136 | tf_op jit(solution)/shard_map/ppermute | solution.py:40
  8.0 7.3 %collective-permute-start.2 = (f32[6,64,128]{2,1,0:T(8,128)S(1)}, f32[6,64,128]{2,1,0:T(8,128)S(1)}, u32[]{:S(2)}, u32[]{:S(2)}) collective-permute-start(f32[6,64,128]{2,1,0:T(8,128)S(1)} %bitcast.19), channel_id=1, source_target_pairs={{0,1},{1,2},{2,3},{3,4},{4,5},{5,6},{6,7},{7,8},{8,9},{9,10},{10,1... | collective-permute-start | bytes 589832 | tf_op jit(solution)/shard_map/ppermute | solution.py:40
  39.9 4.8 %collective-permute-start.4 = (f32[31,8,128]{2,1,0:T(8,128)S(1)}, f32[31,8,128]{2,1,0:T(8,128)S(1)}, u32[]{:S(2)}, u32[]{:S(2)}) collective-permute-start(f32[31,8,128]{2,1,0:T(8,128)S(1)} %pad_maximum_fusion.1), channel_id=1, source_target_pairs={{0,16},{16,0},{32,48},{48,32},{64,80},{80,64},{96,112},{112,96},{1... | collective-permute-start | bytes 380936 | tf_op jit(solution)/shard_map/ppermute | solution.py:29
  40.2 7.0 %collective-permute-start.5 = (f32[31,8,128]{2,1,0:T(8,128)S(1)}, f32[31,8,128]{2,1,0:T(8,128)S(1)}, u32[]{:S(2)}, u32[]{:S(2)}) collective-permute-start(f32[31,8,128]{2,1,0:T(8,128)S(1)} %pad_maximum_fusion.2), channel_id=1, source_target_pairs={{1,16},{2,17},{3,18},{4,19},{5,20},{6,21},{7,22},{8,23},{9,24},{10... | collective-permute-start | bytes 380936 | tf_op jit(solution)/shard_map/ppermute | solution.py:40
  57.6 1.2 %collective-permute-start.6 = (f32[8,128]{1,0:T(8,128)S(1)}, f32[8,128]{1,0:T(8,128)S(1)}, u32[]{:S(2)}, u32[]{:S(2)}) collective-permute-start(f32[8,128]{1,0:T(8,128)S(1)} %slice_reduce_fusion), channel_id=1, source_target_pairs={{0,16},{16,0},{32,48},{48,32},{64,80},{80,64},{96,112},{112,96},{1... | collective-permute-start | bytes 12296 | tf_op jit(solution)/shard_map/ppermute | solution.py:29
  58.8 22.1 %collective-permute-start.7 = (f32[8,13,8,128]{3,2,1,0:T(8,128)S(1)}, f32[8,13,8,128]{3,2,1,0:T(8,128)S(1)}, u32[]{:S(2)}, u32[]{:S(2)}) collective-permute-start(f32[8,13,8,128]{3,2,1,0:T(8,128)S(1)} %all_to_all.16.gathered), channel_id=1, source_target_pairs={{0,16},{16,0},{32,48},{48,32},{64,80},{80,64},{96,112},{112,96},{1... | collective-permute-start | bytes 1277960 | tf_op jit(solution)/shard_map/ppermute | solution.py:29

commit v12 on v8

--- a/solution.py
+++ b/solution.py
@@ -355,10 +355,10 @@
     tiles = run(vectors_kernel, shape(chips, 13, *tile), place, mine, near, far)
 
     gathered = over_chips(tiles)
-    sums = gathered[:, 12].sum(axis=0)
+    sums = gathered[:, 12, :4].sum(axis=0)
     sums, gathered = lax.optimization_barrier((sums + swap_cores(sums), gathered))
     others = swap_cores(gathered)
-    sums = lax.all_to_all(jnp.broadcast_to(sums, (slabs, *tile)), "gz", split_axis=0, concat_axis=0, tiled=True)
+    sums = lax.all_to_all(jnp.broadcast_to(sums, (slabs, *sums.shape)), "gz", split_axis=0, concat_axis=0, tiled=True)
     result = shape(2, 4, ny, nx)
     return tuple(run(outputs_kernel, (result, result), place, sums, gathered, others))
 

time: 82.8 us -> 82.8 us (level)
  no operation moved by 1% of the time
where the time goes in v12:
time: 82.8 us; the launch traced here: 82.5 us
  blocking collectives  54 us (65%)
  starting transfers between devices  13.8 us (17%)
  Pallas kernels  6.52 us (8%)
  waiting for transfers between devices  4.62 us (6%)
  other arithmetic  2.02 us (2%)
  between operations  1.41 us (2%)
    all_to_all x2, blocking collectives, over_chips(): lax.all_to_all(parts, 'freq', split_axis=0, concat_axis=0, tiled=True, ax...  31.8 us
    all_to_all x1, blocking collectives, body(): lax.all_to_all(jnp.broadcast_to(sums, (slabs, *sums.shape)), 'gz', split_...  22.2 us
    ppermute x5, starting transfers between devices, swap_cores(): return lax.ppermute(array, 'freq', pairs)  7.3 us
    ppermute x3, starting transfers between devices, to_slabs(): return lax.ppermute(array, ('freq', 'gz'), pairs)  6.54 us
    pallas_call x4, Pallas kernels, run(): pl.pallas_call(kernel, out_shape=shapes, in_specs=[smem] * scalars + [vme...  6.52 us
    ppermute x3, waiting for transfers between devices, to_slabs(): return lax.ppermute(array, ('freq', 'gz'), pairs)  3.12 us
  transfers between devices with their start and end apart: 8, of which 4 were waited for; matrix products, arithmetic and copies ran while one was open for 2% of the time, Pallas kernels for 2%

profile of v12, /device:TPU:1, one launch (start us, length us, event | category | flops | bytes accessed | tf_op | source)
XLA Modules:
  0.0 82.5 jit_solution(17339373763848232324)
XLA Ops:
  0.6 0.0 copy-start
  0.6 0.0 copy-start.1
  0.7 3.3 %collective-permute-start.1 = (f32[1,2,3,4,64,128]{5,4,3,2,1,0:T(8,128)}, f32[1,2,3,4,64,128]{5,4,3,2,1,0:T(8,128)S(1)}, u32[]{:S(2)}, u32[]{:S(2)}) collective-permute-start(f32[1,2,3,4,64,128]{5,4,3,2,1,0:T(8,128)} %param.3), channel_id=1, source_target_pairs={{0,16},{16,0},{32,48},{48,32},{64,80},{80,64},{96,112},{112,96},{1... | collective-permute-start | bytes 2359304 | tf_op jit(solution)/shard_map/ppermute | solution.py:29
  4.0 0.8 slice_convert_fusion
  4.7 1.1 %slice_select_fusion = (f32[2,3,1,64,128]{4,3,2,1,0:T(8,128)S(1)}, f32[2,3,1,64,128]{4,3,2,1,0:T(8,128)S(1)}) fusion(f32[2,3,4,64,128]{4,3,2,1,0:T(8,128)} %bitcast.11, pred[]{:T(512)S(6)} %eq.8), kind=kLoop, calls=%fused_computation.1 | loop fusion | flops 98304 | bytes 786433 | tf_op jit(solution)/shard_map/jit(_where)/select_n | solution.py:343
  5.8 1.9 %collective-permute-start.3 = (f32[7,64,128]{2,1,0:T(8,128)S(1)}, f32[7,64,128]{2,1,0:T(8,128)S(1)}, u32[]{:S(2)}, u32[]{:S(2)}) collective-permute-start(f32[7,64,128]{2,1,0:T(8,128)S(1)} %pad_maximum_fusion), channel_id=1, source_target_pairs={{1,16},{2,17},{3,18},{4,19},{5,20},{6,21},{7,22},{8,23},{9,24},{10... | collective-permute-start | bytes 688136 | tf_op jit(solution)/shard_map/ppermute | solution.py:40
  7.8 1.3 %collective-permute-start.2 = (f32[6,64,128]{2,1,0:T(8,128)S(1)}, f32[6,64,128]{2,1,0:T(8,128)S(1)}, u32[]{:S(2)}, u32[]{:S(2)}) collective-permute-start(f32[6,64,128]{2,1,0:T(8,128)S(1)} %bitcast.19), channel_id=1, source_target_pairs={{0,1},{1,2},{2,3},{3,4},{4,5},{5,6},{6,7},{7,8},{8,9},{9,10},{10,1... | collective-permute-start | bytes 589832 | tf_op jit(solution)/shard_map/ppermute | solution.py:40
  9.1 2.8 %collective-permute-start = (s32[1]{0:T(128)}, s32[1]{0:T(128)}, u32[]{:S(2)}, u32[]{:S(2)}) collective-permute-start(s32[1]{0:T(128)} %param.4), channel_id=1, source_target_pairs={{0,16},{16,0},{32,48},{48,32},{64,80},{80,64},{96,112},{112,96},{1... | collective-permute-start | bytes 20 | tf_op jit(solution)/shard_map/ppermute | solution.py:29
  12.6 0.1 pad_add_fusion.place
  12.6 0.4 collective-permute-done.other_index
  13.0 0.0 collective-permute-done.1
  13.0 0.0 copy-done
  13.0 0.0 copy-done.1
  13.0 2.0 %shard_map.50.inner = f32[8,20,8,128]{3,2,1,0:T(8,128)S(1)} custom-call(s32[2]{0:T(128)S(1)} %pad_add_fusion.place, s32[1]{0:T(128)S(6)} %copy.5.index, s32[1]{0:T(128)} %collective-permute-done.other_index, f32[2,3,4,64,128]{4,3,2,1,0:T(8,128)S(1)} %bitcast.12, f32[2,3,4,64,128]{4,3,2,1,0:T(8,128)S(1)} %bitcast.14, s32[4,64,128]{2,1,0:T(8,128)S(1)} %copy-done.1), custom_call_target="tpu_custom_call" | custom-call | tf_op jit(solution)/shard_map/pallas_call | solution.py:318
  15.0 0.2 collective-permute-done.2.same
  15.3 0.0 collective-permute-done.3.cross
  15.3 2.1 %shard_map.51 = f32[8,40,8,128]{3,2,1,0:T(8,128)S(1)} custom-call(s32[2]{0:T(128)S(1)} %pad_add_fusion.place, s32[1]{0:T(128)S(6)} %copy.5.index, s32[1]{0:T(128)} %collective-permute-done.other_index, f32[2,3,4,64,128]{4,3,2,1,0:T(8,128)S(1)} %bitcast.13, f32[2,3,4,64,128]{4,3,2,1,0:T(8,128)S(1)} %bitcast.15, s32[4,64,128]{2,1,0:T(8,128)S(1)} %copy-done.1, ...), custom_call_target="tpu_custom_call" | custom-call | tf_op jit(solution)/shard_map/pallas_call | solution.py:318
  17.4 22.3 %all_to_all.15 = f32[8,40,8,128]{3,2,1,0:T(8,128)S(1)} all-to-all(f32[8,40,8,128]{3,2,1,0:T(8,128)S(1)} %shard_map.51), channel_id=1, replica_groups={{0,32,64,96,128,160,192,224},{16,48,80,112,144,176,208,240},{1,33,65,97..., dimensions={0} | all-to-all | bytes 2621440 | tf_op jit(solution)/shard_map/all_to_all | solution.py:46
  39.7 0.1 reduce_sum.18
  39.8 0.9 %collective-permute-start.4 = (f32[31,8,128]{2,1,0:T(8,128)S(1)}, f32[31,8,128]{2,1,0:T(8,128)S(1)}, u32[]{:S(2)}, u32[]{:S(2)}) collective-permute-start(f32[31,8,128]{2,1,0:T(8,128)S(1)} %pad_maximum_fusion.1), channel_id=1, source_target_pairs={{0,16},{16,0},{32,48},{48,32},{64,80},{80,64},{96,112},{112,96},{1... | collective-permute-start | bytes 380936 | tf_op jit(solution)/shard_map/ppermute | solution.py:29
  40.7 3.3 %collective-permute-start.5 = (f32[31,8,128]{2,1,0:T(8,128)S(1)}, f32[31,8,128]{2,1,0:T(8,128)S(1)}, u32[]{:S(2)}, u32[]{:S(2)}) collective-permute-start(f32[31,8,128]{2,1,0:T(8,128)S(1)} %pad_maximum_fusion.2), channel_id=1, source_target_pairs={{1,16},{2,17},{3,18},{4,19},{5,20},{6,21},{7,22},{8,23},{9,24},{10... | collective-permute-start | bytes 380936 | tf_op jit(solution)/shard_map/ppermute | solution.py:40
  44.1 0.0 collective-permute-done.4.near
  44.1 2.9 %collective-permute-done.5.far = f32[31,8,128]{2,1,0:T(8,128)S(1)} collective-permute-done((f32[31,8,128]{2,1,0:T(8,128)S(1)}, f32[31,8,128]{2,1,0:T(8,128)S(1)}, u32[]{:S(2)}, u32[]{:S(2)}) %collective-permute-start.5) | collective-permute-done | bytes 127008 | tf_op jit(solution)/shard_map/ppermute | solution.py:40
  47.0 0.8 %shard_map.52 = f32[8,13,8,128]{3,2,1,0:T(8,128)S(1)} custom-call(s32[2]{0:T(128)S(1)} %pad_add_fusion.place, f32[2,20,8,128]{3,2,1,0:T(8,128)S(1)} %bitcast.17, f32[31,8,128]{2,1,0:T(8,128)S(1)} %collective-permute-done.4.near, f32[31,8,128]{2,1,0:T(8,128)S(1)} %collective-permute-done.5.far), custom_call_target="tpu_custom_call" | custom-call | tf_op jit(solution)/shard_map/pallas_call | solution.py:318
  47.8 9.5 %all_to_all.16.gathered = f32[8,13,8,128]{3,2,1,0:T(8,128)S(1)} all-to-all(f32[8,13,8,128]{3,2,1,0:T(8,128)S(1)} %shard_map.52), channel_id=1, replica_groups={{0,32,64,96,128,160,192,224},{16,48,80,112,144,176,208,240},{1,33,65,97..., dimensions={0} | all-to-all | bytes 851968 | tf_op jit(solution)/shard_map/all_to_all | solution.py:46
  57.3 0.1 collective-permute-start.6
  57.4 1.1 %collective-permute-done.6 = f32[4,128]{1,0:T(4,128)S(1)} collective-permute-done((f32[4,128]{1,0:T(4,128)S(1)}, f32[4,128]{1,0:T(4,128)S(1)}, u32[]{:S(2)}, u32[]{:S(2)}) %collective-permute-start.6) | collective-permute-done | bytes 2080 | tf_op jit(solution)/shard_map/ppermute | solution.py:29
  58.6 0.2 collective-permute-start.7
  58.7 22.2 %all_to_all.17.sums = f32[16,4,128]{2,1,0:T(4,128)S(1)} all-to-all(f32[16,4,128]{2,1,0:T(4,128)S(1)} %broadcast_in_dim.3), channel_id=1, replica_groups=mesh['freq'=16,'gz'=16] {'gz'}, dimensions={0} | all-to-all | bytes 65536 | tf_op jit(solution)/shard_map/all_to_all | solution.py:361
  80.9 0.0 collective-permute-done.7.others
  80.9 1.5 %shard_map.53 = (f32[2,4,64,128]{3,2,1,0:T(8,128)}, f32[2,4,64,128]{3,2,1,0:T(8,128)}) custom-call(s32[2]{0:T(128)S(1)} %pad_add_fusion.place, f32[16,4,128]{2,1,0:T(4,128)S(1)} %all_to_all.17.sums, f32[8,13,8,128]{3,2,1,0:T(8,128)S(1)} %all_to_all.16.gathered, f32[8,13,8,128]{3,2,1,0:T(8,128)S(1)} %collective-permute-done.7.others), custom_call_target="tpu_custom_call" | custom-call | tf_op jit(solution)/shard_map/pallas_call | solution.py:318
  (8 shorter events, 0.1 us)
Async XLA Ops:
  0.6 12.4 %copy-start = (f32[1,2,3,4,64,128]{5,4,3,2,1,0:T(8,128)S(1)}, f32[1,2,3,4,64,128]{5,4,3,2,1,0:T(8,128)}, u32[]{:S(2)}) copy-start(f32[1,2,3,4,64,128]{5,4,3,2,1,0:T(8,128)} %param.3) | copy-start | bytes 2359300
  0.6 12.3 %copy-start.1 = (s32[4,64,128]{2,1,0:T(8,128)S(1)}, s32[4,64,128]{2,1,0:T(8,128)}, u32[]{:S(2)}) copy-start(s32[4,64,128]{2,1,0:T(8,128)} %tissue.3) | copy-start | bytes 393220
  0.7 12.3 %collective-permute-start.1 = (f32[1,2,3,4,64,128]{5,4,3,2,1,0:T(8,128)}, f32[1,2,3,4,64,128]{5,4,3,2,1,0:T(8,128)S(1)}, u32[]{:S(2)}, u32[]{:S(2)}) collective-permute-start(f32[1,2,3,4,64,128]{5,4,3,2,1,0:T(8,128)} %param.3), channel_id=1, source_target_pairs={{0,16},{16,0},{32,48},{48,32},{64,80},{80,64},{96,112},{112,96},{1... | collective-permute-start | bytes 2359304 | tf_op jit(solution)/shard_map/ppermute | solution.py:29
  5.8 9.4 %collective-permute-start.3 = (f32[7,64,128]{2,1,0:T(8,128)S(1)}, f32[7,64,128]{2,1,0:T(8,128)S(1)}, u32[]{:S(2)}, u32[]{:S(2)}) collective-permute-start(f32[7,64,128]{2,1,0:T(8,128)S(1)} %pad_maximum_fusion), channel_id=1, source_target_pairs={{1,16},{2,17},{3,18},{4,19},{5,20},{6,21},{7,22},{8,23},{9,24},{10... | collective-permute-start | bytes 688136 | tf_op jit(solution)/shard_map/ppermute | solution.py:40
  7.8 7.5 %collective-permute-start.2 = (f32[6,64,128]{2,1,0:T(8,128)S(1)}, f32[6,64,128]{2,1,0:T(8,128)S(1)}, u32[]{:S(2)}, u32[]{:S(2)}) collective-permute-start(f32[6,64,128]{2,1,0:T(8,128)S(1)} %bitcast.19), channel_id=1, source_target_pairs={{0,1},{1,2},{2,3},{3,4},{4,5},{5,6},{6,7},{7,8},{8,9},{9,10},{10,1... | collective-permute-start | bytes 589832 | tf_op jit(solution)/shard_map/ppermute | solution.py:40
  9.1 3.9 %collective-permute-start = (s32[1]{0:T(128)}, s32[1]{0:T(128)}, u32[]{:S(2)}, u32[]{:S(2)}) collective-permute-start(s32[1]{0:T(128)} %param.4), channel_id=1, source_target_pairs={{0,16},{16,0},{32,48},{48,32},{64,80},{80,64},{96,112},{112,96},{1... | collective-permute-start | bytes 20 | tf_op jit(solution)/shard_map/ppermute | solution.py:29
  39.8 4.2 %collective-permute-start.4 = (f32[31,8,128]{2,1,0:T(8,128)S(1)}, f32[31,8,128]{2,1,0:T(8,128)S(1)}, u32[]{:S(2)}, u32[]{:S(2)}) collective-permute-start(f32[31,8,128]{2,1,0:T(8,128)S(1)} %pad_maximum_fusion.1), channel_id=1, source_target_pairs={{0,16},{16,0},{32,48},{48,32},{64,80},{80,64},{96,112},{112,96},{1... | collective-permute-start | bytes 380936 | tf_op jit(solution)/shard_map/ppermute | solution.py:29
  40.7 6.2 %collective-permute-start.5 = (f32[31,8,128]{2,1,0:T(8,128)S(1)}, f32[31,8,128]{2,1,0:T(8,128)S(1)}, u32[]{:S(2)}, u32[]{:S(2)}) collective-permute-start(f32[31,8,128]{2,1,0:T(8,128)S(1)} %pad_maximum_fusion.2), channel_id=1, source_target_pairs={{1,16},{2,17},{3,18},{4,19},{5,20},{6,21},{7,22},{8,23},{9,24},{10... | collective-permute-start | bytes 380936 | tf_op jit(solution)/shard_map/ppermute | solution.py:40
  57.3 1.2 %collective-permute-start.6 = (f32[4,128]{1,0:T(4,128)S(1)}, f32[4,128]{1,0:T(4,128)S(1)}, u32[]{:S(2)}, u32[]{:S(2)}) collective-permute-start(f32[4,128]{1,0:T(4,128)S(1)} %slice_reduce_fusion), channel_id=1, source_target_pairs={{0,16},{16,0},{32,48},{48,32},{64,80},{80,64},{96,112},{112,96},{1... | collective-permute-start | bytes 6152 | tf_op jit(solution)/shard_map/ppermute | solution.py:29
  58.6 22.4 %collective-permute-start.7 = (f32[8,13,8,128]{3,2,1,0:T(8,128)S(1)}, f32[8,13,8,128]{3,2,1,0:T(8,128)S(1)}, u32[]{:S(2)}, u32[]{:S(2)}) collective-permute-start(f32[8,13,8,128]{3,2,1,0:T(8,128)S(1)} %all_to_all.16.gathered), channel_id=1, source_target_pairs={{0,16},{16,0},{32,48},{48,32},{64,80},{80,64},{96,112},{112,96},{1... | collective-permute-start | bytes 1277960 | tf_op jit(solution)/shard_map/ppermute | solution.py:29
